TPU v7x, 32 devices: a whole 2x2x4 slice. The times are simulated.
32 devices in a mesh: wide: 16 (over z, x, core), narrow: 2 (over y).
Axes of the slice: x: 2, y: 2, z: 4, core: 2. Of those that a mesh axis runs over, the one named last changes fastest.
Arguments:
- question_word_vectors: bfloat16 [32, 64, 768], P(('wide', 'narrow')), may hold values from -6 to 6
- question_numbers: int32 [32, 64], P(('wide', 'narrow')), may hold values from 0 to 2, never falling along the last dimension, each value on 1 to 40 neighbouring positions
- document_word_vectors: bfloat16 [32, 256, 768], P(('wide', 'narrow')), may hold values from -6 to 6
- document_numbers: int32 [32, 256], P(('wide', 'narrow')), may hold values from 0 to 3, never falling along the last dimension, each value on 1 to 106 neighbouring positions
- matching_document: int32 [96], P(('wide', 'narrow')), may hold values from 0 to 127
- distance_class_lookup: int32 [511], replicated, may hold values from 0 to 31
- softness_scalar: float32 [1], replicated, may hold values from 0.01 to 0.04
- distance_shift_grid: float32 [32, 12], replicated, may hold values from -4 to 4
- rescale_factors: float32 [3, 768], replicated, may hold values from 0.5 to 1.5
- asking_matrix: bfloat16 [768, 768], replicated, may hold values from -0.109375 to 0.109375
- addressing_matrix: bfloat16 [768, 768], replicated, may hold values from -0.109375 to 0.109375
- content_matrix: bfloat16 [768, 768], replicated, may hold values from -0.21875 to 0.21875
- attention_merge_matrix: bfloat16 [768, 768], replicated, may hold values from -1.75 to 1.75
- gating_matrix: bfloat16 [768, 2048], replicated, may hold values from -0.21875 to 0.21875
- expansion_matrix: bfloat16 [768, 2048], replicated, may hold values from -0.21875 to 0.21875
- contraction_matrix: bfloat16 [2048, 768], replicated, may hold values from -0.1875 to 0.1875
- pooling_matrix: bfloat16 [768, 768], replicated, may hold values from -0.21875 to 0.21875
Outputs:
- loss: float32 [1], replicated
- query_vectors: float32 [96, 768], P(('wide', 'narrow'))
- passage_vectors: float32 [128, 768], P(('wide', 'narrow'))
- query_grads: float32 [32, 64, 768], P(('wide', 'narrow'))
- passage_grads: float32 [32, 256, 768], P(('wide', 'narrow'))
- gain_grads: float32 [3, 768], replicated
- bias_grads: float32 [32, 12], replicated
- grad_query_w: float32 [768, 768], P('narrow', 'wide')
- grad_key_w: float32 [768, 768], P('narrow', 'wide')
- grad_value_w: float32 [768, 768], P('narrow', 'wide')
- grad_out_w: float32 [768, 768], P('narrow', 'wide')
- grad_gate_w: float32 [768, 2048], P('narrow', 'wide')
- grad_up_w: float32 [768, 2048], P('narrow', 'wide')
- grad_down_w: float32 [2048, 768], P('narrow', 'wide')
- grad_proj_w: float32 [768, 768], P('narrow', 'wide')
Inputs may be any that keep to these rules, and one draw needn't show every extreme that they name: `question_numbers`: query ids of a row never fall, every query has at least one token and at most 40. `document_numbers`: passage ids of a row never fall, every passage has at least one token and at most 106. `matching_document`: passages numbered over all passage rows, row by row. `distance_class_lookup`: entry j - i + 255 is the bucket of key j seen from token i.
All inputs are finite; a program needn't handle non-finite values.
Results may differ from a plain program's by a relative error of at most 0.03.
Values may be sent and summed in bfloat16 or wider, within the bound.
No kernel may reach another device: no remote copies, remote signals or barrier semaphores. Data moves between devices by JAX's collectives and lax.ppermute only.
A program may use at most 192 MiB of HBM per device.

v0:
```python
import functools

import jax
import jax.numpy as jnp
from jax import lax
from jax.experimental import pallas as pl
from jax.experimental.pallas import tpu as pltpu
from jax.sharding import PartitionSpec as P

LAYERS = 2
QSEGS = 3
PSEGS = 4
HDIM = 64
PACK = 8

HIGHEST = lax.Precision.HIGHEST
EPSILON = 1e-06
MASKED = -1000000000.0
BF = jnp.bfloat16
F32 = jnp.float32
AXES = ("wide", "narrow")


def low(a):
    return a.astype(BF)


def product(a, b):
    return jnp.dot(a, b, preferred_element_type=F32)


def dot_tn(a, b, precision=None):
    return lax.dot_general(
        a, b, (((0,), (0,)), ((), ())), preferred_element_type=F32, precision=precision
    )


def dot_nt(a, b, precision=None):
    return lax.dot_general(
        a, b, (((1,), (1,)), ((), ())), preferred_element_type=F32, precision=precision
    )


def rms_norm(x, gain_vec):
    return x * lax.rsqrt(jnp.mean(x * x, axis=-1, keepdims=True) + EPSILON) * gain_vec


def norm_back(x, gain_vec, grad_in):
    outcome, pullback = jax.vjp(rms_norm, x, gain_vec)
    return pullback(grad_in)


def whole():
    return pl.BlockSpec(memory_space=pltpu.VMEM)


def bias_kernel(qlen, plen, lookup_ref, grid_ref, qseg_ref, pseg_ref, pbias_ref, qbias_ref, wide_s, short_s):
    heads, buckets = grid_ref.shape
    width = 2 * plen
    wide_s[...] = jnp.full((1, width), -1, jnp.int32)
    wide_s[:, : lookup_ref.shape[1]] = lookup_ref[...]
    onehot = (
        lax.broadcasted_iota(jnp.int32, (buckets, width), 0)
        == jnp.broadcast_to(wide_s[...], (buckets, width))
    ).astype(F32)
    table = jnp.dot(grid_ref[...], onehot, precision=HIGHEST, preferred_element_type=F32)
    pcol = jnp.transpose(jnp.broadcast_to(pseg_ref[...], (plen, plen)))
    psame = pcol == jnp.broadcast_to(pseg_ref[...], (plen, plen))
    short_s[...] = jnp.full((1, 128), -1, jnp.int32)
    short_s[:, :qlen] = qseg_ref[...]
    qcol = jnp.transpose(jnp.broadcast_to(short_s[...], (128, 128)))
    qsame = (qcol == jnp.broadcast_to(short_s[...], (128, 128)))[:qlen, :qlen]
    for head in range(heads):
        rows = jnp.broadcast_to(table[head : head + 1, :], (plen, width))
        rolled = pltpu.roll(rows, width - (plen - 1), 1, stride=1, stride_axis=0)
        block = rolled[:, :plen]
        pbias_ref[head] = jnp.where(psame, block, MASKED)
        qbias_ref[head] = jnp.where(qsame, block[:qlen, :qlen], MASKED)


def half_mask(lanes, side):
    return (lax.broadcasted_iota(jnp.int32, (1, lanes), 1) // HDIM) == side


def attend_kernel(qlen, q_ref, k_ref, v_ref, pbias_ref, qbias_ref, o_ref, pp_ref, pq_ref):
    pairs = q_ref.shape[1] // 128
    spans = ((0, qlen, qbias_ref, pq_ref), (qlen, q_ref.shape[0] - qlen, pbias_ref, pp_ref))

    def pair(i, carry):
        lanes = pl.ds(pl.multiple_of(i * 128, 128), 128)
        for start, length, bias_ref, keep_ref in spans:
            rows = pl.ds(start, length)
            q2, k2, v2 = q_ref[rows, lanes], k_ref[rows, lanes], v_ref[rows, lanes]
            total = None
            for side in range(2):
                mine = half_mask(128, side)
                zero = jnp.zeros_like(k2)
                s = dot_nt(q2, jnp.where(mine, k2, zero)) + bias_ref[2 * i + side]
                top = jnp.max(s, axis=-1, keepdims=True)
                e = jnp.exp(s - top)
                p = low(e * (1.0 / jnp.sum(e, axis=-1, keepdims=True)))
                keep_ref[2 * i + side] = p
                part = product(p, jnp.where(mine, v2, zero))
                total = part if total is None else total + part
            o_ref[rows, lanes] = low(total)
        return carry

    lax.fori_loop(0, pairs, pair, 0)


def attend_back_kernel(
    qlen, q_ref, k_ref, v_ref, o_ref, go_ref, pp_ref, pq_ref, acc_ref, gq_ref, gk_ref, gv_ref, ds_ref
):
    pairs = q_ref.shape[1] // 128
    plen = q_ref.shape[0] - qlen

    def pair(i, carry):
        lanes = pl.ds(pl.multiple_of(i * 128, 128), 128)
        for start, length, keep_ref in ((qlen, plen, pp_ref), (0, qlen, pq_ref)):
            rows = pl.ds(start, length)
            q2, k2, v2 = q_ref[rows, lanes], k_ref[rows, lanes], v_ref[rows, lanes]
            o2, go2 = o_ref[rows, lanes], go_ref[rows, lanes]
            prod = o2.astype(F32) * go2.astype(F32)
            gq, gk, gv = None, None, None
            for side in range(2):
                mine = half_mask(128, side)
                zero = jnp.zeros_like(k2)
                p = keep_ref[2 * i + side]
                gp = dot_nt(go2, jnp.where(mine, v2, zero))
                delta = jnp.sum(jnp.where(mine, prod, 0.0), axis=-1, keepdims=True)
                ds = p.astype(F32) * (gp - delta)
                if start == qlen:
                    if acc_ref is None:
                        ds_ref[2 * i + side] = ds
                    else:
                        ds_ref[2 * i + side] = ds + acc_ref[2 * i + side]
                else:
                    ds_ref[2 * i + side, :length, :length] += ds
                dsl = low(ds)
                a = product(dsl, jnp.where(mine, k2, zero))
                b = dot_tn(dsl, jnp.where(mine, q2, zero))
                c = dot_tn(p, jnp.where(mine, go2, zero))
                gq = a if gq is None else gq + a
                gk = b if gk is None else gk + b
                gv = c if gv is None else gv + c
            gq_ref[rows, lanes] = low(gq)
            gk_ref[rows, lanes] = low(gk)
            gv_ref[rows, lanes] = low(gv)
        return carry

    lax.fori_loop(0, pairs, pair, 0)


def attend_back(q, k, v, o, go, pp, pq, acc):
    heads, plen, _ = pp.shape
    qlen = pq.shape[1]
    operands = [q, k, v, o, go, pp, pq] + ([] if acc is None else [acc])

    def body(*refs):
        ins = list(refs[: len(operands)])
        if acc is None:
            ins.append(None)
        attend_back_kernel(qlen, *ins, *refs[len(operands) :])

    return pl.pallas_call(
        body,
        out_shape=(jax.ShapeDtypeStruct(q.shape, BF),) * 3
        + (jax.ShapeDtypeStruct((heads, plen, plen), F32),),
        in_specs=[whole()] * len(operands),
        out_specs=(whole(),) * 4,
        name="attend_back",
        compiler_params=pltpu.CompilerParams(vmem_limit_bytes=14 << 20),
        cost_estimate=pl.CostEstimate(
            flops=8 * heads * HDIM * plen * plen, bytes_accessed=12 * heads * plen * plen, transcendentals=0
        ),
    )(*operands)


def small_kernel(
    buckets, ds_ref, lookup_ref, in_ref, mid_ref, final_ref, loss_ref, out_ref, diag_ref, wide_s
):
    heads, plen, _ = ds_ref.shape
    out_ref[...] = jnp.zeros_like(out_ref)
    out_ref[0:1, :] = in_ref[...]
    out_ref[1:2, :] = mid_ref[...]
    out_ref[2:3, :] = final_ref[...]
    out_ref[3:4, :128] = loss_ref[...]
    width = 2 * plen
    wide_s[...] = jnp.full((1, width), -1, jnp.int32)
    wide_s[:, : lookup_ref.shape[1]] = lookup_ref[...]
    for head in range(heads):
        block = ds_ref[head]
        wide_block = jnp.concatenate([block, jnp.zeros_like(block)], axis=1)
        rows = plen
        while rows > 8:
            rows //= 2
            wide_block = wide_block[:rows] + pltpu.roll(wide_block[rows:], width - rows, 1)
        at = lax.broadcasted_iota(jnp.int32, (8, width), 0)
        for bit in (4, 2, 1):
            moved = pltpu.roll(wide_block, width - bit, 1)
            wide_block = jnp.where((at & bit) != 0, moved, wide_block)
        rolled = pltpu.roll(wide_block, plen - 1, 1)
        diag_ref[head : head + 1, :] = jnp.sum(rolled, axis=0, keepdims=True)
    onehot = (
        lax.broadcasted_iota(jnp.int32, (buckets, width), 0)
        == jnp.broadcast_to(wide_s[...], (buckets, width))
    ).astype(F32)
    out_ref[4 : 4 + heads, :buckets] = dot_nt(diag_ref[...], onehot, HIGHEST)


def small_sums(ds, lookup, buckets, gain_in, gain_mid, gain_final, loss):
    heads, plen, _ = ds.shape
    width = 2 * plen
    return pl.pallas_call(
        functools.partial(small_kernel, buckets),
        out_shape=jax.ShapeDtypeStruct((4 + heads, gain_in.shape[1]), F32),
        in_specs=[whole()] * 6,
        out_specs=whole(),
        scratch_shapes=[pltpu.VMEM((heads, width), F32), pltpu.VMEM((1, width), jnp.int32)],
        name="small_sums",
        compiler_params=pltpu.CompilerParams(vmem_limit_bytes=8 << 20),
    )(ds, lookup[None], gain_in, gain_mid, gain_final, loss)


def segment_table(seg_ref, first):
    rows, length = PACK, seg_ref.shape[1]
    slot = lax.broadcasted_iota(jnp.int32, (rows, length), 0)
    return (slot == jnp.broadcast_to(seg_ref[...], (rows, length)) + first).astype(F32)


def pool_kernel(
    x_ref, gain_ref, qseg_ref, pseg_ref, label_ref, wp_ref, packed_ref, vec_ref, e_ref, pooled_ref
):
    qlen = qseg_ref.shape[1]
    x = x_ref[...]
    z = x * lax.rsqrt(jnp.mean(x * x, axis=-1, keepdims=True) + EPSILON) * gain_ref[...]
    qt, pt = segment_table(qseg_ref, 0), segment_table(pseg_ref, QSEGS)
    sizes = jnp.sum(qt, axis=1, keepdims=True) + jnp.sum(pt, axis=1, keepdims=True)
    sums = jnp.dot(qt, z[:qlen], precision=HIGHEST, preferred_element_type=F32) + jnp.dot(
        pt, z[qlen:], precision=HIGHEST, preferred_element_type=F32
    )
    pooled = low(sums / jnp.maximum(sizes, 1.0))
    pooled_ref[...] = pooled
    e = product(pooled, wp_ref[...])
    e_ref[...] = e
    vec = e * lax.rsqrt(jnp.sum(e * e, axis=-1, keepdims=True) + EPSILON)
    vec_ref[...] = vec
    at = lax.broadcasted_iota(jnp.int32, vec.shape, 1)
    row = lax.broadcasted_iota(jnp.int32, vec.shape, 0)
    code = jnp.zeros(vec.shape, F32)
    for i in range(QSEGS):
        label = label_ref[i]
        high = lax.shift_right_logical(label, 5).astype(F32)
        rest = (label & 31).astype(F32)
        code = jnp.where(at == i, high, jnp.where(at == QSEGS + i, rest, code))
    packed_ref[...] = low(jnp.where(row == PACK - 1, code, vec))


SLOPE = 0.7978845608028654
CUBE = 0.044715
SAVED = ("h", "q", "k", "v", "pp", "pq", "o", "x_mid", "normed", "da", "db", "u")


def unit_scale(x):
    return lax.rsqrt(jnp.mean(x * x, axis=-1, keepdims=True) + EPSILON)


def gated_parts(a, b):
    square = a * a
    th = jnp.tanh(a * (SLOPE + (SLOPE * CUBE) * square))
    half = 0.5 + 0.5 * th
    value = a * half
    slope = half + (0.5 * a) * (1.0 - th * th) * (SLOPE + (3.0 * SLOPE * CUBE) * square)
    return low(value * b), low(b * slope), low(value)


def forward_kernel(qlen, plen, n_tiles, *refs):
    (qx_ref, px_ref, lookup_ref, grid_ref, qseg_ref, pseg_ref, gains_ref, label_ref), refs = refs[:8], refs[8:]
    hbm, refs = refs[:8], refs[8:]
    packed_ref, vec_ref, e_ref, pooled_ref, x_mid_out, x_out = refs[:6]
    refs = refs[6:]
    outs = [dict(zip(SAVED, refs[n * len(SAVED) : (n + 1) * len(SAVED)])) for n in range(LAYERS)]
    refs = refs[LAYERS * len(SAVED) :]
    held, refs = refs[:8], refs[8:]
    keep, refs = dict(zip(SAVED, refs[: len(SAVED)])), refs[len(SAVED) :]
    x_s, pbias_s, qbias_s, wide_s, short_s, in_sem, out_sem, x_sem = refs
    wq_s, wk_s, wv_s, wo_s, wg_s, wu_s, wd_s, wp_s = held
    fetch = [pltpu.make_async_copy(a, b, in_sem.at[i]) for i, (a, b) in enumerate(zip(hbm, held))]
    for c in fetch:
        c.start()
    x_s[0, :qlen] = qx_ref[...].astype(F32)
    x_s[0, qlen:] = px_ref[...].astype(F32)
    bias_kernel(qlen, plen, lookup_ref, grid_ref, qseg_ref, pseg_ref, pbias_s, qbias_s, wide_s, short_s)

    def write(n, name):
        i = n * len(SAVED) + SAVED.index(name)
        return pltpu.make_async_copy(keep[name].at[n], outs[n][name], out_sem.at[i])

    def send(layer, *names):
        for n in range(LAYERS):

            @pl.when(layer == n)
            def _():
                for name in names:
                    write(n, name).start()

    def arrive(layer, *ids):
        @pl.when(layer == 0)
        def _():
            for i in ids:
                fetch[i].wait()

    def layer_step(layer, carry):
        x = x_s[layer]
        h = low(x * unit_scale(x) * gains_ref[0:1, :])
        keep["h"][layer] = h
        for i, (name, w) in enumerate((("q", wq_s), ("k", wk_s), ("v", wv_s))):
            arrive(layer, i)
            keep[name][layer] = low(product(h, w[...]))
        send(layer, "h", "q", "k", "v")
        at = {name: keep[name].at[layer] for name in SAVED}
        attend_kernel(qlen, at["q"], at["k"], at["v"], pbias_s, qbias_s, at["o"], at["pp"], at["pq"])
        send(layer, "o", "pp", "pq")
        arrive(layer, 3)
        x_mid = x_s[layer] + product(at["o"][...], wo_s[...])
        at["x_mid"][...] = x_mid
        normed = low(x_mid * unit_scale(x_mid) * gains_ref[1:2, :])
        at["normed"][...] = normed
        send(layer, "x_mid", "normed")
        arrive(layer, 4, 5)
        size = wg_s.shape[1] // n_tiles
        for t in range(n_tiles):
            lanes = slice(t * size, (t + 1) * size)
            a = product(normed, wg_s[:, lanes])
            b = product(normed, wu_s[:, lanes])
            u, da, db = gated_parts(a, b)
            at["u"][:, lanes] = u
            at["da"][:, lanes] = da
            at["db"][:, lanes] = db
        send(layer, "u", "da", "db")
        arrive(layer, 6)
        x_s[layer + 1] = at["x_mid"][...] + product(at["u"][...], wd_s[...])
        return carry

    lax.fori_loop(0, LAYERS, layer_step, 0)
    inner = pltpu.make_async_copy(x_s.at[1], x_mid_out, x_sem.at[0])
    outer = pltpu.make_async_copy(x_s.at[LAYERS], x_out, x_sem.at[1])
    inner.start()
    outer.start()
    fetch[7].wait()
    pool_kernel(
        x_s.at[LAYERS], gains_ref.at[2:3], qseg_ref, pseg_ref, label_ref, wp_s, packed_ref, vec_ref, e_ref, pooled_ref
    )
    for n in range(LAYERS):
        for name in SAVED:
            write(n, name).wait()
    inner.wait()
    outer.wait()


def saved_shapes(total, qlen, plen, feat, hidden, heads):
    tok, ff = ((total, feat), BF), ((total, hidden), BF)
    kinds = dict(h=tok, q=tok, k=tok, v=tok, o=tok, normed=tok, da=ff, db=ff, u=ff)
    kinds["pp"], kinds["pq"] = ((heads, plen, plen), BF), ((heads, qlen, qlen), BF)
    kinds["x_mid"] = ((total, feat), F32)
    return [kinds[name] for name in SAVED]


def forward(qx, px, lookup, grid, qseg, pseg, gains, labels, matrices):
    qlen, feat = qx.shape
    plen, heads, hidden = px.shape[0], grid.shape[0], matrices[4].shape[1]
    total = qlen + plen
    kinds = saved_shapes(total, qlen, plen, feat, hidden, heads)
    small = (PACK, feat)
    shapes = [(small, BF), (small, F32), (small, F32), (small, BF), ((total, feat), F32), ((total, feat), F32)]
    shapes += kinds * LAYERS
    anywhere = pl.BlockSpec(memory_space=pltpu.HBM)
    smem = pl.BlockSpec(memory_space=pltpu.SMEM)
    weights = sum(m.size for m in matrices)
    outs = pl.pallas_call(
        functools.partial(forward_kernel, qlen, plen, 4),
        out_shape=tuple(jax.ShapeDtypeStruct(*s) for s in shapes),
        in_specs=[whole()] * 7 + [smem] + [anywhere] * 8,
        out_specs=(whole(),) * 4 + (anywhere,) * (2 + LAYERS * len(SAVED)),
        scratch_shapes=[pltpu.VMEM(m.shape, BF) for m in matrices]
        + [pltpu.VMEM((LAYERS,) + shape, dtype) for shape, dtype in kinds]
        + [
            pltpu.VMEM((LAYERS + 1, total, feat), F32),
            pltpu.VMEM((heads, plen, plen), F32),
            pltpu.VMEM((heads, qlen, qlen), F32),
            pltpu.VMEM((1, 2 * plen), jnp.int32),
            pltpu.VMEM((1, 128), jnp.int32),
            pltpu.SemaphoreType.DMA((8,)),
            pltpu.SemaphoreType.DMA((LAYERS * len(SAVED),)),
            pltpu.SemaphoreType.DMA((2,)),
        ],
        name="forward",
        compiler_params=pltpu.CompilerParams(vmem_limit_bytes=56 << 20),
        cost_estimate=pl.CostEstimate(
            flops=2 * LAYERS * total * weights, bytes_accessed=2 * weights, transcendentals=LAYERS * total * hidden
        ),
    )(qx, px, lookup[None], grid, qseg, pseg, gains, labels, *matrices)
    saved = [dict(zip(SAVED, outs[6 + n * len(SAVED) : 6 + (n + 1) * len(SAVED)])) for n in range(LAYERS)]
    return outs[:6], saved


def loss_kernel(
    narrow, stages, me_ref, sharp_ref, here_ref, there_ref, vec_ref, e_ref, x_ref, gain_ref,
    qseg_ref, pseg_ref, wp_ref, gx_ref, ggain_ref, loss_ref, ge_ref, flat_s,
):
    half = here_ref.shape[0]
    flat_s[:half, :] = here_ref[...]
    flat_s[half:, :] = there_ref[...]
    size = 2 * half
    tile = min(size, 256)
    sharp = sharp_ref[0]
    lane = lax.broadcasted_iota(jnp.int32, (1, size), 1)
    block, slot = lax.shift_right_logical(lane, 3), lane & (PACK - 1)
    dw, dn = jnp.zeros_like(block), jnp.zeros_like(block)
    for k, (axis, bit) in enumerate(stages):
        on = (lax.shift_right_logical(block, k) & 1) * bit
        dw, dn = (dw + on, dn) if axis == "wide" else (dw, dn + on)
    device = (dw ^ me_ref[0]) * narrow + (dn ^ me_ref[1])
    is_passage = (slot >= QSEGS) & (slot < QSEGS + PSEGS)
    document = jnp.where(is_passage, device * PSEGS + slot - QSEGS, -2)
    row = lax.broadcasted_iota(jnp.int32, (tile, 1), 0)
    row_slot = row & (PACK - 1)
    is_query = row_slot < QSEGS
    across = lax.broadcasted_iota(jnp.int32, (tile, tile), 1)
    source = low((across == row - row_slot + PACK - 1).astype(F32))
    place = lax.broadcasted_iota(jnp.int32, (tile, 128), 1)
    weigh = jnp.where(place == row_slot, 32.0, 0.0) + jnp.where(place == row_slot + QSEGS, 1.0, 0.0)
    mine = lax.broadcasted_iota(jnp.int32, (1, 128), 1) < PACK
    grad = None
    for t in range(size // tile):
        rows = flat_s[t * tile : (t + 1) * tile, :]
        match = dot_nt(rows, flat_s[...]) / sharp
        match = jnp.where(is_passage, match, MASKED)
        label = jnp.sum(product(source, rows[:, :128]) * weigh, axis=1, keepdims=True)
        hit = (label.astype(jnp.int32) == document) & is_query
        top = jnp.max(match, axis=1, keepdims=True)
        ex = jnp.exp(match - top)
        line = jnp.sum(ex, axis=1, keepdims=True)
        g = (ex / line - hit.astype(F32)) / sharp
        g = low(jnp.where(is_query & is_passage, g, 0.0))
        back = dot_tn(jnp.where(mine, g[:, :128], jnp.zeros_like(g[:, :128])), rows)[:PACK]
        if t == 0:
            part = jnp.sum(jnp.where(hit, match, 0.0), axis=1, keepdims=True)
            part = jnp.where(is_query & (row < PACK), top + jnp.log(line) - part, 0.0)
            loss_ref[...] = jnp.broadcast_to(jnp.sum(part, axis=0, keepdims=True), loss_ref.shape)
            grad = product(g[:16], flat_s[...])[:PACK]
        grad = grad + back
    e, vec = e_ref[...], vec_ref[...]
    scale = lax.rsqrt(jnp.sum(e * e, axis=-1, keepdims=True) + EPSILON)
    ge = low((grad - vec * jnp.sum(vec * grad, axis=-1, keepdims=True)) * scale)
    ge_ref[...] = ge
    qt, pt = segment_table(qseg_ref, 0), segment_table(pseg_ref, QSEGS)
    sizes = jnp.sum(qt, axis=1, keepdims=True) + jnp.sum(pt, axis=1, keepdims=True)
    pooled = dot_nt(ge, wp_ref[...]) / jnp.maximum(sizes, 1.0)
    qlen = qseg_ref.shape[1]
    gain = gain_ref[...]
    total = None
    for table, start, count in ((qt, 0, qlen), (pt, qlen, pseg_ref.shape[1])):
        gz = dot_tn(table, pooled, HIGHEST)
        x = x_ref[start : start + count, :]
        r = lax.rsqrt(jnp.mean(x * x, axis=-1, keepdims=True) + EPSILON)
        unit = x * r
        scaled = gz * gain
        gx_ref[start : start + count, :] = r * (
            scaled - unit * jnp.mean(unit * scaled, axis=-1, keepdims=True)
        )
        part = jnp.sum(gz * unit, axis=0, keepdims=True)
        total = part if total is None else total + part
    ggain_ref[...] = total


BACK = ("grad_f", "ga", "gb", "gy", "gq", "gk", "gv", "ds", "grad_f1", "ga1", "gb1", "grad_x")


def through_norm(x, gain, grad):
    r = unit_scale(x)
    unit = x * r
    scaled = grad * gain
    back = r * (scaled - unit * jnp.mean(unit * scaled, axis=-1, keepdims=True))
    return back, jnp.sum(grad * unit, axis=0, keepdims=True)


def back_kernel(narrow, stages, qlen, n_tiles, n_held, *refs):
    me_ref, sharp_ref, here_ref, there_ref, vec_ref, e_ref, gains_ref, qseg_ref, pseg_ref = refs[:9]
    refs = refs[9:]
    hbm, refs = refs[:n_held], refs[n_held:]
    ggain_ref, loss_ref, ge_ref, gmid_ref, gin_ref = refs[:5]
    outs, refs = dict(zip(BACK, refs[5 : 5 + len(BACK)])), refs[5 + len(BACK) :]
    held, refs = refs[:n_held], refs[n_held:]
    keep, refs = dict(zip(BACK, refs[: len(BACK)])), refs[len(BACK) :]
    flat_s, gx_s, go_s, in_sem, out_sem = refs
    fetch = [pltpu.make_async_copy(a, b, in_sem.at[i]) for i, (a, b) in enumerate(zip(hbm, held))]
    for c in fetch:
        c.start()
    (x2_s, wp_s, wd_s, da_s, db_s, wg_s, wu_s, xm_s, wo_s, v_s, o_s, pp_s, k_s, q_s, pq_s) = held[:15]
    wq_s, wk_s, wv_s, x_s, da1_s, db1_s = held[15:]

    def send(*names):
        for name in names:
            pltpu.make_async_copy(keep[name], outs[name], out_sem.at[BACK.index(name)]).start()

    fetch[0].wait()
    fetch[1].wait()
    loss_kernel(
        narrow, stages, me_ref, sharp_ref, here_ref, there_ref, vec_ref, e_ref, x2_s, gains_ref.at[2:3],
        qseg_ref, pseg_ref, wp_s, gx_s, ggain_ref, loss_ref, ge_ref, flat_s,
    )

    def gated_back(x_ref, da, db, names):
        grad_f = low(x_ref[...])
        keep[names[0]][...] = grad_f
        size = da.shape[1] // n_tiles
        for t in range(n_tiles):
            lanes = slice(t * size, (t + 1) * size)
            gu = dot_nt(grad_f, wd_s[lanes, :])
            keep[names[1]][:, lanes] = low(gu * da[:, lanes].astype(F32))
            keep[names[2]][:, lanes] = low(gu * db[:, lanes].astype(F32))
        send(*names)

    for i in (2, 3, 4):
        fetch[i].wait()
    gated_back(gx_s, da_s, db_s, BACK[:3])
    for i in (5, 6, 7):
        fetch[i].wait()
    grad = dot_nt(keep["ga"][...], wg_s[...]) + dot_nt(keep["gb"][...], wu_s[...])
    back, gmid_ref[...] = through_norm(xm_s[...], gains_ref[1:2, :], grad)
    grad_mid = gx_s[...] + back
    gx_s[...] = grad_mid
    gy = low(grad_mid)
    keep["gy"][...] = gy
    send("gy")
    fetch[8].wait()
    go_s[...] = low(dot_nt(gy, wo_s[...]))
    for i in range(9, 15):
        fetch[i].wait()
    attend_back_kernel(
        qlen, q_s, k_s, v_s, o_s, go_s, pp_s, pq_s, None, keep["gq"], keep["gk"], keep["gv"], keep["ds"]
    )
    send("gq", "gk", "gv", "ds")
    for i in range(15, 19):
        fetch[i].wait()
    grad = dot_nt(keep["gq"][...], wq_s[...]) + dot_nt(keep["gk"][...], wk_s[...])
    grad = grad + dot_nt(keep["gv"][...], wv_s[...])
    back, gin_ref[...] = through_norm(x_s[...], gains_ref[0:1, :], grad)
    keep["grad_x"][...] = gx_s[...] + back
    send("grad_x")
    fetch[19].wait()
    fetch[20].wait()
    gated_back(keep["grad_x"], da1_s, db1_s, BACK[8:11])
    for name in BACK:
        pltpu.make_async_copy(keep[name], outs[name], out_sem.at[BACK.index(name)]).wait()


def loss_and_back(me, narrow, stages, sharp, here, there, vec, e, gains, qseg, pseg, x_last, x_in, first, second, matrices):
    wq, wk, wv, wo, wg, wu, wd, wp = matrices
    total, feat = x_last.shape
    qlen, plen = qseg.shape[1], pseg.shape[1]
    heads, hidden = second["pp"].shape[0], wd.shape[0]
    size = 2 * here.shape[0]
    t = second
    fetched = [x_last, wp, wd, t["da"], t["db"], wg, wu, t["x_mid"], wo, t["v"], t["o"], t["pp"], t["k"], t["q"], t["pq"]]
    fetched += [wq, wk, wv, x_in, first["da"], first["db"]]
    tok, ff = ((total, feat), BF), ((total, hidden), BF)
    kinds = [tok, ff, ff, tok, tok, tok, tok, ((heads, plen, plen), F32), tok, ff, ff, ((total, feat), F32)]
    small = [((1, feat), F32), ((1, 128), F32), ((PACK, feat), BF), ((1, feat), F32), ((1, feat), F32)]
    anywhere = pl.BlockSpec(memory_space=pltpu.HBM)
    smem = pl.BlockSpec(memory_space=pltpu.SMEM)
    weights = sum(m.size for m in matrices)
    outs = pl.pallas_call(
        functools.partial(back_kernel, narrow, stages, qlen, 4, len(fetched)),
        out_shape=tuple(jax.ShapeDtypeStruct(*s) for s in small + kinds),
        in_specs=[smem, smem] + [whole()] * 7 + [anywhere] * len(fetched),
        out_specs=(whole(),) * 5 + (anywhere,) * len(kinds),
        scratch_shapes=[pltpu.VMEM(a.shape, a.dtype) for a in fetched]
        + [pltpu.VMEM(*k) for k in kinds]
        + [
            pltpu.VMEM((size, feat), BF),
            pltpu.VMEM((total, feat), F32),
            pltpu.VMEM((total, feat), BF),
            pltpu.SemaphoreType.DMA((len(fetched),)),
            pltpu.SemaphoreType.DMA((len(kinds),)),
        ],
        name="loss_and_back",
        compiler_params=pltpu.CompilerParams(vmem_limit_bytes=56 << 20),
        cost_estimate=pl.CostEstimate(
            flops=3 * total * weights, bytes_accessed=2 * weights, transcendentals=0
        ),
    )(me, sharp, here, there, vec, e, gains, qseg, pseg, *fetched)
    return outs[:5], dict(zip(BACK, outs[5:]))


def join_kernel(*refs):
    ins, out_ref = refs[:-1], refs[-1]
    rows = ins[0].shape[0]
    for i, ref in enumerate(ins):
        out_ref[i * rows : (i + 1) * rows, :] = ref[...]


def join(*parts):
    a = parts[0]
    return pl.pallas_call(
        join_kernel,
        out_shape=jax.ShapeDtypeStruct((len(parts) * a.shape[0], a.shape[1]), a.dtype),
        in_specs=[whole()] * len(parts),
        out_specs=whole(),
        name="join",
        compiler_params=pltpu.CompilerParams(vmem_limit_bytes=4 << 20),
    )(*parts)


def stage_orders(wide, narrow):
    wbits = [1 << i for i in range(wide.bit_length() - 1)]
    nbits = [1 << i for i in range(narrow.bit_length() - 1)]
    w = lambda bits: [("wide", b) for b in bits]
    n = [("narrow", b) for b in nbits]
    tail = w(wbits[2:])
    return (w(wbits[:1]) + w(wbits[1:2]) + n + tail, w(wbits[:1]) + n + w(wbits[1:2]) + tail)


def place_of(order, dw, dn):
    place = 0
    for axis, bit in order:
        own = dw if axis == "wide" else dn
        place = place * 2 + (own // bit) % 2
    return place


def traced_place(order, dw, dn):
    place = 0
    for axis, bit in order:
        own = dw if axis == "wide" else dn
        place = place * 2 + (lax.shift_right_logical(own, bit.bit_length() - 1) & 1)
    return place


def wgrad_kernel(jobs, groups, n_ops, me_ref, *refs):
    ops, (keep_ref, send_ref) = refs[:n_ops], refs[n_ops : n_ops + 2]
    held = refs[n_ops + 2 : n_ops + 2 + len(groups)]
    turned_s, sems = refs[-2:]
    me_w, me_n = me_ref[0], me_ref[1]
    half = keep_ref.shape[0]
    copies = []
    for ids, buf in zip(groups, held):
        first, own = 0, []
        for i in ids:
            count = ops[i].shape[0]
            sem = sems.at[sum(len(c) for c in copies) + len(own)]
            own.append(pltpu.make_async_copy(ops[i], buf.at[first : first + count], sem))
            first += count
        copies.append(own)
    for own in copies:
        for c in own:
            c.start()
    ready = set()

    def arrive(g):
        if g not in ready:
            for c in copies[g]:
                c.wait()
            ready.add(g)

    def store(acc, job, w_first, n_first):
        row_axis, block_rows, block_lanes, targets = job[2:]
        blocks = [
            (bi, bj)
            for bi in range(acc.shape[0] // block_rows)
            for bj in range(acc.shape[1] // block_lanes)
        ]
        bases = [traced_place(t[0], w_first ^ me_w, n_first ^ me_n) for t in targets]
        for core in range(2):

            @pl.when((me_w & 1) == core)
            def _():
                for bi, bj in blocks:
                    w, n = (bi, bj) if row_axis == "wide" else (bj, bi)
                    out_ref = keep_ref if (w & 1) == core else send_ref
                    for (order, first, count, offset), base in zip(targets, bases):
                        at = (base ^ place_of(order, w, n)) & (half - 1)
                        for k in range(block_lanes // 128):
                            lane = bj * block_lanes + k * 128
                            row = bi * block_rows + first
                            out_ref[at, offset + k * count : offset + (k + 1) * count, :] = acc[
                                row : row + count, lane : lane + 128
                            ]

    for job in jobs:
        rg, lg, row_axis, block_rows, block_lanes, targets = job
        arrive(rg)
        arrive(lg)
        row_s, lane_s = held[rg], held[lg]
        depth, rows, lanes = row_s.shape[0], row_s.shape[1], lane_s.shape[1]
        tile_rows = 384
        tile_lanes = block_lanes
        while tile_lanes < 512 and lanes % (2 * tile_lanes) == 0:
            tile_lanes *= 2
        per_row, per_lane = tile_rows // block_rows, tile_lanes // block_lanes

        def row_step(rt, carry):
            mine = row_s[:, pl.ds(pl.multiple_of(rt * tile_rows, 128), tile_rows)]
            if depth > 16:
                turned_s[...] = mine.T

            def lane_step(lt, inner):
                part = lane_s[:, pl.ds(pl.multiple_of(lt * tile_lanes, 128), tile_lanes)]
                acc = product(turned_s[...], part) if depth > 16 else dot_tn(mine, part)
                if row_axis == "wide":
                    store(low(acc), job, rt * per_row, lt * per_lane)
                else:
                    store(low(acc), job, lt * per_lane, rt * per_row)
                return inner

            if lanes == tile_lanes:
                return lane_step(0, carry)
            return lax.fori_loop(0, lanes // tile_lanes, lane_step, carry)

        lax.fori_loop(0, rows // tile_rows, row_step, 0)


def wgrad(me, ops, groups, jobs, total_rows, wide, narrow, vmem):
    half = wide * narrow // 2
    width = lambda g: ops[groups[g][0]].shape[1]
    depth = [sum(ops[i].shape[0] for i in g) for g in groups]
    full = []
    for rg, lg, row_axis, targets in jobs:
        split = (wide, narrow) if row_axis == "wide" else (narrow, wide)
        full.append((rg, lg, row_axis, width(rg) // split[0], width(lg) // split[1], targets))
    flops = sum(2 * depth[j[0]] * width(j[0]) * width(j[1]) for j in full)
    return pl.pallas_call(
        functools.partial(wgrad_kernel, full, groups, len(ops)),
        out_shape=(jax.ShapeDtypeStruct((half, total_rows, 128), BF),) * 2,
        in_specs=[pl.BlockSpec(memory_space=pltpu.SMEM)]
        + [pl.BlockSpec(memory_space=pltpu.HBM)] * len(ops),
        out_specs=(whole(),) * 2,
        scratch_shapes=[pltpu.VMEM((d, width(g)), BF) for g, d in enumerate(depth)]
        + [pltpu.VMEM((384, max(depth)), BF), pltpu.SemaphoreType.DMA((sum(map(len, groups)),))],
        name="wgrad",
        compiler_params=pltpu.CompilerParams(vmem_limit_bytes=vmem << 20),
        cost_estimate=pl.CostEstimate(flops=flops, bytes_accessed=flops // 256, transcendentals=0),
    )(me, *ops)


def swap(a, *stage):
    dw = sum(bit for axis, bit in stage if axis == "wide")
    dn = sum(bit for axis, bit in stage if axis == "narrow")
    wide, narrow = lax.axis_size("wide"), lax.axis_size("narrow")
    if not dn:
        return lax.ppermute(a, "wide", [(i, i ^ dw) for i in range(wide)])
    if not dw:
        return lax.ppermute(a, "narrow", [(i, i ^ dn) for i in range(narrow)])
    pairs = [(i * narrow + j, (i ^ dw) * narrow + (j ^ dn)) for i in range(wide) for j in range(narrow)]
    return lax.ppermute(a, AXES, pairs)


def relatives(stage):
    if len(stage) == 1:
        return [stage]
    return [(stage[1],), (stage[0],), tuple(stage)]


def grouped(order, direct):
    if not direct:
        return [(s,) for s in order]
    return [(s,) for s in order[:-2]] + [tuple(order[-2:])]


class Chunk:
    def __init__(self, keep, send, split, orders, finals, direct=False):
        self.rows, self.split, self.finals = keep.shape[1], split, finals
        self.orders = [grouped(order, direct) for order in orders]
        self.stage, self.parts = 0, [(keep, send)]
        self.done = False

    def spans(self, stage):
        if self.orders[0][stage] == self.orders[1][stage] and (
            stage == 0 or self.orders[0][stage:] == self.orders[1][stage:]
        ):
            return [(0, self.rows, self.orders[0])]
        return [(0, self.split, self.orders[0]), (self.split, self.rows, self.orders[1])]

    def start(self):
        return [
            [swap(a, *to) for a, to in zip(part[1:], relatives(order[self.stage]))]
            for part, (_, _, order) in zip(self.parts, self.spans(self.stage))
        ]


def doubled(value, stages):
    for stage in stages:
        value = value + swap(value, stage)
    return value


def advance(flows):
    operands, shapes, steps = [], [], []
    for f in flows:
        now = f.spans(f.stage)
        last = f.stage == len(f.orders[0]) - 1
        first_in, first_out = len(operands), len(shapes)
        for part, got in zip(f.parts, f.got):
            operands += [part[0]] + got
        half = f.parts[0][0].shape[0] // 2
        if last:
            for kind, offset, rows, lanes in f.finals:
                shapes.append(jax.ShapeDtypeStruct((rows, lanes), F32))
            steps.append(("final", first_in, first_out, f.finals, len(f.got[0])))
        else:
            later = f.spans(f.stage + 1)
            ways = 2 ** len(f.orders[0][f.stage + 1])
            for lo, hi, _ in later:
                shapes += [jax.ShapeDtypeStruct((2 * half // ways, hi - lo, 128), BF)] * ways
            steps.append(
                ("halve", first_in, first_out, [n[:2] for n in now], [n[:2] for n in later], ways)
            )

    def whole_sum(ins, i, count, pick):
        total = pick(ins[i]) + pick(ins[i + 1])
        return total if count == 1 else total + (pick(ins[i + 2]) + pick(ins[i + 3]))

    def body(*refs):
        ins, outs = refs[: len(operands)], refs[len(operands) :]
        for step in steps:
            kind, i, o = step[:3]
            if kind == "final":
                for n, (_, offset, rows, lanes) in enumerate(step[3]):
                    for k in range(lanes // 128):
                        span = pl.ds(offset + k * rows, rows)
                        value = whole_sum(ins, i, step[4], lambda ref: ref[0, span, :].astype(F32))
                        outs[o + n][:, k * 128 : (k + 1) * 128] = value
            else:
                ways = step[5]
                for p, (lo, hi) in enumerate(step[3]):
                    for q, (lo2, hi2) in enumerate(step[4]):
                        a, b = max(lo, lo2), min(hi, hi2)
                        if a >= b:
                            continue
                        keep_ref, got_ref = ins[i + 2 * p], ins[i + 2 * p + 1]
                        count = keep_ref.shape[0] // ways
                        for side in range(ways):
                            out_ref = outs[o + ways * q + side]

                            def block(n, carry):
                                src = pl.ds(a - lo, b - a)
                                value = keep_ref[side * count + n, src, :].astype(F32)
                                value = value + got_ref[side * count + n, src, :].astype(F32)
                                out_ref[n, a - lo2 : b - lo2, :] = low(value)
                                return carry

                            if count == 1:
                                block(0, 0)
                            else:
                                lax.fori_loop(0, count, block, 0)

    room = (1 << 20) + sum(a.size * a.dtype.itemsize for a in operands + shapes)
    outs = pl.pallas_call(
        body,
        out_shape=tuple(shapes),
        in_specs=[whole()] * len(operands),
        out_specs=(whole(),) * len(shapes),
        name="advance",
        compiler_params=pltpu.CompilerParams(vmem_limit_bytes=room),
    )(*operands)
    at = 0
    for f, step in zip(flows, steps):
        f.stage += 1
        if step[0] == "final":
            f.result = [
                out.T if final[0] == "turn" else out
                for out, final in zip(outs[at : at + len(step[3])], step[3])
            ]
            at += len(step[3])
            f.done = True
        else:
            ways = step[5]
            f.parts = [tuple(outs[at + ways * q : at + ways * (q + 1)]) for q in range(len(step[4]))]
            at += ways * len(step[4])


def exchange(begin, compute, inputs):
    sent, inputs = lax.optimization_barrier(([f.parts for f in begin], inputs))
    for f, value in zip(begin, sent):
        f.parts = value
    for f in begin:
        f.got = f.start()
    got, made = lax.optimization_barrier(([f.got for f in begin], compute(*inputs)))
    for f, value in zip(begin, got):
        f.got = value
    advance(begin)
    return made


def gather_stages(order):
    far, near = order[3:], order[1:3]
    return [far[i : i + 2] for i in range(0, len(far), 2)] + [near] + [order[:1]]


def gather_all(rows, stages):
    for stage in stages[:-1]:
        got = [swap(rows, *to) for to in ([stage] if len(stage) == 1 else [stage[:1], stage[1:], stage])]
        rows = join(rows, *got)
    return rows, swap(rows, *stages[-1])


def local(
    wide,
    narrow,
    query_x,
    query_seg,
    passage_x,
    passage_seg,
    labels,
    lookup,
    softness,
    bias_grid,
    gains,
    wq,
    wk,
    wv,
    wo,
    wg,
    wu,
    wd,
    wp,
):
    qrows, qlen, feat = query_x.shape
    prows, plen, _ = passage_x.shape
    buckets, heads = bias_grid.shape
    order_a, order_b = stage_orders(wide, narrow)
    me_w, me_n = lax.axis_index("wide"), lax.axis_index("narrow")
    me = jnp.stack([me_w, me_n]).astype(jnp.int32)

    hidden = wd.shape[0]
    block, cols, ff_block, ff_cols = feat // wide, feat // narrow, hidden // wide, hidden // narrow
    matrices = (wq, wk, wv, wo, wg, wu, wd, wp)
    (packed, vectors, e, pooled, x_between, x_last), (first, second) = forward(
        query_x.reshape(-1, feat),
        passage_x.reshape(-1, feat),
        lookup,
        bias_grid.T,
        query_seg,
        passage_seg,
        gains,
        labels,
        matrices,
    )
    groups = gather_stages(order_a)
    stages = [bit for group in groups for bit in group]
    here, there = gather_all(packed, groups)
    (gain_final, loss_part, grad_e, gain_mid, gain_in), back = loss_and_back(
        me, narrow, stages, softness, here, there, vectors, e, gains, query_seg, passage_seg,
        x_last, x_between, first, second, matrices,
    )
    gain_mid, gain_in = gain_mid[0], gain_in[0]
    ffn_2 = (back["grad_f"], back["ga"], back["gb"])
    att_2 = (back["gy"], back["gq"], back["gk"], back["gv"])
    acc, grad_x = back["ds"], back["grad_x"]
    grad_f, grad_a, grad_b = back["grad_f1"], back["ga1"], back["gb1"]
    h, q, k, v, pp, pq, o, x_mid, normed, _, _, u = (first[name] for name in SAVED)
    h_2, o_2, normed_2, u_2 = second["h"], second["o"], second["normed"], second["u"]

    def attention_back(grad_a, grad_b):
        grad_normed = dot_nt(grad_a, wg) + dot_nt(grad_b, wu)
        back_mid, more = norm_back(x_mid, gains[1], grad_normed)
        grad_mid = grad_x + back_mid
        grad_y = low(grad_mid)
        grad_o = low(dot_nt(grad_y, wo))
        grad_q, grad_k, grad_v, total = attend_back(q, k, v, o, grad_o, pp, pq, acc)
        return grad_mid, gain_mid + more, grad_y, grad_q, grad_k, grad_v, total

    def input_back(grad_q, grad_k, grad_v, grad_mid, gain_mid, acc):
        grad_h = dot_nt(grad_q, wq) + dot_nt(grad_k, wk) + dot_nt(grad_v, wv)
        x = jnp.concatenate([query_x.reshape(-1, feat), passage_x.reshape(-1, feat)], axis=0).astype(F32)
        back_in, more = norm_back(x, gains[0], grad_h)
        sums = small_sums(
            acc, lookup, buckets, (gain_in + more)[None], gain_mid[None], gain_final, loss_part
        )
        return grad_mid + back_in, sums

    if cols % 128 or ff_block % 128 or block % 16:
        grad_mid, gain_mid, grad_y, grad_q, grad_k, grad_v, acc = attention_back(grad_a, grad_b)
        grad_x, sums = input_back(grad_q, grad_k, grad_v, grad_mid, gain_mid, acc)
        sums = doubled(sums, order_a)

        def scatter(*pairs):
            full = low(sum(dot_tn(left, right) for left, right in pairs))
            full = lax.psum_scatter(full, "wide", scatter_dimension=1, tiled=True)
            return lax.psum_scatter(full, "narrow", scatter_dimension=0, tiled=True).astype(F32)

        grad_query = scatter((h, grad_q), (h_2, att_2[1]))
        grad_key = scatter((h, grad_k), (h_2, att_2[2]))
        grad_value = scatter((h, grad_v), (h_2, att_2[3]))
        grad_out = scatter((o, grad_y), (o_2, att_2[0]))
        grad_gate = scatter((normed, grad_a), (normed_2, ffn_2[1]))
        grad_up = scatter((normed, grad_b), (normed_2, ffn_2[2]))
        grad_down = scatter((u, grad_f), (u_2, ffn_2[0]))
        grad_proj = scatter((pooled, grad_e))
    else:
        orders = (order_a, order_b)
        down_rows, att_rows = block * ff_cols // 128, block * cols // 128
        parts = wgrad(
            me,
            [grad_f, ffn_2[0], u, u_2, normed, normed_2, grad_a, ffn_2[1]],
            [(0, 1), (2, 3), (4, 5), (6, 7)],
            [
                (0, 1, "wide", [(order_a, 0, block, 0)]),
                (2, 3, "narrow", [(order_b, 0, cols, down_rows)]),
            ],
            down_rows + cols,
            wide,
            narrow,
            16,
        )
        finals = [("turn", 0, block, ff_cols), ("keep", down_rows, cols, ff_block)]
        ffn = Chunk(*parts, down_rows, orders, finals)

        cut = (cols + att_rows) // 2 // 16 * 16

        def make_up(grad_b, *rest):
            return wgrad(
                me,
                [normed, normed_2, grad_b, ffn_2[2], grad_e, pooled],
                [(0, 1), (2, 3), (4,), (5,)],
                [
                    (0, 1, "narrow", [(order_a, 0, cut, 0), (order_b, cut, cols - cut, cut)]),
                    (2, 3, "wide", [(order_b, 0, block, cols)]),
                ],
                cols + att_rows,
                wide,
                narrow,
                12,
            )

        parts = exchange([ffn], make_up, (grad_b, normed, normed_2, grad_a))
        finals = [("keep", 0, cols, ff_block), ("turn", cols, block, cols)]
        up = Chunk(*parts, cut, orders, finals)

        def rest_back(grad_a, grad_b):
            grad_mid, gain_mid, grad_y, grad_q, grad_k, grad_v, acc = attention_back(grad_a, grad_b)
            grad_x, sums = input_back(grad_q, grad_k, grad_v, grad_mid, gain_mid, acc)
            return grad_x, sums, grad_y, grad_q, grad_k, grad_v

        grad_x, sums, *grads = exchange([ffn, up], rest_back, (grad_a, grad_b))

        def make_rest(sums, grad_y, grad_q, grad_k, grad_v):
            got = [swap(sums, *to) for to in relatives(order_a[-2:])]
            parts = wgrad(
                me,
                [grad_y, att_2[0], o, o_2, grad_q, att_2[1], h, h_2, grad_k, att_2[2], grad_v, att_2[3]],
                [(0, 1), (2, 3), (4, 5), (6, 7), (8, 9), (10, 11)],
                [
                    (0, 1, "wide", [(order_a, 0, block, 0)]),
                    (2, 3, "wide", [(order_a, 0, block, att_rows)]),
                    (4, 3, "wide", [(order_b, 0, block, 2 * att_rows)]),
                    (5, 3, "wide", [(order_b, 0, block, 3 * att_rows)]),
                ],
                4 * att_rows,
                wide,
                narrow,
                12,
            )
            got, parts = lax.optimization_barrier((got, parts))
            return parts, (sums + got[0]) + (got[1] + got[2])

        parts, sums = exchange([ffn, up], make_rest, (sums, *grads))
        att = Chunk(*parts, 2 * att_rows, orders, [("turn", i * att_rows, block, cols) for i in range(4)], True)
        for n in range(3):
            live = [f for f in (att, up, ffn) if not f.done]
            sums = exchange(live, lambda value: doubled(value, order_a[n : n + 1]), (sums,))
        exchange([att], lambda: (), ())
        grad_down, grad_gate = ffn.result
        grad_up, grad_proj = up.result
        grad_out, grad_query, grad_key, grad_value = att.result
    gain_total, bucket_total = sums[:3], sums[4 : 4 + heads, :buckets]
    mean_loss = sums[3, :1] / (qrows * QSEGS * wide * narrow)
    return (
        mean_loss,
        vectors[:QSEGS],
        vectors[QSEGS : QSEGS + PSEGS],
        grad_x[:qlen].reshape(1, qlen, feat),
        grad_x[qlen:].reshape(1, plen, feat),
        gain_total,
        bucket_total.T,
        grad_query,
        grad_key,
        grad_value,
        grad_out,
        grad_gate,
        grad_up,
        grad_down,
        grad_proj,
    )


def solution(mesh):
    rows3, rows2, rows1 = P(AXES, None, None), P(AXES, None), P(AXES)
    return jax.shard_map(
        functools.partial(local, mesh.shape["wide"], mesh.shape["narrow"]),
        mesh=mesh,
        in_specs=(rows3, rows2, rows3, rows2, rows1) + (P(),) * 12,
        out_specs=(P(), rows2, rows2, rows3, rows3, P(), P()) + (P("narrow", "wide"),) * 8,
        check_vma=False,
    )
```

profile of v0, /device:TPU:0, one launch (start us, length us, event | category | flops | bytes accessed | tf_op | source)
XLA Modules:
  0.0 205.2 jit_solution(15383185308782811530)
XLA Ops:
  0.6 30.4 %forward.1 = (bf16[8,768]{1,0:T(8,128)(2,1)}, f32[8,768]{1,0:T(8,128)}, f32[8,768]{1,0:T(8,128)}, bf16[8,768]{1,0:T(8,128)(2,1)}, f32[320,768]{1,0:T(8,128)}, /*...) custom-call(bf16[64,768]{1,0:T(8,128)(2,1)} %bitcast.37, ...), custom_call_target="tpu_custom_call" | custom-call | flops 9814671360 | bytes 15335424 | tf_op jit(solution)/shard_map/forward/pallas_call | solution.py:380
  31.1 3.1 %collective-permute-start = (bf16[8,768]{1,0:T(8,128)(2,1)}, bf16[8,768]{1,0:T(8,128)(2,1)S(1)}, u32[]{:S(2)}, u32[]{:S(2)}) collective-permute-start(bf16[8,768]{1,0:T(8,128)(2,1)} %get-tuple-element.210.refs_0_), channel_id=1, source_target_pairs={{0,8},{2,10},{4,12},{6,14},{8,0},{10,2},{12,4},{14,6},{16,24},{18,... | collective-permute-start | bytes 36872 | tf_op jit(solution)/shard_map/ppermute | solution.py:752
  34.2 2.6 %collective-permute-start.1 = (bf16[8,768]{1,0:T(8,128)(2,1)}, bf16[8,768]{1,0:T(8,128)(2,1)S(1)}, u32[]{:S(2)}, u32[]{:S(2)}) collective-permute-start(bf16[8,768]{1,0:T(8,128)(2,1)} %get-tuple-element.210.refs_0_), channel_id=1, source_target_pairs={{0,16},{2,18},{4,20},{6,22},{8,24},{10,26},{12,28},{14,30},{16,0},... | collective-permute-start | bytes 36872 | tf_op jit(solution)/shard_map/ppermute | solution.py:752
  36.8 2.2 %collective-permute-done.1.refs_2_ = bf16[8,768]{1,0:T(8,128)(2,1)S(1)} collective-permute-done((bf16[8,768]{1,0:T(8,128)(2,1)}, bf16[8,768]{1,0:T(8,128)(2,1)S(1)}, u32[]{:S(2)}, u32[]{:S(2)}) %collective-permute-start.1) | collective-permute-done | bytes 12320 | tf_op jit(solution)/shard_map/ppermute | solution.py:752
  39.0 3.5 %collective-permute-done.2.refs_3_ = bf16[8,768]{1,0:T(8,128)(2,1)S(1)} collective-permute-done((bf16[8,768]{1,0:T(8,128)(2,1)}, bf16[8,768]{1,0:T(8,128)(2,1)S(1)}, u32[]{:S(2)}, u32[]{:S(2)}) %collective-permute-start.2) | collective-permute-done | bytes 12320 | tf_op jit(solution)/shard_map/ppermute | solution.py:752
  42.5 0.7 copy-done.9
  43.2 1.5 collective-permute-start.3
  44.7 1.5 collective-permute-start.4
  46.7 0.7 collective-permute-done.3.refs_1_
  47.4 1.4 collective-permute-done.4.refs_2_
  48.8 2.4 %collective-permute-done.5.refs_3_ = bf16[32,768]{1,0:T(8,128)(2,1)S(1)} collective-permute-done((bf16[32,768]{1,0:T(8,128)(2,1)S(1)}, bf16[32,768]{1,0:T(8,128)(2,1)S(1)}, u32[]{:S(2)}, u32[]{:S(2)}) %collective-permute-start.5) | collective-permute-done | bytes 49184 | tf_op jit(solution)/shard_map/ppermute | solution.py:756
  52.7 0.7 copy-done.43
  53.4 21.7 %loss_and_back.1 = (f32[1,768]{1,0:T(1,128)}, f32[1,128]{1,0:T(1,128)}, bf16[8,768]{1,0:T(8,128)(2,1)}, f32[1,768]{1,0:T(1,128)}, f32[1,768]{1,0:T(1,128)}, /*in...) custom-call(s32[2]{0:T(128)} %pad_add_fusion.refs_0_.me_ref, ...), custom_call_target="tpu_custom_call" | custom-call | flops 7361003520 | bytes 15335424 | tf_op jit(solution)/shard_map/loss_and_back/pallas_call | solution.py:574
  75.2 1.3 copy-done.15
  76.6 1.3 copy-done.18
  77.9 1.0 copy-done.23
  78.9 1.0 copy-done.24
  80.0 10.7 %wgrad.3 = (bf16[16,768,128]{2,1,0:T(8,128)(2,1)S(1)}, bf16[16,768,128]{2,1,0:T(8,128)(2,1)S(1)}) custom-call(s32[2]{0:T(128)S(1)} %copy-done.12, bf16[320,768]{1,0:T(8,128)(2,1)S(1)} %copy-done.24, bf16[320,768]{1,0:T(8,128)(2,1)S(1)} %copy-done.23, bf16[320,2048]{1,0:T(8,128)(2,1)S(1)} %copy-done.28, bf16[320,2048]{1,0:T(8,128)(2,1)S(1)} %copy-done.29, ...), custom_call_target="tpu_custom_call" | custom-call | flops 4026531840 | bytes 15728640 | tf_op jit(solution)/shard_map/wgrad/pallas_call | solution.py:733
  92.0 6.8 %wgrad.4 = (bf16[16,528,128]{2,1,0:T(8,128)(2,1)S(1)}, bf16[16,528,128]{2,1,0:T(8,128)(2,1)S(1)}) custom-call(s32[2]{0:T(128)S(1)} %copy-done.12, bf16[320,768]{1,0:T(8,128)(2,1)S(1)} %copy-done.26, bf16[320,768]{1,0:T(8,128)(2,1)S(1)} %copy-done.27, bf16[320,2048]{1,0:T(8,128)(2,1)S(1)} %copy-done.14, bf16[320,2048]{1,0:T(8,128)(2,1)S(1)} %copy-done.17, ...), custom_call_target="tpu_custom_call" | custom-call | flops 2022703104 | bytes 7901184 | tf_op jit(solution)/shard_map/wgrad/pallas_call | solution.py:733
  98.8 0.9 advance.7
  100.1 1.0 copy-done.36
  101.1 1.2 fusion.10
  102.3 0.7 copy-done.37
  103.0 1.5 multiply_reduce_fusion
  106.8 1.0 copy-done
  108.8 5.0 %attend_back.1 = (bf16[320,768]{1,0:T(8,128)(2,1)S(1)}, bf16[320,768]{1,0:T(8,128)(2,1)S(1)}, bf16[320,768]{1,0:T(8,128)(2,1)S(1)}, f32[12,256,256]{2,1,0:T(8,128)S(1)}) custom-call(bf16[320,768]{1,0:T(8,128)(2,1)S(1)} %copy-done.4, bf16[320,768]{1,0:T(8,128)(2,1)S(1)} %copy-done.5, bf16[320,768]{1,0:T(8,128)(2,1)S(1)} %copy-done.6, ...), custom_call_target="tpu_custom_call" | custom-call | flops 402653184 | bytes 9437184 | tf_op jit(solution)/shard_map/attend_back/pallas_call | solution.py:165
  114.4 0.7 copy-done.33
  115.6 0.7 copy-done.40
  116.3 0.8 fusion.5
  117.2 2.0 small_sums.1
  119.6 4.9 %collective-permute-done.8.refs_1_ = bf16[8,384,128]{2,1,0:T(8,128)(2,1)S(1)} collective-permute-done((bf16[8,384,128]{2,1,0:T(8,128)(2,1)S(1)}, bf16[8,384,128]{2,1,0:T(8,128)(2,1)S(1)}, u32[]{:S(2)}, u32[]{:S(2)}) %collective-permute-start.8) | collective-permute-done | bytes 786464 | tf_op jit(solution)/shard_map/ppermute | solution.py:752
  124.7 1.1 advance.8
  125.9 0.8 collective-permute-start.16
  127.1 1.6 collective-permute-start.13
  128.7 3.6 %collective-permute-start.17 = (f32[16,768]{1,0:T(8,128)S(1)}, f32[16,768]{1,0:T(8,128)S(1)}, u32[]{:S(2)}, u32[]{:S(2)}) collective-permute-start(f32[16,768]{1,0:T(8,128)S(1)} %small_sums.1), channel_id=1, source_target_pairs={{0,24},{2,26},{4,28},{6,30},{8,16},{10,18},{12,20},{14,22},{16,8},... | collective-permute-start | bytes 147464 | tf_op jit(solution)/shard_map/ppermute | solution.py:752
  132.3 1.5 collective-permute-start.11
  134.4 10.6 %wgrad.5 = (bf16[16,576,128]{2,1,0:T(8,128)(2,1)S(1)}, bf16[16,576,128]{2,1,0:T(8,128)(2,1)S(1)}) custom-call(s32[2]{0:T(128)S(1)} %copy-done.12, bf16[320,768]{1,0:T(8,128)(2,1)S(1)} %get-tuple-element.298.refs_0_, bf16[320,768]{1,0:T(8,128)(2,1)S(1)} %copy-done.19, bf16[320,768]{1,0:T(8,128)(2,1)S(1)} %copy-done.3, bf16[320,768]{1,0:T(8,128)(2,1)S(1)} %copy-done.7, ...), custom_call_target="tpu_custom_call" | custom-call | flops 3019898880 | bytes 11796480 | tf_op jit(solution)/shard_map/wgrad/pallas_call | solution.py:733
  145.0 3.1 %collective-permute-done.11.refs_1_ = bf16[4,384,128]{2,1,0:T(8,128)(2,1)S(1)} collective-permute-done((bf16[4,384,128]{2,1,0:T(8,128)(2,1)S(1)}, bf16[4,384,128]{2,1,0:T(8,128)(2,1)S(1)}, u32[]{:S(2)}, u32[]{:S(2)}) %collective-permute-start.11) | collective-permute-done | bytes 393248 | tf_op jit(solution)/shard_map/ppermute | solution.py:754
  148.8 1.7 collective-permute-start.21
  150.5 1.5 collective-permute-start.20
  152.0 1.0 collective-permute-start.19
  153.0 1.2 collective-permute-done.22
  154.2 5.8 %collective-permute-done.19.refs_3_ = bf16[4,256,128]{2,1,0:T(8,128)(2,1)S(1)} collective-permute-done((bf16[4,256,128]{2,1,0:T(8,128)(2,1)S(1)}, bf16[4,256,128]{2,1,0:T(8,128)(2,1)S(1)}, u32[]{:S(2)}, u32[]{:S(2)}) %collective-permute-start.19) | collective-permute-done | bytes 262176 | tf_op jit(solution)/shard_map/ppermute | solution.py:754
  160.3 0.9 advance.10
  161.3 1.5 collective-permute-start.23
  162.8 1.0 collective-permute-start.24
  163.8 1.6 collective-permute-start.25
  165.5 2.6 %collective-permute-start.26 = (bf16[1,768,128]{2,1,0:T(8,128)(2,1)S(1)}, bf16[1,768,128]{2,1,0:T(8,128)(2,1)S(1)}, u32[]{:S(2)}, u32[]{:S(2)}) collective-permute-start(bf16[1,768,128]{2,1,0:T(8,128)(2,1)S(1)} %get-tuple-element.358), channel_id=1, source_target_pairs={{0,16},{2,18},{4,20},{6,22},{8,24},{10,26},{12,28},{14,30},{16,0},... | collective-permute-start | bytes 589832 | tf_op jit(solution)/shard_map/ppermute | solution.py:752
  169.8 7.4 %collective-permute-done.27 = f32[16,768]{1,0:T(8,128)S(1)} collective-permute-done((f32[16,768]{1,0:T(8,128)S(1)}, f32[16,768]{1,0:T(8,128)S(1)}, u32[]{:S(2)}, u32[]{:S(2)}) %collective-permute-start.27) | collective-permute-done | bytes 49184 | tf_op jit(solution)/shard_map/ppermute | solution.py:752
  177.3 1.1 advance.11
  178.4 1.0 collective-permute-start.28
  179.5 1.4 collective-permute-start.29
  180.9 0.9 slice_bitcast_fusion
  181.8 1.0 collective-permute-start.31
  182.8 2.4 %collective-permute-start.30 = (bf16[1,528,128]{2,1,0:T(8,128)(2,1)S(1)}, bf16[1,528,128]{2,1,0:T(8,128)(2,1)S(1)}, u32[]{:S(2)}, u32[]{:S(2)}) collective-permute-start(bf16[1,528,128]{2,1,0:T(8,128)(2,1)S(1)} %get-tuple-element.376), channel_id=1, source_target_pairs={{0,16},{2,18},{4,20},{6,22},{8,24},{10,26},{12,28},{14,30},{16,0},... | collective-permute-start | bytes 405512 | tf_op jit(solution)/shard_map/ppermute | solution.py:752
  185.2 0.7 slice_bitcast_fusion.1
  185.9 1.1 collective-permute-done.31
  187.0 3.1 %collective-permute-done.30.refs_5_ = bf16[1,528,128]{2,1,0:T(8,128)(2,1)S(1)} collective-permute-done((bf16[1,528,128]{2,1,0:T(8,128)(2,1)S(1)}, bf16[1,528,128]{2,1,0:T(8,128)(2,1)S(1)}, u32[]{:S(2)}, u32[]{:S(2)}) %collective-permute-start.30) | collective-permute-done | bytes 135200 | tf_op jit(solution)/shard_map/ppermute | solution.py:752
  190.1 0.6 slice.34
  191.3 0.8 advance.12
  192.0 1.1 collective-permute-start.32
  193.1 2.8 %collective-permute-start.33 = (bf16[1,576,128]{2,1,0:T(8,128)(2,1)S(1)}, bf16[1,576,128]{2,1,0:T(8,128)(2,1)S(1)}, u32[]{:S(2)}, u32[]{:S(2)}) collective-permute-start(bf16[1,576,128]{2,1,0:T(8,128)(2,1)S(1)} %get-tuple-element.392), channel_id=1, source_target_pairs={{0,8},{2,10},{4,12},{6,14},{8,0},{10,2},{12,4},{14,6},{16,24},{18,... | collective-permute-start | bytes 442376 | tf_op jit(solution)/shard_map/ppermute | solution.py:752
  197.7 5.6 %collective-permute-done.32.refs_1_ = bf16[1,576,128]{2,1,0:T(8,128)(2,1)S(1)} collective-permute-done((bf16[1,576,128]{2,1,0:T(8,128)(2,1)S(1)}, bf16[1,576,128]{2,1,0:T(8,128)(2,1)S(1)}, u32[]{:S(2)}, u32[]{:S(2)}) %collective-permute-start.32) | collective-permute-done | bytes 147488 | tf_op jit(solution)/shard_map/ppermute | solution.py:752
  203.3 0.7 advance.13
  (146 shorter events, 13.6 us)
Async XLA Ops:
  31.1 5.7 %collective-permute-start = (bf16[8,768]{1,0:T(8,128)(2,1)}, bf16[8,768]{1,0:T(8,128)(2,1)S(1)}, u32[]{:S(2)}, u32[]{:S(2)}) collective-permute-start(bf16[8,768]{1,0:T(8,128)(2,1)} %get-tuple-element.210.refs_0_), channel_id=1, source_target_pairs={{0,8},{2,10},{4,12},{6,14},{8,0},{10,2},{12,4},{14,6},{16,24},{18,... | collective-permute-start | bytes 36872 | tf_op jit(solution)/shard_map/ppermute | solution.py:752
  34.2 4.8 %collective-permute-start.1 = (bf16[8,768]{1,0:T(8,128)(2,1)}, bf16[8,768]{1,0:T(8,128)(2,1)S(1)}, u32[]{:S(2)}, u32[]{:S(2)}) collective-permute-start(bf16[8,768]{1,0:T(8,128)(2,1)} %get-tuple-element.210.refs_0_), channel_id=1, source_target_pairs={{0,16},{2,18},{4,20},{6,22},{8,24},{10,26},{12,28},{14,30},{16,0},... | collective-permute-start | bytes 36872 | tf_op jit(solution)/shard_map/ppermute | solution.py:752
  36.8 5.7 %collective-permute-start.2 = (bf16[8,768]{1,0:T(8,128)(2,1)}, bf16[8,768]{1,0:T(8,128)(2,1)S(1)}, u32[]{:S(2)}, u32[]{:S(2)}) collective-permute-start(bf16[8,768]{1,0:T(8,128)(2,1)} %get-tuple-element.210.refs_0_), channel_id=1, source_target_pairs={{0,24},{2,26},{4,28},{6,30},{8,16},{10,18},{12,20},{14,22},{16,8},... | collective-permute-start | bytes 36872 | tf_op jit(solution)/shard_map/ppermute | solution.py:752
  43.2 4.2 %collective-permute-start.3 = (bf16[32,768]{1,0:T(8,128)(2,1)S(1)}, bf16[32,768]{1,0:T(8,128)(2,1)S(1)}, u32[]{:S(2)}, u32[]{:S(2)}) collective-permute-start(bf16[32,768]{1,0:T(8,128)(2,1)S(1)} %join.2.refs_0_), channel_id=1, source_target_pairs={{0,4},{2,6},{4,0},{6,2},{8,12},{10,14},{12,8},{14,10},{16,20},{18,... | collective-permute-start | bytes 147464 | tf_op jit(solution)/shard_map/ppermute | solution.py:752
  44.7 4.1 %collective-permute-start.4 = (bf16[32,768]{1,0:T(8,128)(2,1)S(1)}, bf16[32,768]{1,0:T(8,128)(2,1)S(1)}, u32[]{:S(2)}, u32[]{:S(2)}) collective-permute-start(bf16[32,768]{1,0:T(8,128)(2,1)S(1)} %join.2.refs_0_), channel_id=1, source_target_pairs={{0,1},{1,0},{2,3},{3,2},{4,5},{5,4},{6,7},{7,6},{8,9},{9,8},{10,11... | collective-permute-start | bytes 147464 | tf_op jit(solution)/shard_map/ppermute | solution.py:754
  46.2 5.0 %collective-permute-start.5 = (bf16[32,768]{1,0:T(8,128)(2,1)S(1)}, bf16[32,768]{1,0:T(8,128)(2,1)S(1)}, u32[]{:S(2)}, u32[]{:S(2)}) collective-permute-start(bf16[32,768]{1,0:T(8,128)(2,1)S(1)} %join.2.refs_0_), channel_id=1, source_target_pairs={{0,5},{1,4},{2,7},{3,6},{4,1},{5,0},{6,3},{7,2},{8,13},{9,12},{10,... | collective-permute-start | bytes 147464 | tf_op jit(solution)/shard_map/ppermute | solution.py:756
  51.2 1.5 collective-permute-start.6
  53.4 21.8 %copy-start.12 = (s32[2]{0:T(128)S(1)}, s32[2]{0:T(128)}, u32[]{:S(2)}) copy-start(s32[2]{0:T(128)} %pad_add_fusion.refs_0_.me_ref) | copy-start | bytes 28
  53.4 21.8 %copy-start.26 = (bf16[320,768]{1,0:T(8,128)(2,1)S(1)}, bf16[320,768]{1,0:T(8,128)(2,1)}, u32[]{:S(2)}) copy-start(bf16[320,768]{1,0:T(8,128)(2,1)} %get-tuple-element.230.refs_4_.refs_0_) | copy-start | bytes 1474564
  53.4 21.8 %copy-start.27 = (bf16[320,768]{1,0:T(8,128)(2,1)S(1)}, bf16[320,768]{1,0:T(8,128)(2,1)}, u32[]{:S(2)}) copy-start(bf16[320,768]{1,0:T(8,128)(2,1)} %get-tuple-element.231.refs_5_.refs_1_) | copy-start | bytes 1474564
  53.4 21.8 %copy-start.28 = (bf16[320,2048]{1,0:T(8,128)(2,1)S(1)}, bf16[320,2048]{1,0:T(8,128)(2,1)}, u32[]{:S(2)}) copy-start(bf16[320,2048]{1,0:T(8,128)(2,1)} %get-tuple-element.228.refs_2_) | copy-start | bytes 3932164
  53.4 21.8 %copy-start.29 = (bf16[320,2048]{1,0:T(8,128)(2,1)S(1)}, bf16[320,2048]{1,0:T(8,128)(2,1)}, u32[]{:S(2)}) copy-start(bf16[320,2048]{1,0:T(8,128)(2,1)} %get-tuple-element.229.refs_3_) | copy-start | bytes 3932164
  79.9 11.2 %copy-start.38 = (bf16[1,256,768]{2,1,0:T(8,128)(2,1)S(1)}, bf16[1,256,768]{2,1,0:T(8,128)(2,1)}, u32[]{:S(2)}) copy-start(bf16[1,256,768]{2,1,0:T(8,128)(2,1)} %param.19) | copy-start | bytes 1179652
  79.9 11.2 %copy-start.42 = (bf16[1,64,768]{2,1,0:T(8,128)(2,1)S(1)}, bf16[1,64,768]{2,1,0:T(8,128)(2,1)}, u32[]{:S(2)}) copy-start(bf16[1,64,768]{2,1,0:T(8,128)(2,1)} %param.17) | copy-start | bytes 294916
  79.9 11.4 %copy-start.45 = (f32[3,768]{1,0:T(4,128)S(1)}, f32[3,768]{1,0:T(4,128)}, u32[]{:S(2)}) copy-start(f32[3,768]{1,0:T(4,128)} %refs_6_.3) | copy-start | bytes 27652
  79.9 11.4 %copy-start.35 = (f32[320,768]{1,0:T(8,128)S(1)}, f32[320,768]{1,0:T(8,128)}, u32[]{:S(2)}) copy-start(f32[320,768]{1,0:T(8,128)} %get-tuple-element.259) | copy-start | bytes 2949124
  79.9 11.6 %copy-start.17 = (bf16[320,2048]{1,0:T(8,128)(2,1)S(1)}, bf16[320,2048]{1,0:T(8,128)(2,1)}, u32[]{:S(2)}) copy-start(bf16[320,2048]{1,0:T(8,128)(2,1)} %get-tuple-element.240.refs_3_) | copy-start | bytes 3932164
  90.7 8.1 %collective-permute-start.7 = (bf16[16,768,128]{2,1,0:T(8,128)(2,1)S(1)}, bf16[16,768,128]{2,1,0:T(8,128)(2,1)S(1)}, u32[]{:S(2)}, u32[]{:S(2)}) collective-permute-start(bf16[16,768,128]{2,1,0:T(8,128)(2,1)S(1)} %get-tuple-element.238), channel_id=1, source_target_pairs={{0,2},{2,0},{4,6},{6,4},{8,10},{10,8},{12,14},{14,12},{16,18},{18,... | collective-permute-start | bytes 9437192 | tf_op jit(solution)/shard_map/ppermute | solution.py:752
  98.8 2.3 %copy-start.36 = (bf16[768,2048]{1,0:T(8,128)(2,1)S(1)}, bf16[768,2048]{1,0:T(8,128)(2,1)}, u32[]{:S(2)}) copy-start(bf16[768,2048]{1,0:T(8,128)(2,1)} %refs_14_.3) | copy-start | bytes 9437188
  103.0 2.9 %copy-start.41 = (f32[320,768]{1,0:T(8,128)S(1)}, f32[320,768]{1,0:T(8,128)}, u32[]{:S(2)}) copy-start(f32[320,768]{1,0:T(8,128)} %get-tuple-element.256) | copy-start | bytes 2949124
  103.0 3.2 %copy-start.39 = (bf16[768,768]{1,0:T(8,128)(2,1)S(1)}, bf16[768,768]{1,0:T(8,128)(2,1)}, u32[]{:S(2)}) copy-start(bf16[768,768]{1,0:T(8,128)(2,1)} %refs_17_.1) | copy-start | bytes 3538948
  103.0 3.8 %copy-start.8 = (bf16[12,64,64]{2,1,0:T(8,128)(2,1)S(1)}, bf16[12,64,64]{2,1,0:T(8,128)(2,1)}, u32[]{:S(2)}) copy-start(bf16[12,64,64]{2,1,0:T(8,128)(2,1)} %get-tuple-element.265.refs_6_) | copy-start | bytes 294916
  104.5 20.3 %collective-permute-start.10 = (bf16[16,528,128]{2,1,0:T(8,128)(2,1)S(1)}, bf16[16,528,128]{2,1,0:T(8,128)(2,1)S(1)}, u32[]{:S(2)}, u32[]{:S(2)}) collective-permute-start(bf16[16,528,128]{2,1,0:T(8,128)(2,1)S(1)} %get-tuple-element.255), channel_id=1, source_target_pairs={{0,2},{2,0},{4,6},{6,4},{8,10},{10,8},{12,14},{14,12},{16,18},{18,... | collective-permute-start | bytes 6488072 | tf_op jit(solution)/shard_map/ppermute | solution.py:752
  104.8 19.7 %collective-permute-start.8 = (bf16[8,384,128]{2,1,0:T(8,128)(2,1)S(1)}, bf16[8,384,128]{2,1,0:T(8,128)(2,1)S(1)}, u32[]{:S(2)}, u32[]{:S(2)}) collective-permute-start(bf16[8,384,128]{2,1,0:T(8,128)(2,1)S(1)} %get-tuple-element.253), channel_id=1, source_target_pairs={{0,4},{2,6},{4,0},{6,2},{8,12},{10,14},{12,8},{14,10},{16,20},{18,... | collective-permute-start | bytes 2359304 | tf_op jit(solution)/shard_map/ppermute | solution.py:752
  105.3 19.4 %collective-permute-start.9 = (bf16[8,384,128]{2,1,0:T(8,128)(2,1)S(1)}, bf16[8,384,128]{2,1,0:T(8,128)(2,1)S(1)}, u32[]{:S(2)}, u32[]{:S(2)}) collective-permute-start(bf16[8,384,128]{2,1,0:T(8,128)(2,1)S(1)} %get-tuple-element.254), channel_id=1, source_target_pairs={{0,1},{1,0},{2,3},{3,2},{4,5},{5,4},{6,7},{7,6},{8,9},{9,8},{10,11... | collective-permute-start | bytes 2359304 | tf_op jit(solution)/shard_map/ppermute | solution.py:754
  105.8 1.9 copy-start
  105.8 2.0 copy-start.4
  105.8 2.1 %copy-start.5 = (bf16[320,768]{1,0:T(8,128)(2,1)S(1)}, bf16[320,768]{1,0:T(8,128)(2,1)}, u32[]{:S(2)}) copy-start(bf16[320,768]{1,0:T(8,128)(2,1)} %get-tuple-element.261.refs_1_) | copy-start | bytes 1474564
  105.9 2.3 %copy-start.6 = (bf16[320,768]{1,0:T(8,128)(2,1)S(1)}, bf16[320,768]{1,0:T(8,128)(2,1)}, u32[]{:S(2)}) copy-start(bf16[320,768]{1,0:T(8,128)(2,1)} %get-tuple-element.262.refs_2_) | copy-start | bytes 1474564
  106.1 2.6 %copy-start.1 = (bf16[12,256,256]{2,1,0:T(8,128)(2,1)S(1)}, bf16[12,256,256]{2,1,0:T(8,128)(2,1)}, u32[]{:S(2)}) copy-start(bf16[12,256,256]{2,1,0:T(8,128)(2,1)} %get-tuple-element.264.refs_5_) | copy-start | bytes 4718596
  106.2 2.6 %copy-start.3 = (bf16[320,768]{1,0:T(8,128)(2,1)S(1)}, bf16[320,768]{1,0:T(8,128)(2,1)}, u32[]{:S(2)}) copy-start(bf16[320,768]{1,0:T(8,128)(2,1)} %get-tuple-element.263.refs_3_.refs_2_) | copy-start | bytes 1474564
  108.8 5.0 %copy-start.34 = (bf16[768,768]{1,0:T(8,128)(2,1)S(1)}, bf16[768,768]{1,0:T(8,128)(2,1)}, u32[]{:S(2)}) copy-start(bf16[768,768]{1,0:T(8,128)(2,1)} %refs_25_.1) | copy-start | bytes 3538948
  119.5 14.8 %copy-start.7 = (bf16[320,768]{1,0:T(8,128)(2,1)S(1)}, bf16[320,768]{1,0:T(8,128)(2,1)}, u32[]{:S(2)}) copy-start(bf16[320,768]{1,0:T(8,128)(2,1)} %get-tuple-element.218.refs_19_.refs_3_) | copy-start | bytes 1474564
  119.6 14.8 %copy-start.19 = (bf16[320,768]{1,0:T(8,128)(2,1)S(1)}, bf16[320,768]{1,0:T(8,128)(2,1)}, u32[]{:S(2)}) copy-start(bf16[320,768]{1,0:T(8,128)(2,1)} %get-tuple-element.299.refs_1_) | copy-start | bytes 1474564
  119.6 14.8 %copy-start.20 = (bf16[320,768]{1,0:T(8,128)(2,1)S(1)}, bf16[320,768]{1,0:T(8,128)(2,1)}, u32[]{:S(2)}) copy-start(bf16[320,768]{1,0:T(8,128)(2,1)} %get-tuple-element.301.refs_5_) | copy-start | bytes 1474564
  119.6 14.8 %copy-start.21 = (bf16[320,768]{1,0:T(8,128)(2,1)S(1)}, bf16[320,768]{1,0:T(8,128)(2,1)}, u32[]{:S(2)}) copy-start(bf16[320,768]{1,0:T(8,128)(2,1)} %get-tuple-element.305.refs_9_) | copy-start | bytes 1474564
  119.6 14.8 %copy-start.22 = (bf16[320,768]{1,0:T(8,128)(2,1)S(1)}, bf16[320,768]{1,0:T(8,128)(2,1)}, u32[]{:S(2)}) copy-start(bf16[320,768]{1,0:T(8,128)(2,1)} %get-tuple-element.307.refs_11_) | copy-start | bytes 1474564
  119.6 14.8 %copy-start.30 = (bf16[320,768]{1,0:T(8,128)(2,1)S(1)}, bf16[320,768]{1,0:T(8,128)(2,1)}, u32[]{:S(2)}) copy-start(bf16[320,768]{1,0:T(8,128)(2,1)} %get-tuple-element.302.refs_6_) | copy-start | bytes 1474564
  119.6 14.8 %copy-start.31 = (bf16[320,768]{1,0:T(8,128)(2,1)S(1)}, bf16[320,768]{1,0:T(8,128)(2,1)}, u32[]{:S(2)}) copy-start(bf16[320,768]{1,0:T(8,128)(2,1)} %get-tuple-element.303.refs_7_) | copy-start | bytes 1474564
  125.8 6.5 %collective-permute-start.15 = (f32[16,768]{1,0:T(8,128)S(1)}, f32[16,768]{1,0:T(8,128)S(1)}, u32[]{:S(2)}, u32[]{:S(2)}) collective-permute-start(f32[16,768]{1,0:T(8,128)S(1)} %small_sums.1), channel_id=1, source_target_pairs={{0,16},{2,18},{4,20},{6,22},{8,24},{10,26},{12,28},{14,30},{16,0},... | collective-permute-start | bytes 147464 | tf_op jit(solution)/shard_map/ppermute | solution.py:752
  125.9 7.9 %collective-permute-start.16 = (f32[16,768]{1,0:T(8,128)S(1)}, f32[16,768]{1,0:T(8,128)S(1)}, u32[]{:S(2)}, u32[]{:S(2)}) collective-permute-start(f32[16,768]{1,0:T(8,128)S(1)} %small_sums.1), channel_id=1, source_target_pairs={{0,8},{2,10},{4,12},{6,14},{8,0},{10,2},{12,4},{14,6},{16,24},{18,... | collective-permute-start | bytes 147464 | tf_op jit(solution)/shard_map/ppermute | solution.py:752
  126.7 21.5 %collective-permute-start.14 = (bf16[8,272,128]{2,1,0:T(8,128)(2,1)S(1)}, bf16[8,272,128]{2,1,0:T(8,128)(2,1)S(1)}, u32[]{:S(2)}, u32[]{:S(2)}) collective-permute-start(bf16[8,272,128]{2,1,0:T(8,128)(2,1)S(1)} %get-tuple-element.296), channel_id=1, source_target_pairs={{0,1},{1,0},{2,3},{3,2},{4,5},{5,4},{6,7},{7,6},{8,9},{9,8},{10,11... | collective-permute-start | bytes 1671176 | tf_op jit(solution)/shard_map/ppermute | solution.py:754
  127.1 21.1 %collective-permute-start.13 = (bf16[8,256,128]{2,1,0:T(8,128)(2,1)S(1)}, bf16[8,256,128]{2,1,0:T(8,128)(2,1)S(1)}, u32[]{:S(2)}, u32[]{:S(2)}) collective-permute-start(bf16[8,256,128]{2,1,0:T(8,128)(2,1)S(1)} %get-tuple-element.295), channel_id=1, source_target_pairs={{0,4},{2,6},{4,0},{6,2},{8,12},{10,14},{12,8},{14,10},{16,20},{18,... | collective-permute-start | bytes 1572872 | tf_op jit(solution)/shard_map/ppermute | solution.py:752
  128.7 16.3 %collective-permute-start.17 = (f32[16,768]{1,0:T(8,128)S(1)}, f32[16,768]{1,0:T(8,128)S(1)}, u32[]{:S(2)}, u32[]{:S(2)}) collective-permute-start(f32[16,768]{1,0:T(8,128)S(1)} %small_sums.1), channel_id=1, source_target_pairs={{0,24},{2,26},{4,28},{6,30},{8,16},{10,18},{12,20},{14,22},{16,8},... | collective-permute-start | bytes 147464 | tf_op jit(solution)/shard_map/ppermute | solution.py:752
  132.3 15.9 %collective-permute-start.11 = (bf16[4,384,128]{2,1,0:T(8,128)(2,1)S(1)}, bf16[4,384,128]{2,1,0:T(8,128)(2,1)S(1)}, u32[]{:S(2)}, u32[]{:S(2)}) collective-permute-start(bf16[4,384,128]{2,1,0:T(8,128)(2,1)S(1)} %get-tuple-element.293), channel_id=1, source_target_pairs={{0,1},{1,0},{2,3},{3,2},{4,5},{5,4},{6,7},{7,6},{8,9},{9,8},{10,11... | collective-permute-start | bytes 1179656 | tf_op jit(solution)/shard_map/ppermute | solution.py:754
  133.8 14.4 %collective-permute-start.12 = (bf16[4,384,128]{2,1,0:T(8,128)(2,1)S(1)}, bf16[4,384,128]{2,1,0:T(8,128)(2,1)S(1)}, u32[]{:S(2)}, u32[]{:S(2)}) collective-permute-start(bf16[4,384,128]{2,1,0:T(8,128)(2,1)S(1)} %get-tuple-element.294), channel_id=1, source_target_pairs={{0,4},{2,6},{4,0},{6,2},{8,12},{10,14},{12,8},{14,10},{16,20},{18,... | collective-permute-start | bytes 1179656 | tf_op jit(solution)/shard_map/ppermute | solution.py:752
  148.7 11.6 %collective-permute-start.18 = (bf16[16,576,128]{2,1,0:T(8,128)(2,1)S(1)}, bf16[16,576,128]{2,1,0:T(8,128)(2,1)S(1)}, u32[]{:S(2)}, u32[]{:S(2)}) collective-permute-start(bf16[16,576,128]{2,1,0:T(8,128)(2,1)S(1)} %get-tuple-element.333), channel_id=1, source_target_pairs={{0,2},{2,0},{4,6},{6,4},{8,10},{10,8},{12,14},{14,12},{16,18},{18,... | collective-permute-start | bytes 7077896 | tf_op jit(solution)/shard_map/ppermute | solution.py:752
  148.8 11.5 %collective-permute-start.21 = (bf16[2,768,128]{2,1,0:T(8,128)(2,1)S(1)}, bf16[2,768,128]{2,1,0:T(8,128)(2,1)S(1)}, u32[]{:S(2)}, u32[]{:S(2)}) collective-permute-start(bf16[2,768,128]{2,1,0:T(8,128)(2,1)S(1)} %get-tuple-element.336), channel_id=1, source_target_pairs={{0,8},{2,10},{4,12},{6,14},{8,0},{10,2},{12,4},{14,6},{16,24},{18,... | collective-permute-start | bytes 1179656 | tf_op jit(solution)/shard_map/ppermute | solution.py:752
  150.5 9.5 %collective-permute-start.20 = (bf16[4,272,128]{2,1,0:T(8,128)(2,1)S(1)}, bf16[4,272,128]{2,1,0:T(8,128)(2,1)S(1)}, u32[]{:S(2)}, u32[]{:S(2)}) collective-permute-start(bf16[4,272,128]{2,1,0:T(8,128)(2,1)S(1)} %get-tuple-element.335), channel_id=1, source_target_pairs={{0,4},{2,6},{4,0},{6,2},{8,12},{10,14},{12,8},{14,10},{16,20},{18,... | collective-permute-start | bytes 835592 | tf_op jit(solution)/shard_map/ppermute | solution.py:752
  152.0 8.1 %collective-permute-start.19 = (bf16[4,256,128]{2,1,0:T(8,128)(2,1)S(1)}, bf16[4,256,128]{2,1,0:T(8,128)(2,1)S(1)}, u32[]{:S(2)}, u32[]{:S(2)}) collective-permute-start(bf16[4,256,128]{2,1,0:T(8,128)(2,1)S(1)} %get-tuple-element.334), channel_id=1, source_target_pairs={{0,1},{1,0},{2,3},{3,2},{4,5},{5,4},{6,7},{7,6},{8,9},{9,8},{10,11... | collective-permute-start | bytes 786440 | tf_op jit(solution)/shard_map/ppermute | solution.py:754
  153.0 1.2 collective-permute-start.22
  154.2 14.4 %copy-start.44 = (f32[8,768]{1,0:T(8,128)S(1)}, f32[8,768]{1,0:T(8,128)}, u32[]{:S(2)}) copy-start(f32[8,768]{1,0:T(8,128)} %get-tuple-element.211.refs_4_) | copy-start | bytes 73732
  161.3 16.0 %collective-permute-start.23 = (bf16[8,288,128]{2,1,0:T(8,128)(2,1)S(1)}, bf16[8,288,128]{2,1,0:T(8,128)(2,1)S(1)}, u32[]{:S(2)}, u32[]{:S(2)}) collective-permute-start(bf16[8,288,128]{2,1,0:T(8,128)(2,1)S(1)} %get-tuple-element.355), channel_id=1, source_target_pairs={{0,4},{2,6},{4,0},{6,2},{8,12},{10,14},{12,8},{14,10},{16,20},{18,... | collective-permute-start | bytes 1769480 | tf_op jit(solution)/shard_map/ppermute | solution.py:752
  162.8 14.5 %collective-permute-start.24 = (bf16[8,288,128]{2,1,0:T(8,128)(2,1)S(1)}, bf16[8,288,128]{2,1,0:T(8,128)(2,1)S(1)}, u32[]{:S(2)}, u32[]{:S(2)}) collective-permute-start(bf16[8,288,128]{2,1,0:T(8,128)(2,1)S(1)} %get-tuple-element.356), channel_id=1, source_target_pairs={{0,1},{1,0},{2,3},{3,2},{4,5},{5,4},{6,7},{7,6},{8,9},{9,8},{10,11... | collective-permute-start | bytes 1769480 | tf_op jit(solution)/shard_map/ppermute | solution.py:754
  163.8 13.4 %collective-permute-start.25 = (bf16[2,528,128]{2,1,0:T(8,128)(2,1)S(1)}, bf16[2,528,128]{2,1,0:T(8,128)(2,1)S(1)}, u32[]{:S(2)}, u32[]{:S(2)}) collective-permute-start(bf16[2,528,128]{2,1,0:T(8,128)(2,1)S(1)} %get-tuple-element.357), channel_id=1, source_target_pairs={{0,8},{2,10},{4,12},{6,14},{8,0},{10,2},{12,4},{14,6},{16,24},{18,... | collective-permute-start | bytes 811016 | tf_op jit(solution)/shard_map/ppermute | solution.py:752
  165.5 11.8 %collective-permute-start.26 = (bf16[1,768,128]{2,1,0:T(8,128)(2,1)S(1)}, bf16[1,768,128]{2,1,0:T(8,128)(2,1)S(1)}, u32[]{:S(2)}, u32[]{:S(2)}) collective-permute-start(bf16[1,768,128]{2,1,0:T(8,128)(2,1)S(1)} %get-tuple-element.358), channel_id=1, source_target_pairs={{0,16},{2,18},{4,20},{6,22},{8,24},{10,26},{12,28},{14,30},{16,0},... | collective-permute-start | bytes 589832 | tf_op jit(solution)/shard_map/ppermute | solution.py:752
  168.0 9.2 %collective-permute-start.27 = (f32[16,768]{1,0:T(8,128)S(1)}, f32[16,768]{1,0:T(8,128)S(1)}, u32[]{:S(2)}, u32[]{:S(2)}) collective-permute-start(f32[16,768]{1,0:T(8,128)S(1)} %add.73), channel_id=1, source_target_pairs={{0,4},{2,6},{4,0},{6,2},{8,12},{10,14},{12,8},{14,10},{16,20},{18,... | collective-permute-start | bytes 147464 | tf_op jit(solution)/shard_map/ppermute | solution.py:752
  178.4 11.7 %collective-permute-start.28 = (bf16[4,288,128]{2,1,0:T(8,128)(2,1)S(1)}, bf16[4,288,128]{2,1,0:T(8,128)(2,1)S(1)}, u32[]{:S(2)}, u32[]{:S(2)}) collective-permute-start(bf16[4,288,128]{2,1,0:T(8,128)(2,1)S(1)} %get-tuple-element.374), channel_id=1, source_target_pairs={{0,1},{1,0},{2,3},{3,2},{4,5},{5,4},{6,7},{7,6},{8,9},{9,8},{10,11... | collective-permute-start | bytes 884744 | tf_op jit(solution)/shard_map/ppermute | solution.py:754
  179.5 10.7 %collective-permute-start.29 = (bf16[4,288,128]{2,1,0:T(8,128)(2,1)S(1)}, bf16[4,288,128]{2,1,0:T(8,128)(2,1)S(1)}, u32[]{:S(2)}, u32[]{:S(2)}) collective-permute-start(bf16[4,288,128]{2,1,0:T(8,128)(2,1)S(1)} %get-tuple-element.375), channel_id=1, source_target_pairs={{0,4},{2,6},{4,0},{6,2},{8,12},{10,14},{12,8},{14,10},{16,20},{18,... | collective-permute-start | bytes 884744 | tf_op jit(solution)/shard_map/ppermute | solution.py:752
  181.8 5.3 %collective-permute-start.31 = (f32[16,768]{1,0:T(8,128)S(1)}, f32[16,768]{1,0:T(8,128)S(1)}, u32[]{:S(2)}, u32[]{:S(2)}) collective-permute-start(f32[16,768]{1,0:T(8,128)S(1)} %add.74), channel_id=1, source_target_pairs={{0,1},{1,0},{2,3},{3,2},{4,5},{5,4},{6,7},{7,6},{8,9},{9,8},{10,11... | collective-permute-start | bytes 147464 | tf_op jit(solution)/shard_map/ppermute | solution.py:754
  182.8 7.4 %collective-permute-start.30 = (bf16[1,528,128]{2,1,0:T(8,128)(2,1)S(1)}, bf16[1,528,128]{2,1,0:T(8,128)(2,1)S(1)}, u32[]{:S(2)}, u32[]{:S(2)}) collective-permute-start(bf16[1,528,128]{2,1,0:T(8,128)(2,1)S(1)} %get-tuple-element.376), channel_id=1, source_target_pairs={{0,16},{2,18},{4,20},{6,22},{8,24},{10,26},{12,28},{14,30},{16,0},... | collective-permute-start | bytes 405512 | tf_op jit(solution)/shard_map/ppermute | solution.py:752
  192.0 11.3 %collective-permute-start.32 = (bf16[1,576,128]{2,1,0:T(8,128)(2,1)S(1)}, bf16[1,576,128]{2,1,0:T(8,128)(2,1)S(1)}, u32[]{:S(2)}, u32[]{:S(2)}) collective-permute-start(bf16[1,576,128]{2,1,0:T(8,128)(2,1)S(1)} %get-tuple-element.391), channel_id=1, source_target_pairs={{0,16},{2,18},{4,20},{6,22},{8,24},{10,26},{12,28},{14,30},{16,0},... | collective-permute-start | bytes 442376 | tf_op jit(solution)/shard_map/ppermute | solution.py:752
  193.1 10.2 %collective-permute-start.33 = (bf16[1,576,128]{2,1,0:T(8,128)(2,1)S(1)}, bf16[1,576,128]{2,1,0:T(8,128)(2,1)S(1)}, u32[]{:S(2)}, u32[]{:S(2)}) collective-permute-start(bf16[1,576,128]{2,1,0:T(8,128)(2,1)S(1)} %get-tuple-element.392), channel_id=1, source_target_pairs={{0,8},{2,10},{4,12},{6,14},{8,0},{10,2},{12,4},{14,6},{16,24},{18,... | collective-permute-start | bytes 442376 | tf_op jit(solution)/shard_map/ppermute | solution.py:752
  196.0 7.4 %collective-permute-start.34 = (bf16[1,576,128]{2,1,0:T(8,128)(2,1)S(1)}, bf16[1,576,128]{2,1,0:T(8,128)(2,1)S(1)}, u32[]{:S(2)}, u32[]{:S(2)}) collective-permute-start(bf16[1,576,128]{2,1,0:T(8,128)(2,1)S(1)} %get-tuple-element.393), channel_id=1, source_target_pairs={{0,24},{2,26},{4,28},{6,30},{8,16},{10,18},{12,20},{14,22},{16,8},... | collective-permute-start | bytes 442376 | tf_op jit(solution)/shard_map/ppermute | solution.py:752
  (19 other events, 21.5 us)
where the time goes:
time: 206 us; the launch traced here: 205 us
  Pallas kernels  93.3 us (45%)
  waiting for transfers between devices  43.4 us (21%)
  starting transfers between devices  41.3 us (20%)
  local copies, waits for them, and re-layouts  16.7 us (8%)
  matrix products  5.19 us (3%)
  between operations  3.7 us (2%)
    ppermute x26, starting transfers between devices, swap(): return lax.ppermute(a, 'wide', [(i, i ^ dw) for i in range(wide)])  32.8 us
    pallas_call x1, Pallas kernels, forward(): pl.pallas_call(functools.partial(forward_kernel, qlen, plen, 4), out_shap...  30.4 us
    ppermute x26, waiting for transfers between devices, swap(): return lax.ppermute(a, 'wide', [(i, i ^ dw) for i in range(wide)])  29.1 us
    pallas_call x3, Pallas kernels, wgrad(): pl.pallas_call(functools.partial(wgrad_kernel, full, groups, len(ops)), o...  28.1 us
    pallas_call x1, Pallas kernels, loss_and_back(): pl.pallas_call(functools.partial(back_kernel, narrow, stages, qlen, 4, le...  21.7 us
    unnamed x96, local copies, waits for them, and re-layouts  12.1 us
    ppermute x8, waiting for transfers between devices, swap(): return lax.ppermute(a, 'narrow', [(i, i ^ dn) for i in range(narrow)])  11.8 us
    ppermute x8, starting transfers between devices, swap(): return lax.ppermute(a, 'narrow', [(i, i ^ dn) for i in range(narrow)])  8.04 us
  transfers between devices with their start and end apart: 35, of which 17 were waited for; matrix products, arithmetic and copies ran while one was open for 4% of the time, Pallas kernels for 12%

commit v1 on v0

--- a/solution.py
+++ b/solution.py
@@ -39,15 +39,6 @@
     return lax.dot_general(
         a, b, (((1,), (1,)), ((), ())), preferred_element_type=F32, precision=precision
     )
-
-
-def rms_norm(x, gain_vec):
-    return x * lax.rsqrt(jnp.mean(x * x, axis=-1, keepdims=True) + EPSILON) * gain_vec
-
-
-def norm_back(x, gain_vec, grad_in):
-    outcome, pullback = jax.vjp(rms_norm, x, gain_vec)
-    return pullback(grad_in)
 
 
 def whole():
@@ -105,7 +96,7 @@
             o_ref[rows, lanes] = low(total)
         return carry
 
-    lax.fori_loop(0, pairs, pair, 0)
+    lax.fori_loop(0, pairs, pair, 0, unroll=2)
 
 
 def attend_back_kernel(
@@ -148,32 +139,7 @@
             gv_ref[rows, lanes] = low(gv)
         return carry
 
-    lax.fori_loop(0, pairs, pair, 0)
-
-
-def attend_back(q, k, v, o, go, pp, pq, acc):
-    heads, plen, _ = pp.shape
-    qlen = pq.shape[1]
-    operands = [q, k, v, o, go, pp, pq] + ([] if acc is None else [acc])
-
-    def body(*refs):
-        ins = list(refs[: len(operands)])
-        if acc is None:
-            ins.append(None)
-        attend_back_kernel(qlen, *ins, *refs[len(operands) :])
-
-    return pl.pallas_call(
-        body,
-        out_shape=(jax.ShapeDtypeStruct(q.shape, BF),) * 3
-        + (jax.ShapeDtypeStruct((heads, plen, plen), F32),),
-        in_specs=[whole()] * len(operands),
-        out_specs=(whole(),) * 4,
-        name="attend_back",
-        compiler_params=pltpu.CompilerParams(vmem_limit_bytes=14 << 20),
-        cost_estimate=pl.CostEstimate(
-            flops=8 * heads * HDIM * plen * plen, bytes_accessed=12 * heads * plen * plen, transcendentals=0
-        ),
-    )(*operands)
+    lax.fori_loop(0, pairs, pair, 0, unroll=2)
 
 
 def small_kernel(
@@ -206,20 +172,6 @@
         == jnp.broadcast_to(wide_s[...], (buckets, width))
     ).astype(F32)
     out_ref[4 : 4 + heads, :buckets] = dot_nt(diag_ref[...], onehot, HIGHEST)
-
-
-def small_sums(ds, lookup, buckets, gain_in, gain_mid, gain_final, loss):
-    heads, plen, _ = ds.shape
-    width = 2 * plen
-    return pl.pallas_call(
-        functools.partial(small_kernel, buckets),
-        out_shape=jax.ShapeDtypeStruct((4 + heads, gain_in.shape[1]), F32),
-        in_specs=[whole()] * 6,
-        out_specs=whole(),
-        scratch_shapes=[pltpu.VMEM((heads, width), F32), pltpu.VMEM((1, width), jnp.int32)],
-        name="small_sums",
-        compiler_params=pltpu.CompilerParams(vmem_limit_bytes=8 << 20),
-    )(ds, lookup[None], gain_in, gain_mid, gain_final, loss)
 
 
 def segment_table(seg_ref, first):
@@ -405,7 +357,7 @@
 
 
 def loss_kernel(
-    narrow, stages, me_ref, sharp_ref, here_ref, there_ref, vec_ref, e_ref, x_ref, gain_ref,
+    narrow, stages, me_ref, sharp_ref, here_ref, there_ref, e_ref, x_ref, gain_ref,
     qseg_ref, pseg_ref, wp_ref, gx_ref, ggain_ref, loss_ref, ge_ref, flat_s,
 ):
     half = here_ref.shape[0]
@@ -450,8 +402,9 @@
             loss_ref[...] = jnp.broadcast_to(jnp.sum(part, axis=0, keepdims=True), loss_ref.shape)
             grad = product(g[:16], flat_s[...])[:PACK]
         grad = grad + back
-    e, vec = e_ref[...], vec_ref[...]
+    e = e_ref[...]
     scale = lax.rsqrt(jnp.sum(e * e, axis=-1, keepdims=True) + EPSILON)
+    vec = e * scale
     ge = low((grad - vec * jnp.sum(vec * grad, axis=-1, keepdims=True)) * scale)
     ge_ref[...] = ge
     qt, pt = segment_table(qseg_ref, 0), segment_table(pseg_ref, QSEGS)
@@ -474,6 +427,7 @@
     ggain_ref[...] = total
 
 
+PAIRED = ("grad_f", "ga", "grad_f1", "ga1")
 BACK = ("grad_f", "ga", "gb", "gy", "gq", "gk", "gv", "ds", "grad_f1", "ga1", "gb1", "grad_x")
 
 
@@ -485,46 +439,62 @@
     return back, jnp.sum(grad * unit, axis=0, keepdims=True)
 
 
-def back_kernel(narrow, stages, qlen, n_tiles, n_held, *refs):
-    me_ref, sharp_ref, here_ref, there_ref, vec_ref, e_ref, gains_ref, qseg_ref, pseg_ref = refs[:9]
-    refs = refs[9:]
-    hbm, refs = refs[:n_held], refs[n_held:]
+def back_kernel(narrow, stages, qlen, n_tiles, n_held, names, jobs, *refs):
+    me_ref, sharp_ref, here_ref, there_ref, e_ref, gains_ref, qseg_ref, pseg_ref = refs[:8]
+    refs = refs[8:]
+    n_fetch = n_held + (4 if jobs else 0)
+    hbm, refs = refs[:n_fetch], refs[n_fetch:]
     ggain_ref, loss_ref, ge_ref, gmid_ref, gin_ref = refs[:5]
-    outs, refs = dict(zip(BACK, refs[5 : 5 + len(BACK)])), refs[5 + len(BACK) :]
-    held, refs = refs[:n_held], refs[n_held:]
-    keep, refs = dict(zip(BACK, refs[: len(BACK)])), refs[len(BACK) :]
-    flat_s, gx_s, go_s, in_sem, out_sem = refs
+    outs, refs = dict(zip(names, refs[5 : 5 + len(names)])), refs[5 + len(names) :]
+    if jobs:
+        (keep_ref, send_ref), refs = refs[:2], refs[2:]
+    held, refs = list(refs[: n_held - 4]), refs[n_held - 4 :]
+    singles = [n for n in BACK if n not in PAIRED and n != "grad_x"]
+    keep, refs = dict(zip(singles, refs[: len(singles)])), refs[len(singles) :]
+    gf_s, ga_s, wide_s, row_s, flat_s, gx_s, go_s, in_sem, out_sem = refs[:9]
+    total = gx_s.shape[0]
+    keep["grad_x"] = gx_s
+    halves = [buf.at[i * total : (i + 1) * total] for buf in (wide_s, row_s) for i in range(2)]
+    held = held[:3] + halves[:2] + held[3:7] + halves[2:] + held[7:] + halves
+    for i, (name, buf) in enumerate((("grad_f1", gf_s), ("ga1", ga_s), ("grad_f", gf_s), ("ga", ga_s))):
+        keep[name] = buf.at[i // 2 * total : (i // 2 + 1) * total]
     fetch = [pltpu.make_async_copy(a, b, in_sem.at[i]) for i, (a, b) in enumerate(zip(hbm, held))]
-    for c in fetch:
+    for c in fetch[:21]:
         c.start()
     (x2_s, wp_s, wd_s, da_s, db_s, wg_s, wu_s, xm_s, wo_s, v_s, o_s, pp_s, k_s, q_s, pq_s) = held[:15]
-    wq_s, wk_s, wv_s, x_s, da1_s, db1_s = held[15:]
-
-    def send(*names):
-        for name in names:
-            pltpu.make_async_copy(keep[name], outs[name], out_sem.at[BACK.index(name)]).start()
+    wq_s, wk_s, wv_s, x_s, da1_s, db1_s = held[15:21]
+
+    def write(name):
+        return pltpu.make_async_copy(keep[name], outs[name], out_sem.at[names.index(name)])
+
+    def send(*ready):
+        for name in ready:
+            if name in outs:
+                write(name).start()
 
     fetch[0].wait()
     fetch[1].wait()
     loss_kernel(
-        narrow, stages, me_ref, sharp_ref, here_ref, there_ref, vec_ref, e_ref, x2_s, gains_ref.at[2:3],
+        narrow, stages, me_ref, sharp_ref, here_ref, there_ref, e_ref, x2_s, gains_ref.at[2:3],
         qseg_ref, pseg_ref, wp_s, gx_s, ggain_ref, loss_ref, ge_ref, flat_s,
     )
 
-    def gated_back(x_ref, da, db, names):
+    def gated_back(x_ref, da, db, made):
         grad_f = low(x_ref[...])
-        keep[names[0]][...] = grad_f
+        keep[made[0]][...] = grad_f
         size = da.shape[1] // n_tiles
         for t in range(n_tiles):
             lanes = slice(t * size, (t + 1) * size)
             gu = dot_nt(grad_f, wd_s[lanes, :])
-            keep[names[1]][:, lanes] = low(gu * da[:, lanes].astype(F32))
-            keep[names[2]][:, lanes] = low(gu * db[:, lanes].astype(F32))
-        send(*names)
+            keep[made[1]][:, lanes] = low(gu * da[:, lanes].astype(F32))
+            keep[made[2]][:, lanes] = low(gu * db[:, lanes].astype(F32))
+        send(*made)
 
     for i in (2, 3, 4):
         fetch[i].wait()
     gated_back(gx_s, da_s, db_s, BACK[:3])
+    for c in fetch[21:23]:
+        c.start()
     for i in (5, 6, 7):
         fetch[i].wait()
     grad = dot_nt(keep["ga"][...], wg_s[...]) + dot_nt(keep["gb"][...], wu_s[...])
@@ -542,21 +512,27 @@
         qlen, q_s, k_s, v_s, o_s, go_s, pp_s, pq_s, None, keep["gq"], keep["gk"], keep["gv"], keep["ds"]
     )
     send("gq", "gk", "gv", "ds")
+    for c in fetch[23:]:
+        c.start()
     for i in range(15, 19):
         fetch[i].wait()
     grad = dot_nt(keep["gq"][...], wq_s[...]) + dot_nt(keep["gk"][...], wk_s[...])
     grad = grad + dot_nt(keep["gv"][...], wv_s[...])
     back, gin_ref[...] = through_norm(x_s[...], gains_ref[0:1, :], grad)
-    keep["grad_x"][...] = gx_s[...] + back
+    gx_s[...] = gx_s[...] + back
     send("grad_x")
     fetch[19].wait()
     fetch[20].wait()
-    gated_back(keep["grad_x"], da1_s, db1_s, BACK[8:11])
-    for name in BACK:
-        pltpu.make_async_copy(keep[name], outs[name], out_sem.at[BACK.index(name)]).wait()
-
-
-def loss_and_back(me, narrow, stages, sharp, here, there, vec, e, gains, qseg, pseg, x_last, x_in, first, second, matrices):
+    gated_back(gx_s, da1_s, db1_s, BACK[8:11])
+    if jobs:
+        for i in range(21, 25):
+            fetch[i].wait()
+        weight_products(jobs, (gf_s, wide_s, row_s, ga_s), lambda g: None, me_ref, keep_ref, send_ref, refs[9])
+    for name in names:
+        write(name).wait()
+
+
+def loss_and_back(me, narrow, stages, sharp, here, there, e, gains, qseg, pseg, x_last, x_in, first, second, matrices, wide, jobs, total_rows):
     wq, wk, wv, wo, wg, wu, wd, wp = matrices
     total, feat = x_last.shape
     qlen, plen = qseg.shape[1], pseg.shape[1]
@@ -567,31 +543,140 @@
     fetched += [wq, wk, wv, x_in, first["da"], first["db"]]
     tok, ff = ((total, feat), BF), ((total, hidden), BF)
     kinds = [tok, ff, ff, tok, tok, tok, tok, ((heads, plen, plen), F32), tok, ff, ff, ((total, feat), F32)]
+    kinds = dict(zip(BACK, kinds))
+    names = [n for n in BACK if not (jobs and n in ("grad_f", "ga", "grad_f1"))]
+    held = [pltpu.VMEM(a.shape, a.dtype) for i, a in enumerate(fetched) if i not in (3, 4, 9, 10)]
+    n_held = len(fetched)
+    blocks, late = [], []
+    if jobs:
+        fetched += [first["u"], second["u"], first["normed"], second["normed"]]
+        blocks = [((wide * narrow // 2, total_rows, 128), BF)] * 2
+        late = [pltpu.VMEM((384, 2 * total), BF)]
+        widths = (feat, hidden, feat, hidden)
+        jobs = with_blocks(jobs, lambda g: widths[g], wide, narrow)
     small = [((1, feat), F32), ((1, 128), F32), ((PACK, feat), BF), ((1, feat), F32), ((1, feat), F32)]
     anywhere = pl.BlockSpec(memory_space=pltpu.HBM)
     smem = pl.BlockSpec(memory_space=pltpu.SMEM)
     weights = sum(m.size for m in matrices)
     outs = pl.pallas_call(
-        functools.partial(back_kernel, narrow, stages, qlen, 4, len(fetched)),
-        out_shape=tuple(jax.ShapeDtypeStruct(*s) for s in small + kinds),
-        in_specs=[smem, smem] + [whole()] * 7 + [anywhere] * len(fetched),
-        out_specs=(whole(),) * 5 + (anywhere,) * len(kinds),
-        scratch_shapes=[pltpu.VMEM(a.shape, a.dtype) for a in fetched]
-        + [pltpu.VMEM(*k) for k in kinds]
+        functools.partial(back_kernel, narrow, stages, qlen, 4, n_held, names, jobs),
+        out_shape=tuple(jax.ShapeDtypeStruct(*s) for s in small + [kinds[n] for n in names] + blocks),
+        in_specs=[smem, smem] + [whole()] * 6 + [anywhere] * len(fetched),
+        out_specs=(whole(),) * 5 + (anywhere,) * len(names) + (whole(),) * len(blocks),
+        scratch_shapes=held
+        + [pltpu.VMEM(*kinds[n]) for n in BACK if n not in PAIRED and n != "grad_x"]
         + [
+            pltpu.VMEM((2 * total, feat), BF),
+            pltpu.VMEM((2 * total, hidden), BF),
+            pltpu.VMEM((2 * total, hidden), BF),
+            pltpu.VMEM((2 * total, feat), BF),
             pltpu.VMEM((size, feat), BF),
             pltpu.VMEM((total, feat), F32),
             pltpu.VMEM((total, feat), BF),
             pltpu.SemaphoreType.DMA((len(fetched),)),
-            pltpu.SemaphoreType.DMA((len(kinds),)),
-        ],
+            pltpu.SemaphoreType.DMA((len(names),)),
+        ]
+        + late,
         name="loss_and_back",
-        compiler_params=pltpu.CompilerParams(vmem_limit_bytes=56 << 20),
+        compiler_params=pltpu.CompilerParams(vmem_limit_bytes=(54 if jobs else 56) << 20),
         cost_estimate=pl.CostEstimate(
             flops=3 * total * weights, bytes_accessed=2 * weights, transcendentals=0
         ),
-    )(me, sharp, here, there, vec, e, gains, qseg, pseg, *fetched)
-    return outs[:5], dict(zip(BACK, outs[5:]))
+    )(me, sharp, here, there, e, gains, qseg, pseg, *fetched)
+    return outs[:5], dict(zip(names, outs[5:])), outs[5 + len(names) :]
+
+
+REST = ("gy", "gq", "gk", "gv", "grad_x")
+
+
+def rest_kernel(qlen, buckets, n_held, *refs):
+    gains_ref, lookup_ref, gin_ref, gmid_ref, gfin_ref, loss_ref = refs[:6]
+    refs = refs[6:]
+    hbm, refs = refs[:n_held], refs[n_held:]
+    sums_ref, outs, refs = refs[0], dict(zip(REST, refs[1:6])), refs[6:]
+    held, refs = refs[:n_held], refs[n_held:]
+    keep, refs = dict(zip(REST, refs[:5])), refs[5:]
+    go_s, row_s, diag_s, wide_s, in_sem, out_sem = refs
+    (ga_s, wg_s, gb_s, wu_s, xm_s, gx_s, wo_s, q_s, k_s, v_s, o_s, pp_s, pq_s, ds_s) = held[:14]
+    wq_s, wk_s, wv_s, qx_s, px_s = held[14:]
+    fetch = [pltpu.make_async_copy(a, b, in_sem.at[i]) for i, (a, b) in enumerate(zip(hbm, held))]
+    for c in fetch:
+        c.start()
+
+    def arrive(first, last):
+        for i in range(first, last):
+            fetch[i].wait()
+
+    def write(name):
+        return pltpu.make_async_copy(keep[name], outs[name], out_sem.at[REST.index(name)])
+
+    arrive(0, 2)
+    grad = dot_nt(ga_s[...], wg_s[...])
+    arrive(2, 6)
+    grad = grad + dot_nt(gb_s[...], wu_s[...])
+    back, part = through_norm(xm_s[...], gains_ref[1:2, :], grad)
+    row_s[1:2, :] = gmid_ref[...] + part
+    grad_mid = gx_s[...] + back
+    gx_s[...] = grad_mid
+    gy = low(grad_mid)
+    keep["gy"][...] = gy
+    write("gy").start()
+    arrive(6, 7)
+    go_s[...] = low(dot_nt(gy, wo_s[...]))
+    arrive(7, 14)
+    attend_back_kernel(
+        qlen, q_s, k_s, v_s, o_s, go_s, pp_s, pq_s, ds_s, keep["gq"], keep["gk"], keep["gv"], ds_s
+    )
+    for name in REST[1:4]:
+        write(name).start()
+    arrive(14, 19)
+    grad = dot_nt(keep["gq"][...], wq_s[...]) + dot_nt(keep["gk"][...], wk_s[...])
+    grad = grad + dot_nt(keep["gv"][...], wv_s[...])
+    x = jnp.concatenate([qx_s[...], px_s[...]], axis=0).astype(F32)
+    back, part = through_norm(x, gains_ref[0:1, :], grad)
+    row_s[0:1, :] = gin_ref[...] + part
+    keep["grad_x"][...] = gx_s[...] + back
+    write("grad_x").start()
+    small_kernel(
+        buckets, ds_s, lookup_ref, row_s.at[0:1], row_s.at[1:2], gfin_ref, loss_ref, sums_ref, diag_s, wide_s
+    )
+    for name in REST:
+        write(name).wait()
+
+
+def rest_back(gains, lookup, buckets, small, ga, gb, gx, acc, first, matrices, qx, px):
+    wq, wk, wv, wo, wg, wu = matrices[:6]
+    total, feat = gx.shape
+    heads, plen, _ = acc.shape
+    qlen = qx.shape[0]
+    t = first
+    fetched = [ga, wg, gb, wu, t["x_mid"], gx, wo, t["q"], t["k"], t["v"], t["o"], t["pp"], t["pq"], acc]
+    fetched += [wq, wk, wv, qx, px]
+    kinds = [((total, feat), BF)] * 4 + [((total, feat), F32)]
+    anywhere = pl.BlockSpec(memory_space=pltpu.HBM)
+    weights = sum(m.size for m in matrices[:6])
+    outs = pl.pallas_call(
+        functools.partial(rest_kernel, qlen, buckets, len(fetched)),
+        out_shape=tuple(jax.ShapeDtypeStruct(*k) for k in [((4 + heads, feat), F32)] + kinds),
+        in_specs=[whole()] * 6 + [anywhere] * len(fetched),
+        out_specs=(whole(),) + (anywhere,) * len(kinds),
+        scratch_shapes=[pltpu.VMEM(a.shape, a.dtype) for a in fetched]
+        + [pltpu.VMEM(*k) for k in kinds]
+        + [
+            pltpu.VMEM((total, feat), BF),
+            pltpu.VMEM((8, feat), F32),
+            pltpu.VMEM((heads, 2 * plen), F32),
+            pltpu.VMEM((1, 2 * plen), jnp.int32),
+            pltpu.SemaphoreType.DMA((len(fetched),)),
+            pltpu.SemaphoreType.DMA((len(kinds),)),
+        ],
+        name="rest_back",
+        compiler_params=pltpu.CompilerParams(vmem_limit_bytes=50 << 20),
+        cost_estimate=pl.CostEstimate(
+            flops=3 * total * weights, bytes_accessed=2 * weights, transcendentals=0
+        ),
+    )(gains, lookup[None], *small, *fetched)
+    return outs
 
 
 def join_kernel(*refs):
@@ -638,12 +723,71 @@
     return place
 
 
+def weight_products(jobs, held, arrive, me_ref, keep_ref, send_ref, turned_s):
+    me_w, me_n = me_ref[0], me_ref[1]
+    half = keep_ref.shape[0]
+
+    def store(acc, job, w_first, n_first):
+        row_axis, block_rows, block_lanes, targets = job[2:]
+        blocks = [
+            (bi, bj)
+            for bi in range(acc.shape[0] // block_rows)
+            for bj in range(acc.shape[1] // block_lanes)
+        ]
+        bases = [traced_place(t[0], w_first ^ me_w, n_first ^ me_n) for t in targets]
+        for core in range(2):
+
+            @pl.when((me_w & 1) == core)
+            def _():
+                for bi, bj in blocks:
+                    w, n = (bi, bj) if row_axis == "wide" else (bj, bi)
+                    out_ref = keep_ref if (w & 1) == core else send_ref
+                    for (order, first, count, offset), base in zip(targets, bases):
+                        at = (base ^ place_of(order, w, n)) & (half - 1)
+                        for k in range(block_lanes // 128):
+                            lane = bj * block_lanes + k * 128
+                            row = bi * block_rows + first
+                            out_ref[at, offset + k * count : offset + (k + 1) * count, :] = acc[
+                                row : row + count, lane : lane + 128
+                            ]
+
+    for job in jobs:
+        rg, lg, row_axis, block_rows, block_lanes, targets = job
+        arrive(rg)
+        arrive(lg)
+        row_s, lane_s = held[rg], held[lg]
+        depth, rows, lanes = row_s.shape[0], row_s.shape[1], lane_s.shape[1]
+        tile_rows = 384
+        tile_lanes = block_lanes
+        while tile_lanes < 512 and lanes % (2 * tile_lanes) == 0:
+            tile_lanes *= 2
+        per_row, per_lane = tile_rows // block_rows, tile_lanes // block_lanes
+
+        def row_step(rt, carry):
+            mine = row_s[:, pl.ds(pl.multiple_of(rt * tile_rows, 128), tile_rows)]
+            if depth > 16:
+                turned_s[...] = mine.T
+
+            def lane_step(lt, inner):
+                part = lane_s[:, pl.ds(pl.multiple_of(lt * tile_lanes, 128), tile_lanes)]
+                acc = product(turned_s[...], part) if depth > 16 else dot_tn(mine, part)
+                if row_axis == "wide":
+                    store(low(acc), job, rt * per_row, lt * per_lane)
+                else:
+                    store(low(acc), job, lt * per_lane, rt * per_row)
+                return inner
+
+            if lanes == tile_lanes:
+                return lane_step(0, carry)
+            return lax.fori_loop(0, lanes // tile_lanes, lane_step, carry)
+
+        lax.fori_loop(0, rows // tile_rows, row_step, 0)
+
+
 def wgrad_kernel(jobs, groups, n_ops, me_ref, *refs):
     ops, (keep_ref, send_ref) = refs[:n_ops], refs[n_ops : n_ops + 2]
     held = refs[n_ops + 2 : n_ops + 2 + len(groups)]
     turned_s, sems = refs[-2:]
-    me_w, me_n = me_ref[0], me_ref[1]
-    half = keep_ref.shape[0]
     copies = []
     for ids, buf in zip(groups, held):
         first, own = 0, []
@@ -664,71 +808,22 @@
                 c.wait()
             ready.add(g)
 
-    def store(acc, job, w_first, n_first):
-        row_axis, block_rows, block_lanes, targets = job[2:]
-        blocks = [
-            (bi, bj)
-            for bi in range(acc.shape[0] // block_rows)
-            for bj in range(acc.shape[1] // block_lanes)
-        ]
-        bases = [traced_place(t[0], w_first ^ me_w, n_first ^ me_n) for t in targets]
-        for core in range(2):
-
-            @pl.when((me_w & 1) == core)
-            def _():
-                for bi, bj in blocks:
-                    w, n = (bi, bj) if row_axis == "wide" else (bj, bi)
-                    out_ref = keep_ref if (w & 1) == core else send_ref
-                    for (order, first, count, offset), base in zip(targets, bases):
-                        at = (base ^ place_of(order, w, n)) & (half - 1)
-                        for k in range(block_lanes // 128):
-                            lane = bj * block_lanes + k * 128
-                            row = bi * block_rows + first
-                            out_ref[at, offset + k * count : offset + (k + 1) * count, :] = acc[
-                                row : row + count, lane : lane + 128
-                            ]
-
-    for job in jobs:
-        rg, lg, row_axis, block_rows, block_lanes, targets = job
-        arrive(rg)
-        arrive(lg)
-        row_s, lane_s = held[rg], held[lg]
-        depth, rows, lanes = row_s.shape[0], row_s.shape[1], lane_s.shape[1]
-        tile_rows = 384
-        tile_lanes = block_lanes
-        while tile_lanes < 512 and lanes % (2 * tile_lanes) == 0:
-            tile_lanes *= 2
-        per_row, per_lane = tile_rows // block_rows, tile_lanes // block_lanes
-
-        def row_step(rt, carry):
-            mine = row_s[:, pl.ds(pl.multiple_of(rt * tile_rows, 128), tile_rows)]
-            if depth > 16:
-                turned_s[...] = mine.T
-
-            def lane_step(lt, inner):
-                part = lane_s[:, pl.ds(pl.multiple_of(lt * tile_lanes, 128), tile_lanes)]
-                acc = product(turned_s[...], part) if depth > 16 else dot_tn(mine, part)
-                if row_axis == "wide":
-                    store(low(acc), job, rt * per_row, lt * per_lane)
-                else:
-                    store(low(acc), job, lt * per_lane, rt * per_row)
-                return inner
-
-            if lanes == tile_lanes:
-                return lane_step(0, carry)
-            return lax.fori_loop(0, lanes // tile_lanes, lane_step, carry)
-
-        lax.fori_loop(0, rows // tile_rows, row_step, 0)
+    weight_products(jobs, held, arrive, me_ref, keep_ref, send_ref, turned_s)
+
+
+def with_blocks(jobs, width, wide, narrow):
+    full = []
+    for rg, lg, row_axis, targets in jobs:
+        split = (wide, narrow) if row_axis == "wide" else (narrow, wide)
+        full.append((rg, lg, row_axis, width(rg) // split[0], width(lg) // split[1], targets))
+    return full
 
 
 def wgrad(me, ops, groups, jobs, total_rows, wide, narrow, vmem):
     half = wide * narrow // 2
     width = lambda g: ops[groups[g][0]].shape[1]
     depth = [sum(ops[i].shape[0] for i in g) for g in groups]
-    full = []
-    for rg, lg, row_axis, targets in jobs:
-        split = (wide, narrow) if row_axis == "wide" else (narrow, wide)
-        full.append((rg, lg, row_axis, width(rg) // split[0], width(lg) // split[1], targets))
+    full = with_blocks(jobs, width, wide, narrow)
     flops = sum(2 * depth[j[0]] * width(j[0]) * width(j[1]) for j in full)
     return pl.pallas_call(
         functools.partial(wgrad_kernel, full, groups, len(ops)),
@@ -947,43 +1042,39 @@
         labels,
         matrices,
     )
+    down_rows, att_rows = block * ff_cols // 128, block * cols // 128
+    jobs = None
+    if not (cols % 128 or ff_block % 128 or block % 16):
+        jobs = [
+            (0, 1, "wide", [(order_a, 0, block, 0)]),
+            (2, 3, "narrow", [(order_b, 0, cols, down_rows)]),
+        ]
     groups = gather_stages(order_a)
     stages = [bit for group in groups for bit in group]
     here, there = gather_all(packed, groups)
-    (gain_final, loss_part, grad_e, gain_mid, gain_in), back = loss_and_back(
-        me, narrow, stages, softness, here, there, vectors, e, gains, query_seg, passage_seg,
-        x_last, x_between, first, second, matrices,
+    (gain_final, loss_part, grad_e, gain_mid, gain_in), back, parts = loss_and_back(
+        me, narrow, stages, softness, here, there, e, gains, query_seg, passage_seg,
+        x_last, x_between, first, second, matrices, wide, jobs, down_rows + cols,
     )
-    gain_mid, gain_in = gain_mid[0], gain_in[0]
-    ffn_2 = (back["grad_f"], back["ga"], back["gb"])
+    grad_b, grad_b_2 = back["gb1"], back["gb"]
     att_2 = (back["gy"], back["gq"], back["gk"], back["gv"])
-    acc, grad_x = back["ds"], back["grad_x"]
-    grad_f, grad_a, grad_b = back["grad_f1"], back["ga1"], back["gb1"]
-    h, q, k, v, pp, pq, o, x_mid, normed, _, _, u = (first[name] for name in SAVED)
-    h_2, o_2, normed_2, u_2 = second["h"], second["o"], second["normed"], second["u"]
-
-    def attention_back(grad_a, grad_b):
-        grad_normed = dot_nt(grad_a, wg) + dot_nt(grad_b, wu)
-        back_mid, more = norm_back(x_mid, gains[1], grad_normed)
-        grad_mid = grad_x + back_mid
-        grad_y = low(grad_mid)
-        grad_o = low(dot_nt(grad_y, wo))
-        grad_q, grad_k, grad_v, total = attend_back(q, k, v, o, grad_o, pp, pq, acc)
-        return grad_mid, gain_mid + more, grad_y, grad_q, grad_k, grad_v, total
-
-    def input_back(grad_q, grad_k, grad_v, grad_mid, gain_mid, acc):
-        grad_h = dot_nt(grad_q, wq) + dot_nt(grad_k, wk) + dot_nt(grad_v, wv)
-        x = jnp.concatenate([query_x.reshape(-1, feat), passage_x.reshape(-1, feat)], axis=0).astype(F32)
-        back_in, more = norm_back(x, gains[0], grad_h)
-        sums = small_sums(
-            acc, lookup, buckets, (gain_in + more)[None], gain_mid[None], gain_final, loss_part
+    h, o, normed, u = (first[name] for name in ("h", "o", "normed", "u"))
+    h_2, o_2, normed_2, u_2 = (second[name] for name in ("h", "o", "normed", "u"))
+
+    def split_sums(value):
+        return value[:3], value[4 : 4 + heads, :buckets], value[3, :1]
+
+    def finish(grad_a, grad_b):
+        return rest_back(
+            gains, lookup, buckets, (gain_in, gain_mid, gain_final, loss_part), grad_a, grad_b,
+            back["grad_x"], back["ds"], first, matrices, query_x.reshape(-1, feat), passage_x.reshape(-1, feat),
         )
-        return grad_mid + back_in, sums
-
-    if cols % 128 or ff_block % 128 or block % 16:
-        grad_mid, gain_mid, grad_y, grad_q, grad_k, grad_v, acc = attention_back(grad_a, grad_b)
-        grad_x, sums = input_back(grad_q, grad_k, grad_v, grad_mid, gain_mid, acc)
-        sums = doubled(sums, order_a)
+
+    if jobs is None:
+        grad_f, grad_a = back["grad_f1"], back["ga1"]
+        ffn_2 = (back["grad_f"], back["ga"], grad_b_2)
+        sums, grad_y, grad_q, grad_k, grad_v, grad_x = finish(grad_a, grad_b)
+        outs = split_sums(doubled(sums, order_a))
 
         def scatter(*pairs):
             full = low(sum(dot_tn(left, right) for left, right in pairs))
@@ -1000,29 +1091,15 @@
         grad_proj = scatter((pooled, grad_e))
     else:
         orders = (order_a, order_b)
-        down_rows, att_rows = block * ff_cols // 128, block * cols // 128
-        parts = wgrad(
-            me,
-            [grad_f, ffn_2[0], u, u_2, normed, normed_2, grad_a, ffn_2[1]],
-            [(0, 1), (2, 3), (4, 5), (6, 7)],
-            [
-                (0, 1, "wide", [(order_a, 0, block, 0)]),
-                (2, 3, "narrow", [(order_b, 0, cols, down_rows)]),
-            ],
-            down_rows + cols,
-            wide,
-            narrow,
-            16,
-        )
         finals = [("turn", 0, block, ff_cols), ("keep", down_rows, cols, ff_block)]
         ffn = Chunk(*parts, down_rows, orders, finals)
 
         cut = (cols + att_rows) // 2 // 16 * 16
 
-        def make_up(grad_b, *rest):
+        def make_up(grad_b, grad_b_2):
             return wgrad(
                 me,
-                [normed, normed_2, grad_b, ffn_2[2], grad_e, pooled],
+                [normed, normed_2, grad_b, grad_b_2, grad_e, pooled],
                 [(0, 1), (2, 3), (4,), (5,)],
                 [
                     (0, 1, "narrow", [(order_a, 0, cut, 0), (order_b, cut, cols - cut, cut)]),
@@ -1031,22 +1108,17 @@
                 cols + att_rows,
                 wide,
                 narrow,
-                12,
+                48,
             )
 
-        parts = exchange([ffn], make_up, (grad_b, normed, normed_2, grad_a))
+        parts = exchange([ffn], make_up, (grad_b, grad_b_2))
         finals = [("keep", 0, cols, ff_block), ("turn", cols, block, cols)]
         up = Chunk(*parts, cut, orders, finals)
 
-        def rest_back(grad_a, grad_b):
-            grad_mid, gain_mid, grad_y, grad_q, grad_k, grad_v, acc = attention_back(grad_a, grad_b)
-            grad_x, sums = input_back(grad_q, grad_k, grad_v, grad_mid, gain_mid, acc)
-            return grad_x, sums, grad_y, grad_q, grad_k, grad_v
-
-        grad_x, sums, *grads = exchange([ffn, up], rest_back, (grad_a, grad_b))
+        sums, *grads, grad_x = exchange([ffn, up], finish, (back["ga1"], grad_b))
 
         def make_rest(sums, grad_y, grad_q, grad_k, grad_v):
-            got = [swap(sums, *to) for to in relatives(order_a[-2:])]
+            got = swap(sums, order_a[-2])
             parts = wgrad(
                 me,
                 [grad_y, att_2[0], o, o_2, grad_q, att_2[1], h, h_2, grad_k, att_2[2], grad_v, att_2[3]],
@@ -1063,19 +1135,19 @@
                 12,
             )
             got, parts = lax.optimization_barrier((got, parts))
-            return parts, (sums + got[0]) + (got[1] + got[2])
+            return parts, sums + got
 
         parts, sums = exchange([ffn, up], make_rest, (sums, *grads))
         att = Chunk(*parts, 2 * att_rows, orders, [("turn", i * att_rows, block, cols) for i in range(4)], True)
-        for n in range(3):
+        for stage in order_a[-1:] + order_a[:2]:
             live = [f for f in (att, up, ffn) if not f.done]
-            sums = exchange(live, lambda value: doubled(value, order_a[n : n + 1]), (sums,))
-        exchange([att], lambda: (), ())
+            sums = exchange(live, lambda value: doubled(value, [stage]), (sums,))
+        outs = exchange([att], lambda value: split_sums(doubled(value, order_a[2:-2])), (sums,))
         grad_down, grad_gate = ffn.result
         grad_up, grad_proj = up.result
         grad_out, grad_query, grad_key, grad_value = att.result
-    gain_total, bucket_total = sums[:3], sums[4 : 4 + heads, :buckets]
-    mean_loss = sums[3, :1] / (qrows * QSEGS * wide * narrow)
+    gain_total, bucket_total, loss_total = outs
+    mean_loss = loss_total / (qrows * QSEGS * wide * narrow)
     return (
         mean_loss,
         vectors[:QSEGS],

time: 206 us -> 197 us (0.956)
  Pallas kernels: 93.3 us -> 103 us
  local copies, waits for them, and re-layouts: 16.7 us -> 9.38 us
  starting transfers between devices: 41.3 us -> 35.1 us
  matrix products: 5.19 us -> 0 us
    pallas_call x3 -> x2, Pallas kernels: 28.7 us -> 48.1 us  [the longest x1 30.4 us: loss_and_back(): pl.pallas_call(functools.partial(back_kernel, narrow, stages, qlen, 4, n_...]
    pallas_call x3 -> x2, Pallas kernels: 28.1 us -> 18.7 us  [wgrad(): pl.pallas_call(functools.partial(wgrad_kernel, full, groups, len(ops)), o...]
    ppermute x26 -> x25, starting transfers between devices: 32.8 us -> 24.5 us  [swap(): return lax.ppermute(a, 'wide', [(i, i ^ dw) for i in range(wide)])]
    unnamed x96 -> x64, local copies, waits for them, and re-layouts: 12.1 us -> 4.84 us
    dot_general x6 -> x0, matrix products: 5.19 us -> none  [dot_nt(): lax.dot_general(a, b, (((1,), (1,)), ((), ())), preferred_element_type=F3...]
    ppermute x26 -> x25, waiting for transfers between devices: 29.1 us -> 32.5 us  [swap(): return lax.ppermute(a, 'wide', [(i, i ^ dw) for i in range(wide)])]
    ppermute x8, waiting for transfers between devices: 11.8 us -> 9.71 us  [swap(): return lax.ppermute(a, 'narrow', [(i, i ^ dn) for i in range(narrow)])]
  transfers between devices with their start and end apart: 35 -> 34, of which waited for: 17 -> 18; matrix products, arithmetic and copies ran while one was open for 4% -> 3% of each run, Pallas kernels for 12% -> 19%
where the time goes in v1:
time: 197 us; the launch traced here: 196 us
  Pallas kernels  103 us (52%)
  waiting for transfers between devices  44.1 us (22%)
  starting transfers between devices  35.1 us (18%)
  local copies, waits for them, and re-layouts  9.38 us (5%)
  between operations  3.54 us (2%)
    ppermute x25, waiting for transfers between devices, swap(): return lax.ppermute(a, 'wide', [(i, i ^ dw) for i in range(wide)])  32.5 us
    pallas_call x1, Pallas kernels, loss_and_back(): pl.pallas_call(functools.partial(back_kernel, narrow, stages, qlen, 4, n_...  30.4 us
    pallas_call x1, Pallas kernels, forward(): pl.pallas_call(functools.partial(forward_kernel, qlen, plen, 4), out_shap...  29.7 us
    ppermute x25, starting transfers between devices, swap(): return lax.ppermute(a, 'wide', [(i, i ^ dw) for i in range(wide)])  24.5 us
    pallas_call x2, Pallas kernels, wgrad(): pl.pallas_call(functools.partial(wgrad_kernel, full, groups, len(ops)), o...  18.7 us
    pallas_call x1, Pallas kernels, rest_back(): pl.pallas_call(functools.partial(rest_kernel, qlen, buckets, len(fetched)...  17.6 us
    ppermute x8, waiting for transfers between devices, swap(): return lax.ppermute(a, 'narrow', [(i, i ^ dn) for i in range(narrow)])  9.71 us
    ppermute x8, starting transfers between devices, swap(): return lax.ppermute(a, 'narrow', [(i, i ^ dn) for i in range(narrow)])  8.12 us
  transfers between devices with their start and end apart: 34, of which 18 were waited for; matrix products, arithmetic and copies ran while one was open for 3% of the time, Pallas kernels for 19%

profile of v1, /device:TPU:0, one launch (start us, length us, event | category | flops | bytes accessed | tf_op | source)
XLA Modules:
  0.0 196.2 jit_solution(16861394645687681604)
XLA Ops:
  0.6 29.7 %forward.1 = (bf16[8,768]{1,0:T(8,128)(2,1)}, f32[8,768]{1,0:T(8,128)}, f32[8,768]{1,0:T(8,128)}, bf16[8,768]{1,0:T(8,128)(2,1)}, f32[320,768]{1,0:T(8,128)}, /*...) custom-call(bf16[64,768]{1,0:T(8,128)(2,1)} %bitcast.20, ...), custom_call_target="tpu_custom_call" | custom-call | flops 9814671360 | bytes 15335424 | tf_op jit(solution)/shard_map/forward/pallas_call | solution.py:332
  30.4 5.2 %collective-permute-start.2 = (bf16[8,768]{1,0:T(8,128)(2,1)}, bf16[8,768]{1,0:T(8,128)(2,1)S(1)}, u32[]{:S(2)}, u32[]{:S(2)}) collective-permute-start(bf16[8,768]{1,0:T(8,128)(2,1)} %get-tuple-element.212.refs_0_), channel_id=1, source_target_pairs={{0,24},{2,26},{4,28},{6,30},{8,16},{10,18},{12,20},{14,22},{16,8},... | collective-permute-start | bytes 36872 | tf_op jit(solution)/shard_map/ppermute | solution.py:847
  35.5 0.6 collective-permute-start
  36.2 1.2 collective-permute-done.2.refs_3_
  37.4 2.9 %collective-permute-done.1.refs_2_ = bf16[8,768]{1,0:T(8,128)(2,1)S(1)} collective-permute-done((bf16[8,768]{1,0:T(8,128)(2,1)}, bf16[8,768]{1,0:T(8,128)(2,1)S(1)}, u32[]{:S(2)}, u32[]{:S(2)}) %collective-permute-start.1) | collective-permute-done | bytes 12320 | tf_op jit(solution)/shard_map/ppermute | solution.py:847
  40.4 0.7 copy-done.13
  41.1 2.4 %collective-permute-start.5 = (bf16[32,768]{1,0:T(8,128)(2,1)S(1)}, bf16[32,768]{1,0:T(8,128)(2,1)S(1)}, u32[]{:S(2)}, u32[]{:S(2)}) collective-permute-start(bf16[32,768]{1,0:T(8,128)(2,1)S(1)} %join.2.refs_0_), channel_id=1, source_target_pairs={{0,5},{1,4},{2,7},{3,6},{4,1},{5,0},{6,3},{7,2},{8,13},{9,12},{10,... | collective-permute-start | bytes 147464 | tf_op jit(solution)/shard_map/ppermute | solution.py:851
  43.5 0.5 collective-permute-start.4
  44.0 0.5 collective-permute-start.3
  44.6 1.9 collective-permute-done.5.refs_3_
  46.5 1.1 collective-permute-done.4.refs_2_
  47.6 0.5 collective-permute-done.3.refs_1_
  48.9 0.6 pad_add_fusion.refs_0_.me_ref
  49.6 0.7 copy-done.30
  50.3 30.4 %loss_and_back.1 = (f32[1,768]{1,0:T(1,128)}, f32[1,128]{1,0:T(1,128)}, bf16[8,768]{1,0:T(8,128)(2,1)}, f32[1,768]{1,0:T(1,128)}, f32[1,768]{1,0:T(1,128)}, /*in...) custom-call(s32[2]{0:T(128)} %pad_add_fusion.refs_0_.me_ref, ...), custom_call_target="tpu_custom_call" | custom-call | flops 7361003520 | bytes 15335424 | tf_op jit(solution)/shard_map/loss_and_back/pallas_call | solution.py:561
  81.2 1.3 copy-done.1
  82.5 1.3 copy-done.20
  83.8 0.7 copy-done.25
  84.5 8.1 %wgrad.2 = (bf16[16,528,128]{2,1,0:T(8,128)(2,1)S(1)}, bf16[16,528,128]{2,1,0:T(8,128)(2,1)}) custom-call(s32[2]{0:T(128)S(1)} %copy-done.19, bf16[320,768]{1,0:T(8,128)(2,1)S(1)} %copy-done.7, bf16[320,768]{1,0:T(8,128)(2,1)S(1)} %copy-done.8, bf16[320,2048]{1,0:T(8,128)(2,1)S(1)} %copy-done.1, bf16[320,2048]{1,0:T(8,128)(2,1)S(1)} %copy-done.20, ...), custom_call_target="tpu_custom_call" | custom-call | flops 2022703104 | bytes 7901184 | tf_op jit(solution)/shard_map/wgrad/pallas_call | solution.py:828
  92.7 1.7 advance.7
  94.7 0.5 collective-permute-start.8
  95.2 1.5 collective-permute-start.9
  96.8 17.6 %rest_back.1 = (f32[16,768]{1,0:T(8,128)S(1)}, bf16[320,768]{1,0:T(8,128)(2,1)S(1)}, bf16[320,768]{1,0:T(8,128)(2,1)S(1)}, bf16[320,768]{1,0:T(8,128)(2,1)S(1)},...) custom-call(f32[3,768]{1,0:T(4,128)S(1)} %copy-done.12, s32[1,511]{1,0:T(1,128)S(1)} %bitcast.23, ...), custom_call_target="tpu_custom_call" | custom-call | flops 5284823040 | bytes 11010048 | tf_op jit(solution)/shard_map/rest_back/pallas_call | solution.py:658
  114.8 1.1 advance.8
  115.9 1.6 collective-permute-start.14
  117.4 1.5 collective-permute-start.13
  118.9 0.5 collective-permute-start.11
  119.4 0.5 collective-permute-start.12
  120.1 10.6 %wgrad.3 = (bf16[16,576,128]{2,1,0:T(8,128)(2,1)S(1)}, bf16[16,576,128]{2,1,0:T(8,128)(2,1)S(1)}) custom-call(s32[2]{0:T(128)S(1)} %copy-done.19, bf16[320,768]{1,0:T(8,128)(2,1)S(1)} %get-tuple-element.299.refs_0_, bf16[320,768]{1,0:T(8,128)(2,1)S(1)} %copy-done.21, bf16[320,768]{1,0:T(8,128)(2,1)S(1)} %copy-done.3, bf16[320,768]{1,0:T(8,128)(2,1)S(1)} %copy-done.4, ...), custom_call_target="tpu_custom_call" | custom-call | flops 3019898880 | bytes 11796480 | tf_op jit(solution)/shard_map/wgrad/pallas_call | solution.py:828
  130.7 7.8 %collective-permute-done.11.refs_1_ = bf16[4,384,128]{2,1,0:T(8,128)(2,1)S(1)} collective-permute-done((bf16[4,384,128]{2,1,0:T(8,128)(2,1)S(1)}, bf16[4,384,128]{2,1,0:T(8,128)(2,1)S(1)}, u32[]{:S(2)}, u32[]{:S(2)}) %collective-permute-start.11) | collective-permute-done | bytes 393248 | tf_op jit(solution)/shard_map/ppermute | solution.py:849
  138.5 0.4 collective-permute-done.12.refs_3_
  138.9 0.5 advance.9
  139.6 1.3 collective-permute-start.18
  140.9 1.0 collective-permute-start.17
  141.9 2.0 %collective-permute-start.20 = (f32[16,768]{1,0:T(8,128)S(1)}, f32[16,768]{1,0:T(8,128)S(1)}, u32[]{:S(2)}, u32[]{:S(2)}) collective-permute-start(f32[16,768]{1,0:T(8,128)S(1)} %add.15), channel_id=1, source_target_pairs={{0,16},{2,18},{4,20},{6,22},{8,24},{10,26},{12,28},{14,30},{16,0},... | collective-permute-start | bytes 147464 | tf_op jit(solution)/shard_map/ppermute | solution.py:847
  143.9 6.0 %collective-permute-done.20 = f32[16,768]{1,0:T(8,128)S(1)} collective-permute-done((f32[16,768]{1,0:T(8,128)S(1)}, f32[16,768]{1,0:T(8,128)S(1)}, u32[]{:S(2)}, u32[]{:S(2)}) %collective-permute-start.20) | collective-permute-done | bytes 49184 | tf_op jit(solution)/shard_map/ppermute | solution.py:847
  149.9 2.2 %collective-permute-done.19.refs_7_ = bf16[2,768,128]{2,1,0:T(8,128)(2,1)S(1)} collective-permute-done((bf16[2,768,128]{2,1,0:T(8,128)(2,1)S(1)}, bf16[2,768,128]{2,1,0:T(8,128)(2,1)S(1)}, u32[]{:S(2)}, u32[]{:S(2)}) %collective-permute-start.19) | collective-permute-done | bytes 393248 | tf_op jit(solution)/shard_map/ppermute | solution.py:847
  152.1 0.9 advance.10
  153.0 1.3 collective-permute-start.21
  154.3 1.0 collective-permute-start.22
  155.3 2.1 %collective-permute-start.23 = (bf16[2,528,128]{2,1,0:T(8,128)(2,1)S(1)}, bf16[2,528,128]{2,1,0:T(8,128)(2,1)S(1)}, u32[]{:S(2)}, u32[]{:S(2)}) collective-permute-start(bf16[2,528,128]{2,1,0:T(8,128)(2,1)S(1)} %get-tuple-element.356), channel_id=1, source_target_pairs={{0,8},{2,10},{4,12},{6,14},{8,0},{10,2},{12,4},{14,6},{16,24},{18,... | collective-permute-start | bytes 811016 | tf_op jit(solution)/shard_map/ppermute | solution.py:847
  157.6 1.2 collective-permute-done.25
  158.9 9.2 %collective-permute-done.24.refs_7_ = bf16[1,768,128]{2,1,0:T(8,128)(2,1)S(1)} collective-permute-done((bf16[1,768,128]{2,1,0:T(8,128)(2,1)S(1)}, bf16[1,768,128]{2,1,0:T(8,128)(2,1)S(1)}, u32[]{:S(2)}, u32[]{:S(2)}) %collective-permute-start.24) | collective-permute-done | bytes 196640 | tf_op jit(solution)/shard_map/ppermute | solution.py:847
  168.1 0.7 collective-permute-done.22.refs_3_
  168.8 1.1 advance.11
  169.9 1.0 collective-permute-start.26
  170.9 0.8 collective-permute-start.27
  171.7 0.6 slice.25
  172.3 0.6 slice.24
  172.9 1.2 collective-permute-start.29
  174.2 1.5 collective-permute-start.28
  175.7 0.9 slice_bitcast_fusion
  176.6 2.4 %collective-permute-done.29 = f32[16,768]{1,0:T(8,128)S(1)} collective-permute-done((f32[16,768]{1,0:T(8,128)S(1)}, f32[16,768]{1,0:T(8,128)S(1)}, u32[]{:S(2)}, u32[]{:S(2)}) %collective-permute-start.29) | collective-permute-done | bytes 49184 | tf_op jit(solution)/shard_map/ppermute | solution.py:847
  179.1 2.5 %collective-permute-done.28.refs_5_ = bf16[1,528,128]{2,1,0:T(8,128)(2,1)S(1)} collective-permute-done((bf16[1,528,128]{2,1,0:T(8,128)(2,1)S(1)}, bf16[1,528,128]{2,1,0:T(8,128)(2,1)S(1)}, u32[]{:S(2)}, u32[]{:S(2)}) %collective-permute-start.28) | collective-permute-done | bytes 135200 | tf_op jit(solution)/shard_map/ppermute | solution.py:847
  181.5 0.8 advance.12
  182.3 1.0 collective-permute-start.33
  183.5 2.4 %collective-permute-start.31 = (bf16[1,576,128]{2,1,0:T(8,128)(2,1)S(1)}, bf16[1,576,128]{2,1,0:T(8,128)(2,1)S(1)}, u32[]{:S(2)}, u32[]{:S(2)}) collective-permute-start(bf16[1,576,128]{2,1,0:T(8,128)(2,1)S(1)} %get-tuple-element.389), channel_id=1, source_target_pairs={{0,8},{2,10},{4,12},{6,14},{8,0},{10,2},{12,4},{14,6},{16,24},{18,... | collective-permute-start | bytes 442376 | tf_op jit(solution)/shard_map/ppermute | solution.py:847
  185.9 1.8 collective-permute-start.32
  187.8 0.7 slice_bitcast_fusion.1
  188.5 0.5 slice.30
  189.0 0.6 slice.29
  189.6 0.6 slice.28
  190.2 3.5 %collective-permute-done.30.refs_1_ = bf16[1,576,128]{2,1,0:T(8,128)(2,1)S(1)} collective-permute-done((bf16[1,576,128]{2,1,0:T(8,128)(2,1)S(1)}, bf16[1,576,128]{2,1,0:T(8,128)(2,1)S(1)}, u32[]{:S(2)}, u32[]{:S(2)}) %collective-permute-start.30) | collective-permute-done | bytes 147488 | tf_op jit(solution)/shard_map/ppermute | solution.py:847
  194.4 0.7 advance.13
  (95 shorter events, 1.9 us)
Async XLA Ops:
  30.4 7.0 %collective-permute-start.2 = (bf16[8,768]{1,0:T(8,128)(2,1)}, bf16[8,768]{1,0:T(8,128)(2,1)S(1)}, u32[]{:S(2)}, u32[]{:S(2)}) collective-permute-start(bf16[8,768]{1,0:T(8,128)(2,1)} %get-tuple-element.212.refs_0_), channel_id=1, source_target_pairs={{0,24},{2,26},{4,28},{6,30},{8,16},{10,18},{12,20},{14,22},{16,8},... | collective-permute-start | bytes 36872 | tf_op jit(solution)/shard_map/ppermute | solution.py:847
  35.5 4.8 %collective-permute-start.1 = (bf16[8,768]{1,0:T(8,128)(2,1)}, bf16[8,768]{1,0:T(8,128)(2,1)S(1)}, u32[]{:S(2)}, u32[]{:S(2)}) collective-permute-start(bf16[8,768]{1,0:T(8,128)(2,1)} %get-tuple-element.212.refs_0_), channel_id=1, source_target_pairs={{0,16},{2,18},{4,20},{6,22},{8,24},{10,26},{12,28},{14,30},{16,0},... | collective-permute-start | bytes 36872 | tf_op jit(solution)/shard_map/ppermute | solution.py:847
  35.5 4.8 %collective-permute-start = (bf16[8,768]{1,0:T(8,128)(2,1)}, bf16[8,768]{1,0:T(8,128)(2,1)S(1)}, u32[]{:S(2)}, u32[]{:S(2)}) collective-permute-start(bf16[8,768]{1,0:T(8,128)(2,1)} %get-tuple-element.212.refs_0_), channel_id=1, source_target_pairs={{0,8},{2,10},{4,12},{6,14},{8,0},{10,2},{12,4},{14,6},{16,24},{18,... | collective-permute-start | bytes 36872 | tf_op jit(solution)/shard_map/ppermute | solution.py:847
  40.3 0.7 copy-start.13
  41.1 5.4 %collective-permute-start.5 = (bf16[32,768]{1,0:T(8,128)(2,1)S(1)}, bf16[32,768]{1,0:T(8,128)(2,1)S(1)}, u32[]{:S(2)}, u32[]{:S(2)}) collective-permute-start(bf16[32,768]{1,0:T(8,128)(2,1)S(1)} %join.2.refs_0_), channel_id=1, source_target_pairs={{0,5},{1,4},{2,7},{3,6},{4,1},{5,0},{6,3},{7,2},{8,13},{9,12},{10,... | collective-permute-start | bytes 147464 | tf_op jit(solution)/shard_map/ppermute | solution.py:851
  43.5 4.1 %collective-permute-start.4 = (bf16[32,768]{1,0:T(8,128)(2,1)S(1)}, bf16[32,768]{1,0:T(8,128)(2,1)S(1)}, u32[]{:S(2)}, u32[]{:S(2)}) collective-permute-start(bf16[32,768]{1,0:T(8,128)(2,1)S(1)} %join.2.refs_0_), channel_id=1, source_target_pairs={{0,1},{1,0},{2,3},{3,2},{4,5},{5,4},{6,7},{7,6},{8,9},{9,8},{10,11... | collective-permute-start | bytes 147464 | tf_op jit(solution)/shard_map/ppermute | solution.py:849
  44.0 4.1 %collective-permute-start.3 = (bf16[32,768]{1,0:T(8,128)(2,1)S(1)}, bf16[32,768]{1,0:T(8,128)(2,1)S(1)}, u32[]{:S(2)}, u32[]{:S(2)}) collective-permute-start(bf16[32,768]{1,0:T(8,128)(2,1)S(1)} %join.2.refs_0_), channel_id=1, source_target_pairs={{0,4},{2,6},{4,0},{6,2},{8,12},{10,14},{12,8},{14,10},{16,20},{18,... | collective-permute-start | bytes 147464 | tf_op jit(solution)/shard_map/ppermute | solution.py:847
  48.1 1.5 copy-start.2
  48.1 1.5 collective-permute-start.6
  50.3 30.8 %copy-start.7 = (bf16[320,768]{1,0:T(8,128)(2,1)S(1)}, bf16[320,768]{1,0:T(8,128)(2,1)}, u32[]{:S(2)}) copy-start(bf16[320,768]{1,0:T(8,128)(2,1)} %get-tuple-element.229.refs_31_.refs_0_) | copy-start | bytes 1474564
  50.3 30.8 %copy-start.8 = (bf16[320,768]{1,0:T(8,128)(2,1)S(1)}, bf16[320,768]{1,0:T(8,128)(2,1)}, u32[]{:S(2)}) copy-start(bf16[320,768]{1,0:T(8,128)(2,1)} %get-tuple-element.230.refs_32_.refs_1_) | copy-start | bytes 1474564
  50.3 30.8 %copy-start.19 = (s32[2]{0:T(128)S(1)}, s32[2]{0:T(128)}, u32[]{:S(2)}) copy-start(s32[2]{0:T(128)} %pad_add_fusion.refs_0_.me_ref) | copy-start | bytes 28
  50.3 30.8 %copy-start.28 = (bf16[8,768]{1,0:T(8,128)(2,1)S(1)}, bf16[8,768]{1,0:T(8,128)(2,1)}, u32[]{:S(2)}) copy-start(bf16[8,768]{1,0:T(8,128)(2,1)} %get-tuple-element.240.refs_5_) | copy-start | bytes 36868
  80.8 11.8 %collective-permute-start.7 = (bf16[16,768,128]{2,1,0:T(8,128)(2,1)}, bf16[16,768,128]{2,1,0:T(8,128)(2,1)S(1)}, u32[]{:S(2)}, u32[]{:S(2)}) collective-permute-start(bf16[16,768,128]{2,1,0:T(8,128)(2,1)} %get-tuple-element.236), channel_id=1, source_target_pairs={{0,2},{2,0},{4,6},{6,4},{8,10},{10,8},{12,14},{14,12},{16,18},{18,... | collective-permute-start | bytes 9437192 | tf_op jit(solution)/shard_map/ppermute | solution.py:847
  81.2 1.3 copy-start.1
  82.5 1.3 copy-start.20
  84.5 8.1 %copy-start = (bf16[16,768,128]{2,1,0:T(8,128)(2,1)S(1)}, bf16[16,768,128]{2,1,0:T(8,128)(2,1)}, u32[]{:S(2)}) copy-start(bf16[16,768,128]{2,1,0:T(8,128)(2,1)} %get-tuple-element.235.refs_0_) | copy-start | bytes 9437188
  92.6 4.1 %copy-start.5 = (bf16[320,768]{1,0:T(8,128)(2,1)S(1)}, bf16[320,768]{1,0:T(8,128)(2,1)}, u32[]{:S(2)}) copy-start(bf16[320,768]{1,0:T(8,128)(2,1)} %get-tuple-element.263.refs_13_) | copy-start | bytes 1474564
  92.6 4.1 %copy-start.6 = (bf16[320,768]{1,0:T(8,128)(2,1)S(1)}, bf16[320,768]{1,0:T(8,128)(2,1)}, u32[]{:S(2)}) copy-start(bf16[320,768]{1,0:T(8,128)(2,1)} %get-tuple-element.264.refs_14_) | copy-start | bytes 1474564
  92.6 4.1 %copy-start.9 = (bf16[1,256,768]{2,1,0:T(8,128)(2,1)S(1)}, bf16[1,256,768]{2,1,0:T(8,128)(2,1)}, u32[]{:S(2)}) copy-start(bf16[1,256,768]{2,1,0:T(8,128)(2,1)} %param.19) | copy-start | bytes 1179652
  92.6 4.1 %copy-start.10 = (bf16[12,64,64]{2,1,0:T(8,128)(2,1)S(1)}, bf16[12,64,64]{2,1,0:T(8,128)(2,1)}, u32[]{:S(2)}) copy-start(bf16[12,64,64]{2,1,0:T(8,128)(2,1)} %get-tuple-element.268.refs_18_) | copy-start | bytes 294916
  92.7 4.1 %copy-start.11 = (bf16[1,64,768]{2,1,0:T(8,128)(2,1)S(1)}, bf16[1,64,768]{2,1,0:T(8,128)(2,1)}, u32[]{:S(2)}) copy-start(bf16[1,64,768]{2,1,0:T(8,128)(2,1)} %param.17) | copy-start | bytes 294916
  92.7 4.1 %copy-start.12 = (f32[3,768]{1,0:T(4,128)S(1)}, f32[3,768]{1,0:T(4,128)}, u32[]{:S(2)}) copy-start(f32[3,768]{1,0:T(4,128)} %refs_0_.1) | copy-start | bytes 27652
  92.7 4.1 %copy-start.14 = (f32[1,768]{1,0:T(1,128)S(1)}, f32[1,768]{1,0:T(1,128)}, u32[]{:S(2)}) copy-start(f32[1,768]{1,0:T(1,128)} %get-tuple-element.257.refs_4_) | copy-start | bytes 9220
  92.7 4.1 %copy-start.15 = (f32[1,768]{1,0:T(1,128)S(1)}, f32[1,768]{1,0:T(1,128)}, u32[]{:S(2)}) copy-start(f32[1,768]{1,0:T(1,128)} %get-tuple-element.256.refs_3_) | copy-start | bytes 9220
  92.7 4.1 %copy-start.16 = (f32[1,768]{1,0:T(1,128)S(1)}, f32[1,768]{1,0:T(1,128)}, u32[]{:S(2)}) copy-start(f32[1,768]{1,0:T(1,128)} %get-tuple-element.255.refs_2_) | copy-start | bytes 9220
  92.7 4.1 %copy-start.17 = (s32[511]{0:T(512)S(1)}, s32[511]{0:T(512)}, u32[]{:S(2)}) copy-start(s32[511]{0:T(512)} %param.22) | copy-start | bytes 6136
  92.7 4.1 %copy-start.18 = (f32[1,128]{1,0:T(1,128)S(1)}, f32[1,128]{1,0:T(1,128)}, u32[]{:S(2)}) copy-start(f32[1,128]{1,0:T(1,128)} %get-tuple-element.258.refs_5_) | copy-start | bytes 1540
  94.5 20.2 %collective-permute-start.10 = (bf16[16,528,128]{2,1,0:T(8,128)(2,1)}, bf16[16,528,128]{2,1,0:T(8,128)(2,1)S(1)}, u32[]{:S(2)}, u32[]{:S(2)}) collective-permute-start(bf16[16,528,128]{2,1,0:T(8,128)(2,1)} %get-tuple-element.254), channel_id=1, source_target_pairs={{0,2},{2,0},{4,6},{6,4},{8,10},{10,8},{12,14},{14,12},{16,18},{18,... | collective-permute-start | bytes 6488072 | tf_op jit(solution)/shard_map/ppermute | solution.py:847
  94.7 20.0 %collective-permute-start.8 = (bf16[8,384,128]{2,1,0:T(8,128)(2,1)}, bf16[8,384,128]{2,1,0:T(8,128)(2,1)S(1)}, u32[]{:S(2)}, u32[]{:S(2)}) collective-permute-start(bf16[8,384,128]{2,1,0:T(8,128)(2,1)} %get-tuple-element.252), channel_id=1, source_target_pairs={{0,4},{2,6},{4,0},{6,2},{8,12},{10,14},{12,8},{14,10},{16,20},{18,... | collective-permute-start | bytes 2359304 | tf_op jit(solution)/shard_map/ppermute | solution.py:847
  95.2 19.5 %collective-permute-start.9 = (bf16[8,384,128]{2,1,0:T(8,128)(2,1)S(1)}, bf16[8,384,128]{2,1,0:T(8,128)(2,1)S(1)}, u32[]{:S(2)}, u32[]{:S(2)}) collective-permute-start(bf16[8,384,128]{2,1,0:T(8,128)(2,1)S(1)} %get-tuple-element.253), channel_id=1, source_target_pairs={{0,1},{1,0},{2,3},{3,2},{4,5},{5,4},{6,7},{7,6},{8,9},{9,8},{10,11... | collective-permute-start | bytes 2359304 | tf_op jit(solution)/shard_map/ppermute | solution.py:849
  114.7 5.3 %copy-start.3 = (bf16[320,768]{1,0:T(8,128)(2,1)S(1)}, bf16[320,768]{1,0:T(8,128)(2,1)}, u32[]{:S(2)}) copy-start(bf16[320,768]{1,0:T(8,128)(2,1)} %get-tuple-element.266.refs_16_.refs_2_) | copy-start | bytes 1474564
  114.7 5.3 %copy-start.4 = (bf16[320,768]{1,0:T(8,128)(2,1)S(1)}, bf16[320,768]{1,0:T(8,128)(2,1)}, u32[]{:S(2)}) copy-start(bf16[320,768]{1,0:T(8,128)(2,1)} %get-tuple-element.219.refs_18_.refs_3_) | copy-start | bytes 1474564
  114.7 5.3 %copy-start.21 = (bf16[320,768]{1,0:T(8,128)(2,1)S(1)}, bf16[320,768]{1,0:T(8,128)(2,1)}, u32[]{:S(2)}) copy-start(bf16[320,768]{1,0:T(8,128)(2,1)} %get-tuple-element.300.refs_1_) | copy-start | bytes 1474564
  114.7 5.3 %copy-start.22 = (bf16[320,768]{1,0:T(8,128)(2,1)S(1)}, bf16[320,768]{1,0:T(8,128)(2,1)}, u32[]{:S(2)}) copy-start(bf16[320,768]{1,0:T(8,128)(2,1)} %get-tuple-element.302.refs_5_) | copy-start | bytes 1474564
  114.7 5.3 %copy-start.23 = (bf16[320,768]{1,0:T(8,128)(2,1)S(1)}, bf16[320,768]{1,0:T(8,128)(2,1)}, u32[]{:S(2)}) copy-start(bf16[320,768]{1,0:T(8,128)(2,1)} %get-tuple-element.306.refs_9_) | copy-start | bytes 1474564
  114.7 5.3 %copy-start.24 = (bf16[320,768]{1,0:T(8,128)(2,1)S(1)}, bf16[320,768]{1,0:T(8,128)(2,1)}, u32[]{:S(2)}) copy-start(bf16[320,768]{1,0:T(8,128)(2,1)} %get-tuple-element.308.refs_11_) | copy-start | bytes 1474564
  114.8 5.3 %copy-start.26 = (bf16[320,768]{1,0:T(8,128)(2,1)S(1)}, bf16[320,768]{1,0:T(8,128)(2,1)}, u32[]{:S(2)}) copy-start(bf16[320,768]{1,0:T(8,128)(2,1)} %get-tuple-element.303.refs_6_) | copy-start | bytes 1474564
  114.8 5.3 %copy-start.27 = (bf16[320,768]{1,0:T(8,128)(2,1)S(1)}, bf16[320,768]{1,0:T(8,128)(2,1)}, u32[]{:S(2)}) copy-start(bf16[320,768]{1,0:T(8,128)(2,1)} %get-tuple-element.304.refs_7_) | copy-start | bytes 1474564
  115.9 23.0 %collective-permute-start.14 = (bf16[8,272,128]{2,1,0:T(8,128)(2,1)S(1)}, bf16[8,272,128]{2,1,0:T(8,128)(2,1)S(1)}, u32[]{:S(2)}, u32[]{:S(2)}) collective-permute-start(bf16[8,272,128]{2,1,0:T(8,128)(2,1)S(1)} %get-tuple-element.297), channel_id=1, source_target_pairs={{0,1},{1,0},{2,3},{3,2},{4,5},{5,4},{6,7},{7,6},{8,9},{9,8},{10,11... | collective-permute-start | bytes 1671176 | tf_op jit(solution)/shard_map/ppermute | solution.py:849
  117.4 21.4 %collective-permute-start.13 = (bf16[8,256,128]{2,1,0:T(8,128)(2,1)S(1)}, bf16[8,256,128]{2,1,0:T(8,128)(2,1)S(1)}, u32[]{:S(2)}, u32[]{:S(2)}) collective-permute-start(bf16[8,256,128]{2,1,0:T(8,128)(2,1)S(1)} %get-tuple-element.296), channel_id=1, source_target_pairs={{0,4},{2,6},{4,0},{6,2},{8,12},{10,14},{12,8},{14,10},{16,20},{18,... | collective-permute-start | bytes 1572872 | tf_op jit(solution)/shard_map/ppermute | solution.py:847
  118.9 19.5 %collective-permute-start.11 = (bf16[4,384,128]{2,1,0:T(8,128)(2,1)S(1)}, bf16[4,384,128]{2,1,0:T(8,128)(2,1)S(1)}, u32[]{:S(2)}, u32[]{:S(2)}) collective-permute-start(bf16[4,384,128]{2,1,0:T(8,128)(2,1)S(1)} %get-tuple-element.294), channel_id=1, source_target_pairs={{0,1},{1,0},{2,3},{3,2},{4,5},{5,4},{6,7},{7,6},{8,9},{9,8},{10,11... | collective-permute-start | bytes 1179656 | tf_op jit(solution)/shard_map/ppermute | solution.py:849
  119.4 19.4 %collective-permute-start.12 = (bf16[4,384,128]{2,1,0:T(8,128)(2,1)S(1)}, bf16[4,384,128]{2,1,0:T(8,128)(2,1)S(1)}, u32[]{:S(2)}, u32[]{:S(2)}) collective-permute-start(bf16[4,384,128]{2,1,0:T(8,128)(2,1)S(1)} %get-tuple-element.295), channel_id=1, source_target_pairs={{0,4},{2,6},{4,0},{6,2},{8,12},{10,14},{12,8},{14,10},{16,20},{18,... | collective-permute-start | bytes 1179656 | tf_op jit(solution)/shard_map/ppermute | solution.py:847
  120.0 10.7 %collective-permute-start.15 = (f32[16,768]{1,0:T(8,128)S(1)}, f32[16,768]{1,0:T(8,128)S(1)}, u32[]{:S(2)}, u32[]{:S(2)}) collective-permute-start(f32[16,768]{1,0:T(8,128)S(1)} %get-tuple-element.298), channel_id=1, source_target_pairs={{0,8},{2,10},{4,12},{6,14},{8,0},{10,2},{12,4},{14,6},{16,24},{18,... | collective-permute-start | bytes 147464 | tf_op jit(solution)/shard_map/ppermute | solution.py:847
  139.4 12.7 %collective-permute-start.16 = (bf16[16,576,128]{2,1,0:T(8,128)(2,1)S(1)}, bf16[16,576,128]{2,1,0:T(8,128)(2,1)S(1)}, u32[]{:S(2)}, u32[]{:S(2)}) collective-permute-start(bf16[16,576,128]{2,1,0:T(8,128)(2,1)S(1)} %get-tuple-element.332), channel_id=1, source_target_pairs={{0,2},{2,0},{4,6},{6,4},{8,10},{10,8},{12,14},{14,12},{16,18},{18,... | collective-permute-start | bytes 7077896 | tf_op jit(solution)/shard_map/ppermute | solution.py:847
  139.5 12.6 %collective-permute-start.19 = (bf16[2,768,128]{2,1,0:T(8,128)(2,1)S(1)}, bf16[2,768,128]{2,1,0:T(8,128)(2,1)S(1)}, u32[]{:S(2)}, u32[]{:S(2)}) collective-permute-start(bf16[2,768,128]{2,1,0:T(8,128)(2,1)S(1)} %get-tuple-element.335), channel_id=1, source_target_pairs={{0,8},{2,10},{4,12},{6,14},{8,0},{10,2},{12,4},{14,6},{16,24},{18,... | collective-permute-start | bytes 1179656 | tf_op jit(solution)/shard_map/ppermute | solution.py:847
  139.6 10.3 %collective-permute-start.18 = (bf16[4,272,128]{2,1,0:T(8,128)(2,1)S(1)}, bf16[4,272,128]{2,1,0:T(8,128)(2,1)S(1)}, u32[]{:S(2)}, u32[]{:S(2)}) collective-permute-start(bf16[4,272,128]{2,1,0:T(8,128)(2,1)S(1)} %get-tuple-element.334), channel_id=1, source_target_pairs={{0,4},{2,6},{4,0},{6,2},{8,12},{10,14},{12,8},{14,10},{16,20},{18,... | collective-permute-start | bytes 835592 | tf_op jit(solution)/shard_map/ppermute | solution.py:847
  140.9 9.0 %collective-permute-start.17 = (bf16[4,256,128]{2,1,0:T(8,128)(2,1)S(1)}, bf16[4,256,128]{2,1,0:T(8,128)(2,1)S(1)}, u32[]{:S(2)}, u32[]{:S(2)}) collective-permute-start(bf16[4,256,128]{2,1,0:T(8,128)(2,1)S(1)} %get-tuple-element.333), channel_id=1, source_target_pairs={{0,1},{1,0},{2,3},{3,2},{4,5},{5,4},{6,7},{7,6},{8,9},{9,8},{10,11... | collective-permute-start | bytes 786440 | tf_op jit(solution)/shard_map/ppermute | solution.py:849
  141.9 8.0 %collective-permute-start.20 = (f32[16,768]{1,0:T(8,128)S(1)}, f32[16,768]{1,0:T(8,128)S(1)}, u32[]{:S(2)}, u32[]{:S(2)}) collective-permute-start(f32[16,768]{1,0:T(8,128)S(1)} %add.15), channel_id=1, source_target_pairs={{0,16},{2,18},{4,20},{6,22},{8,24},{10,26},{12,28},{14,30},{16,0},... | collective-permute-start | bytes 147464 | tf_op jit(solution)/shard_map/ppermute | solution.py:847
  153.0 15.1 %collective-permute-start.21 = (bf16[8,288,128]{2,1,0:T(8,128)(2,1)S(1)}, bf16[8,288,128]{2,1,0:T(8,128)(2,1)S(1)}, u32[]{:S(2)}, u32[]{:S(2)}) collective-permute-start(bf16[8,288,128]{2,1,0:T(8,128)(2,1)S(1)} %get-tuple-element.354), channel_id=1, source_target_pairs={{0,4},{2,6},{4,0},{6,2},{8,12},{10,14},{12,8},{14,10},{16,20},{18,... | collective-permute-start | bytes 1769480 | tf_op jit(solution)/shard_map/ppermute | solution.py:847
  154.3 14.5 %collective-permute-start.22 = (bf16[8,288,128]{2,1,0:T(8,128)(2,1)S(1)}, bf16[8,288,128]{2,1,0:T(8,128)(2,1)S(1)}, u32[]{:S(2)}, u32[]{:S(2)}) collective-permute-start(bf16[8,288,128]{2,1,0:T(8,128)(2,1)S(1)} %get-tuple-element.355), channel_id=1, source_target_pairs={{0,1},{1,0},{2,3},{3,2},{4,5},{5,4},{6,7},{7,6},{8,9},{9,8},{10,11... | collective-permute-start | bytes 1769480 | tf_op jit(solution)/shard_map/ppermute | solution.py:849
  155.3 12.8 %collective-permute-start.23 = (bf16[2,528,128]{2,1,0:T(8,128)(2,1)S(1)}, bf16[2,528,128]{2,1,0:T(8,128)(2,1)S(1)}, u32[]{:S(2)}, u32[]{:S(2)}) collective-permute-start(bf16[2,528,128]{2,1,0:T(8,128)(2,1)S(1)} %get-tuple-element.356), channel_id=1, source_target_pairs={{0,8},{2,10},{4,12},{6,14},{8,0},{10,2},{12,4},{14,6},{16,24},{18,... | collective-permute-start | bytes 811016 | tf_op jit(solution)/shard_map/ppermute | solution.py:847
  157.4 10.7 %collective-permute-start.24 = (bf16[1,768,128]{2,1,0:T(8,128)(2,1)S(1)}, bf16[1,768,128]{2,1,0:T(8,128)(2,1)S(1)}, u32[]{:S(2)}, u32[]{:S(2)}) collective-permute-start(bf16[1,768,128]{2,1,0:T(8,128)(2,1)S(1)} %get-tuple-element.357), channel_id=1, source_target_pairs={{0,16},{2,18},{4,20},{6,22},{8,24},{10,26},{12,28},{14,30},{16,0},... | collective-permute-start | bytes 589832 | tf_op jit(solution)/shard_map/ppermute | solution.py:847
  157.6 1.2 collective-permute-start.25
  158.8 12.9 %copy-start.31 = (f32[8,768]{1,0:T(8,128)S(1)}, f32[8,768]{1,0:T(8,128)}, u32[]{:S(2)}) copy-start(f32[8,768]{1,0:T(8,128)} %get-tuple-element.393) | copy-start | bytes 73732
  158.8 16.8 %copy-start.29 = (f32[320,768]{1,0:T(8,128)S(1)}, f32[320,768]{1,0:T(8,128)}, u32[]{:S(2)}) copy-start(f32[320,768]{1,0:T(8,128)} %get-tuple-element.394) | copy-start | bytes 2949124
  169.9 11.6 %collective-permute-start.26 = (bf16[4,288,128]{2,1,0:T(8,128)(2,1)S(1)}, bf16[4,288,128]{2,1,0:T(8,128)(2,1)S(1)}, u32[]{:S(2)}, u32[]{:S(2)}) collective-permute-start(bf16[4,288,128]{2,1,0:T(8,128)(2,1)S(1)} %get-tuple-element.374), channel_id=1, source_target_pairs={{0,1},{1,0},{2,3},{3,2},{4,5},{5,4},{6,7},{7,6},{8,9},{9,8},{10,11... | collective-permute-start | bytes 884744 | tf_op jit(solution)/shard_map/ppermute | solution.py:849
  170.9 10.6 %collective-permute-start.27 = (bf16[4,288,128]{2,1,0:T(8,128)(2,1)S(1)}, bf16[4,288,128]{2,1,0:T(8,128)(2,1)S(1)}, u32[]{:S(2)}, u32[]{:S(2)}) collective-permute-start(bf16[4,288,128]{2,1,0:T(8,128)(2,1)S(1)} %get-tuple-element.375), channel_id=1, source_target_pairs={{0,4},{2,6},{4,0},{6,2},{8,12},{10,14},{12,8},{14,10},{16,20},{18,... | collective-permute-start | bytes 884744 | tf_op jit(solution)/shard_map/ppermute | solution.py:847
  172.9 6.1 %collective-permute-start.29 = (f32[16,768]{1,0:T(8,128)S(1)}, f32[16,768]{1,0:T(8,128)S(1)}, u32[]{:S(2)}, u32[]{:S(2)}) collective-permute-start(f32[16,768]{1,0:T(8,128)S(1)} %add.17), channel_id=1, source_target_pairs={{0,4},{2,6},{4,0},{6,2},{8,12},{10,14},{12,8},{14,10},{16,20},{18,... | collective-permute-start | bytes 147464 | tf_op jit(solution)/shard_map/ppermute | solution.py:847
  174.2 7.4 %collective-permute-start.28 = (bf16[1,528,128]{2,1,0:T(8,128)(2,1)S(1)}, bf16[1,528,128]{2,1,0:T(8,128)(2,1)S(1)}, u32[]{:S(2)}, u32[]{:S(2)}) collective-permute-start(bf16[1,528,128]{2,1,0:T(8,128)(2,1)S(1)} %get-tuple-element.376), channel_id=1, source_target_pairs={{0,16},{2,18},{4,20},{6,22},{8,24},{10,26},{12,28},{14,30},{16,0},... | collective-permute-start | bytes 405512 | tf_op jit(solution)/shard_map/ppermute | solution.py:847
  182.3 6.1 %collective-permute-start.33 = (f32[16,768]{1,0:T(8,128)S(1)}, f32[16,768]{1,0:T(8,128)S(1)}, u32[]{:S(2)}, u32[]{:S(2)}) collective-permute-start(f32[16,768]{1,0:T(8,128)S(1)} %add.18), channel_id=1, source_target_pairs={{0,1},{1,0},{2,3},{3,2},{4,5},{5,4},{6,7},{7,6},{8,9},{9,8},{10,11... | collective-permute-start | bytes 147464 | tf_op jit(solution)/shard_map/ppermute | solution.py:849
  183.4 10.4 %collective-permute-start.30 = (bf16[1,576,128]{2,1,0:T(8,128)(2,1)S(1)}, bf16[1,576,128]{2,1,0:T(8,128)(2,1)S(1)}, u32[]{:S(2)}, u32[]{:S(2)}) collective-permute-start(bf16[1,576,128]{2,1,0:T(8,128)(2,1)S(1)} %get-tuple-element.388), channel_id=1, source_target_pairs={{0,16},{2,18},{4,20},{6,22},{8,24},{10,26},{12,28},{14,30},{16,0},... | collective-permute-start | bytes 442376 | tf_op jit(solution)/shard_map/ppermute | solution.py:847
  183.5 10.2 %collective-permute-start.31 = (bf16[1,576,128]{2,1,0:T(8,128)(2,1)S(1)}, bf16[1,576,128]{2,1,0:T(8,128)(2,1)S(1)}, u32[]{:S(2)}, u32[]{:S(2)}) collective-permute-start(bf16[1,576,128]{2,1,0:T(8,128)(2,1)S(1)} %get-tuple-element.389), channel_id=1, source_target_pairs={{0,8},{2,10},{4,12},{6,14},{8,0},{10,2},{12,4},{14,6},{16,24},{18,... | collective-permute-start | bytes 442376 | tf_op jit(solution)/shard_map/ppermute | solution.py:847
  185.9 7.8 %collective-permute-start.32 = (bf16[1,576,128]{2,1,0:T(8,128)(2,1)S(1)}, bf16[1,576,128]{2,1,0:T(8,128)(2,1)S(1)}, u32[]{:S(2)}, u32[]{:S(2)}) collective-permute-start(bf16[1,576,128]{2,1,0:T(8,128)(2,1)S(1)} %get-tuple-element.390), channel_id=1, source_target_pairs={{0,24},{2,26},{4,28},{6,30},{8,16},{10,18},{12,20},{14,22},{16,8},... | collective-permute-start | bytes 442376 | tf_op jit(solution)/shard_map/ppermute | solution.py:847
  (2 other events, 1.4 us)

commit v2 on v1

--- a/solution.py
+++ b/solution.py
@@ -439,7 +439,7 @@
     return back, jnp.sum(grad * unit, axis=0, keepdims=True)
 
 
-def back_kernel(narrow, stages, qlen, n_tiles, n_held, names, jobs, *refs):
+def back_kernel(narrow, stages, qlen, n_tiles, n_held, names, jobs, job_rows, *refs):
     me_ref, sharp_ref, here_ref, there_ref, e_ref, gains_ref, qseg_ref, pseg_ref = refs[:8]
     refs = refs[8:]
     n_fetch = n_held + (4 if jobs else 0)
@@ -527,12 +527,25 @@
     if jobs:
         for i in range(21, 25):
             fetch[i].wait()
-        weight_products(jobs, (gf_s, wide_s, row_s, ga_s), lambda g: None, me_ref, keep_ref, send_ref, refs[9])
+        turned_s, keep_s, send_s, block_sem = refs[9:]
+        first_row, moves = 0, []
+        for i, (job, rows) in enumerate(zip(jobs, job_rows)):
+            weight_products(
+                [job], (gf_s, wide_s, row_s, ga_s), lambda g: None, me_ref, keep_s, send_s, turned_s
+            )
+            span = pl.ds(first_row, rows)
+            for j, (a, b) in enumerate(((send_s, send_ref), (keep_s, keep_ref))):
+                move = pltpu.make_async_copy(a.at[:, span], b.at[:, span], block_sem.at[2 * i + j])
+                move.start()
+                moves.append(move)
+            first_row += rows
+        for move in moves:
+            move.wait()
     for name in names:
         write(name).wait()
 
 
-def loss_and_back(me, narrow, stages, sharp, here, there, e, gains, qseg, pseg, x_last, x_in, first, second, matrices, wide, jobs, total_rows):
+def loss_and_back(me, narrow, stages, sharp, here, there, e, gains, qseg, pseg, x_last, x_in, first, second, matrices, wide, jobs, job_rows):
     wq, wk, wv, wo, wg, wu, wd, wp = matrices
     total, feat = x_last.shape
     qlen, plen = qseg.shape[1], pseg.shape[1]
@@ -550,8 +563,9 @@
     blocks, late = [], []
     if jobs:
         fetched += [first["u"], second["u"], first["normed"], second["normed"]]
-        blocks = [((wide * narrow // 2, total_rows, 128), BF)] * 2
-        late = [pltpu.VMEM((384, 2 * total), BF)]
+        blocks = [((wide * narrow // 2, sum(job_rows), 128), BF)] * 2
+        late = [pltpu.VMEM((384, 2 * total), BF)] + [pltpu.VMEM(*b) for b in blocks]
+        late.append(pltpu.SemaphoreType.DMA((4,)))
         widths = (feat, hidden, feat, hidden)
         jobs = with_blocks(jobs, lambda g: widths[g], wide, narrow)
     small = [((1, feat), F32), ((1, 128), F32), ((PACK, feat), BF), ((1, feat), F32), ((1, feat), F32)]
@@ -559,10 +573,10 @@
     smem = pl.BlockSpec(memory_space=pltpu.SMEM)
     weights = sum(m.size for m in matrices)
     outs = pl.pallas_call(
-        functools.partial(back_kernel, narrow, stages, qlen, 4, n_held, names, jobs),
+        functools.partial(back_kernel, narrow, stages, qlen, 4, n_held, names, jobs, job_rows),
         out_shape=tuple(jax.ShapeDtypeStruct(*s) for s in small + [kinds[n] for n in names] + blocks),
         in_specs=[smem, smem] + [whole()] * 6 + [anywhere] * len(fetched),
-        out_specs=(whole(),) * 5 + (anywhere,) * len(names) + (whole(),) * len(blocks),
+        out_specs=(whole(),) * 5 + (anywhere,) * len(names) + (anywhere,) * len(blocks),
         scratch_shapes=held
         + [pltpu.VMEM(*kinds[n]) for n in BACK if n not in PAIRED and n != "grad_x"]
         + [
@@ -1054,7 +1068,7 @@
     here, there = gather_all(packed, groups)
     (gain_final, loss_part, grad_e, gain_mid, gain_in), back, parts = loss_and_back(
         me, narrow, stages, softness, here, there, e, gains, query_seg, passage_seg,
-        x_last, x_between, first, second, matrices, wide, jobs, down_rows + cols,
+        x_last, x_between, first, second, matrices, wide, jobs, (down_rows, cols),
     )
     grad_b, grad_b_2 = back["gb1"], back["gb"]
     att_2 = (back["gy"], back["gq"], back["gk"], back["gv"])
@@ -1102,13 +1116,13 @@
                 [normed, normed_2, grad_b, grad_b_2, grad_e, pooled],
                 [(0, 1), (2, 3), (4,), (5,)],
                 [
+                    (2, 3, "wide", [(order_b, 0, block, cols)]),
                     (0, 1, "narrow", [(order_a, 0, cut, 0), (order_b, cut, cols - cut, cut)]),
-                    (2, 3, "wide", [(order_b, 0, block, cols)]),
                 ],
                 cols + att_rows,
                 wide,
                 narrow,
-                48,
+                52,
             )
 
         parts = exchange([ffn], make_up, (grad_b, grad_b_2))

time: 197 us -> 194 us (0.985)
  local copies, waits for them, and re-layouts: 9.38 us -> 6.76 us
    unnamed x64 -> x62, local copies, waits for them, and re-layouts: 4.84 us -> 2.22 us
  transfers between devices with their start and end apart: 34 -> 34, of which waited for: 18 -> 16; matrix products, arithmetic and copies ran while one was open for 3% -> 3% of each run, Pallas kernels for 19% -> 20%
where the time goes in v2:
time: 194 us
  Pallas kernels  104 us (54%)
  waiting for transfers between devices  43.4 us (22%)
  starting transfers between devices  35.7 us (18%)
  local copies, waits for them, and re-layouts  6.76 us (3%)
  between operations  3.58 us (2%)
    ppermute x25, waiting for transfers between devices, swap(): return lax.ppermute(a, 'wide', [(i, i ^ dw) for i in range(wide)])  31.7 us
    pallas_call x1, Pallas kernels, loss_and_back(): pl.pallas_call(functools.partial(back_kernel, narrow, stages, qlen, 4, n_...  30.1 us
    pallas_call x1, Pallas kernels, forward(): pl.pallas_call(functools.partial(forward_kernel, qlen, plen, 4), out_shap...  29.8 us
    ppermute x25, starting transfers between devices, swap(): return lax.ppermute(a, 'wide', [(i, i ^ dw) for i in range(wide)])  25.1 us
    pallas_call x2, Pallas kernels, wgrad(): pl.pallas_call(functools.partial(wgrad_kernel, full, groups, len(ops)), o...  20.1 us
    pallas_call x1, Pallas kernels, rest_back(): pl.pallas_call(functools.partial(rest_kernel, qlen, buckets, len(fetched)...  17.8 us
    ppermute x8, waiting for transfers between devices, swap(): return lax.ppermute(a, 'narrow', [(i, i ^ dn) for i in range(narrow)])  9.81 us
    ppermute x8, starting transfers between devices, swap(): return lax.ppermute(a, 'narrow', [(i, i ^ dn) for i in range(narrow)])  8.18 us
  transfers between devices with their start and end apart: 34, of which 16 were waited for; matrix products, arithmetic and copies ran while one was open for 3% of the time, Pallas kernels for 20%

profile of v2, /device:TPU:0, one launch (start us, length us, event | category | flops | bytes accessed | tf_op | source)
XLA Modules:
  0.0 193.9 jit_solution(17220302203287707413)
XLA Ops:
  0.6 29.8 %forward.1 = (bf16[8,768]{1,0:T(8,128)(2,1)}, f32[8,768]{1,0:T(8,128)}, f32[8,768]{1,0:T(8,128)}, bf16[8,768]{1,0:T(8,128)(2,1)}, f32[320,768]{1,0:T(8,128)}, /*...) custom-call(bf16[64,768]{1,0:T(8,128)(2,1)} %bitcast.20, ...), custom_call_target="tpu_custom_call" | custom-call | flops 9814671360 | bytes 15335424 | tf_op jit(solution)/shard_map/forward/pallas_call | solution.py:332
  30.4 5.2 %collective-permute-start.2 = (bf16[8,768]{1,0:T(8,128)(2,1)}, bf16[8,768]{1,0:T(8,128)(2,1)S(1)}, u32[]{:S(2)}, u32[]{:S(2)}) collective-permute-start(bf16[8,768]{1,0:T(8,128)(2,1)} %get-tuple-element.212.refs_0_), channel_id=1, source_target_pairs={{0,24},{2,26},{4,28},{6,30},{8,16},{10,18},{12,20},{14,22},{16,8},... | collective-permute-start | bytes 36872 | tf_op jit(solution)/shard_map/ppermute | solution.py:861
  35.6 0.6 collective-permute-start
  36.2 1.2 collective-permute-done.2.refs_3_
  37.5 2.9 %collective-permute-done.1.refs_2_ = bf16[8,768]{1,0:T(8,128)(2,1)S(1)} collective-permute-done((bf16[8,768]{1,0:T(8,128)(2,1)}, bf16[8,768]{1,0:T(8,128)(2,1)S(1)}, u32[]{:S(2)}, u32[]{:S(2)}) %collective-permute-start.1) | collective-permute-done | bytes 12320 | tf_op jit(solution)/shard_map/ppermute | solution.py:861
  40.4 0.7 copy-done.13
  41.1 2.4 %collective-permute-start.5 = (bf16[32,768]{1,0:T(8,128)(2,1)S(1)}, bf16[32,768]{1,0:T(8,128)(2,1)S(1)}, u32[]{:S(2)}, u32[]{:S(2)}) collective-permute-start(bf16[32,768]{1,0:T(8,128)(2,1)S(1)} %join.2.refs_0_), channel_id=1, source_target_pairs={{0,5},{1,4},{2,7},{3,6},{4,1},{5,0},{6,3},{7,2},{8,13},{9,12},{10,... | collective-permute-start | bytes 147464 | tf_op jit(solution)/shard_map/ppermute | solution.py:865
  43.6 0.5 collective-permute-start.4
  44.1 0.5 collective-permute-start.3
  44.6 1.9 collective-permute-done.5.refs_3_
  46.5 1.1 collective-permute-done.4.refs_2_
  47.6 0.5 collective-permute-done.3.refs_1_
  48.9 0.6 pad_add_fusion.refs_0_.me_ref
  49.7 0.7 copy-done.29
  50.4 30.1 %loss_and_back.1 = (f32[1,768]{1,0:T(1,128)}, f32[1,128]{1,0:T(1,128)}, bf16[8,768]{1,0:T(8,128)(2,1)}, f32[1,768]{1,0:T(1,128)}, f32[1,768]{1,0:T(1,128)}, /*in...) custom-call(s32[2]{0:T(128)} %pad_add_fusion.refs_0_.me_ref, ...), custom_call_target="tpu_custom_call" | custom-call | flops 7361003520 | bytes 15335424 | tf_op jit(solution)/shard_map/loss_and_back/pallas_call | solution.py:575
  80.5 0.4 collective-permute-start.7
  80.9 0.7 copy-done.24
  81.6 9.5 %wgrad.2 = (bf16[16,528,128]{2,1,0:T(8,128)(2,1)}, bf16[16,528,128]{2,1,0:T(8,128)(2,1)}) custom-call(s32[2]{0:T(128)S(1)} %copy-done.19, bf16[320,768]{1,0:T(8,128)(2,1)S(1)} %copy-done.7, bf16[320,768]{1,0:T(8,128)(2,1)S(1)} %copy-done.8, bf16[320,2048]{1,0:T(8,128)(2,1)} %get-tuple-element.260.refs_2_.refs_8_, ...), custom_call_target="tpu_custom_call" | custom-call | flops 2022703104 | bytes 7901184 | tf_op jit(solution)/shard_map/wgrad/pallas_call | solution.py:842
  91.2 0.9 advance.7
  92.1 0.3 collective-permute-start.10
  92.4 0.5 collective-permute-start.8
  92.9 1.5 collective-permute-start.9
  94.5 17.8 %rest_back.1 = (f32[16,768]{1,0:T(8,128)S(1)}, bf16[320,768]{1,0:T(8,128)(2,1)S(1)}, bf16[320,768]{1,0:T(8,128)(2,1)S(1)}, bf16[320,768]{1,0:T(8,128)(2,1)S(1)},...) custom-call(f32[3,768]{1,0:T(4,128)S(1)} %copy-done.12, s32[1,511]{1,0:T(1,128)S(1)} %bitcast.23, ...), custom_call_target="tpu_custom_call" | custom-call | flops 5284823040 | bytes 11010048 | tf_op jit(solution)/shard_map/rest_back/pallas_call | solution.py:672
  112.5 1.1 advance.8
  113.6 1.6 collective-permute-start.14
  115.2 1.5 collective-permute-start.13
  116.6 0.5 collective-permute-start.11
  117.2 0.5 collective-permute-start.12
  117.8 10.6 %wgrad.3 = (bf16[16,576,128]{2,1,0:T(8,128)(2,1)S(1)}, bf16[16,576,128]{2,1,0:T(8,128)(2,1)S(1)}) custom-call(s32[2]{0:T(128)S(1)} %copy-done.19, bf16[320,768]{1,0:T(8,128)(2,1)S(1)} %get-tuple-element.299.refs_0_, bf16[320,768]{1,0:T(8,128)(2,1)S(1)} %copy-done.20, bf16[320,768]{1,0:T(8,128)(2,1)S(1)} %copy-done.3, bf16[320,768]{1,0:T(8,128)(2,1)S(1)} %copy-done.4, ...), custom_call_target="tpu_custom_call" | custom-call | flops 3019898880 | bytes 11796480 | tf_op jit(solution)/shard_map/wgrad/pallas_call | solution.py:842
  128.4 7.9 %collective-permute-done.11.refs_1_ = bf16[4,384,128]{2,1,0:T(8,128)(2,1)S(1)} collective-permute-done((bf16[4,384,128]{2,1,0:T(8,128)(2,1)S(1)}, bf16[4,384,128]{2,1,0:T(8,128)(2,1)S(1)}, u32[]{:S(2)}, u32[]{:S(2)}) %collective-permute-start.11) | collective-permute-done | bytes 393248 | tf_op jit(solution)/shard_map/ppermute | solution.py:863
  136.3 0.5 advance.9
  137.0 1.5 collective-permute-start.18
  138.6 1.0 collective-permute-start.17
  139.6 2.0 %collective-permute-start.20 = (f32[16,768]{1,0:T(8,128)S(1)}, f32[16,768]{1,0:T(8,128)S(1)}, u32[]{:S(2)}, u32[]{:S(2)}) collective-permute-start(f32[16,768]{1,0:T(8,128)S(1)} %add.15), channel_id=1, source_target_pairs={{0,16},{2,18},{4,20},{6,22},{8,24},{10,26},{12,28},{14,30},{16,0},... | collective-permute-start | bytes 147464 | tf_op jit(solution)/shard_map/ppermute | solution.py:861
  141.6 5.7 %collective-permute-done.20 = f32[16,768]{1,0:T(8,128)S(1)} collective-permute-done((f32[16,768]{1,0:T(8,128)S(1)}, f32[16,768]{1,0:T(8,128)S(1)}, u32[]{:S(2)}, u32[]{:S(2)}) %collective-permute-start.20) | collective-permute-done | bytes 49184 | tf_op jit(solution)/shard_map/ppermute | solution.py:861
  147.4 2.2 %collective-permute-done.19.refs_7_ = bf16[2,768,128]{2,1,0:T(8,128)(2,1)S(1)} collective-permute-done((bf16[2,768,128]{2,1,0:T(8,128)(2,1)S(1)}, bf16[2,768,128]{2,1,0:T(8,128)(2,1)S(1)}, u32[]{:S(2)}, u32[]{:S(2)}) %collective-permute-start.19) | collective-permute-done | bytes 393248 | tf_op jit(solution)/shard_map/ppermute | solution.py:861
  149.5 0.9 advance.10
  150.5 1.5 collective-permute-start.21
  152.0 1.0 collective-permute-start.22
  153.0 2.1 %collective-permute-start.23 = (bf16[2,528,128]{2,1,0:T(8,128)(2,1)S(1)}, bf16[2,528,128]{2,1,0:T(8,128)(2,1)S(1)}, u32[]{:S(2)}, u32[]{:S(2)}) collective-permute-start(bf16[2,528,128]{2,1,0:T(8,128)(2,1)S(1)} %get-tuple-element.356), channel_id=1, source_target_pairs={{0,8},{2,10},{4,12},{6,14},{8,0},{10,2},{12,4},{14,6},{16,24},{18,... | collective-permute-start | bytes 811016 | tf_op jit(solution)/shard_map/ppermute | solution.py:861
  155.1 0.2 collective-permute-start.24
  155.4 1.2 collective-permute-done.25
  156.6 9.2 %collective-permute-done.24.refs_7_ = bf16[1,768,128]{2,1,0:T(8,128)(2,1)S(1)} collective-permute-done((bf16[1,768,128]{2,1,0:T(8,128)(2,1)S(1)}, bf16[1,768,128]{2,1,0:T(8,128)(2,1)S(1)}, u32[]{:S(2)}, u32[]{:S(2)}) %collective-permute-start.24) | collective-permute-done | bytes 196640 | tf_op jit(solution)/shard_map/ppermute | solution.py:861
  165.8 0.7 collective-permute-done.22.refs_3_
  166.5 1.1 advance.11
  167.7 1.0 collective-permute-start.26
  168.7 0.5 collective-permute-start.27
  169.2 0.6 slice.25
  169.8 0.6 slice.24
  170.4 1.5 collective-permute-start.29
  171.9 1.5 collective-permute-start.28
  173.4 0.9 slice_bitcast_fusion
  174.4 2.4 %collective-permute-done.29 = f32[16,768]{1,0:T(8,128)S(1)} collective-permute-done((f32[16,768]{1,0:T(8,128)S(1)}, f32[16,768]{1,0:T(8,128)S(1)}, u32[]{:S(2)}, u32[]{:S(2)}) %collective-permute-start.29) | collective-permute-done | bytes 49184 | tf_op jit(solution)/shard_map/ppermute | solution.py:861
  176.8 2.5 %collective-permute-done.28.refs_5_ = bf16[1,528,128]{2,1,0:T(8,128)(2,1)S(1)} collective-permute-done((bf16[1,528,128]{2,1,0:T(8,128)(2,1)S(1)}, bf16[1,528,128]{2,1,0:T(8,128)(2,1)S(1)}, u32[]{:S(2)}, u32[]{:S(2)}) %collective-permute-start.28) | collective-permute-done | bytes 135200 | tf_op jit(solution)/shard_map/ppermute | solution.py:861
  179.3 0.8 advance.12
  180.1 1.0 collective-permute-start.33
  181.2 2.4 %collective-permute-start.31 = (bf16[1,576,128]{2,1,0:T(8,128)(2,1)S(1)}, bf16[1,576,128]{2,1,0:T(8,128)(2,1)S(1)}, u32[]{:S(2)}, u32[]{:S(2)}) collective-permute-start(bf16[1,576,128]{2,1,0:T(8,128)(2,1)S(1)} %get-tuple-element.389), channel_id=1, source_target_pairs={{0,8},{2,10},{4,12},{6,14},{8,0},{10,2},{12,4},{14,6},{16,24},{18,... | collective-permute-start | bytes 442376 | tf_op jit(solution)/shard_map/ppermute | solution.py:861
  183.6 1.8 collective-permute-start.32
  185.5 0.7 slice_bitcast_fusion.1
  186.2 0.5 slice.30
  186.7 0.6 slice.29
  187.3 0.6 slice.28
  187.9 3.5 %collective-permute-done.30.refs_1_ = bf16[1,576,128]{2,1,0:T(8,128)(2,1)S(1)} collective-permute-done((bf16[1,576,128]{2,1,0:T(8,128)(2,1)S(1)}, bf16[1,576,128]{2,1,0:T(8,128)(2,1)S(1)}, u32[]{:S(2)}, u32[]{:S(2)}) %collective-permute-start.30) | collective-permute-done | bytes 147488 | tf_op jit(solution)/shard_map/ppermute | solution.py:861
  192.1 0.7 advance.13
  (93 shorter events, 0.9 us)
Async XLA Ops:
  30.4 7.0 %collective-permute-start.2 = (bf16[8,768]{1,0:T(8,128)(2,1)}, bf16[8,768]{1,0:T(8,128)(2,1)S(1)}, u32[]{:S(2)}, u32[]{:S(2)}) collective-permute-start(bf16[8,768]{1,0:T(8,128)(2,1)} %get-tuple-element.212.refs_0_), channel_id=1, source_target_pairs={{0,24},{2,26},{4,28},{6,30},{8,16},{10,18},{12,20},{14,22},{16,8},... | collective-permute-start | bytes 36872 | tf_op jit(solution)/shard_map/ppermute | solution.py:861
  35.6 4.8 %collective-permute-start.1 = (bf16[8,768]{1,0:T(8,128)(2,1)}, bf16[8,768]{1,0:T(8,128)(2,1)S(1)}, u32[]{:S(2)}, u32[]{:S(2)}) collective-permute-start(bf16[8,768]{1,0:T(8,128)(2,1)} %get-tuple-element.212.refs_0_), channel_id=1, source_target_pairs={{0,16},{2,18},{4,20},{6,22},{8,24},{10,26},{12,28},{14,30},{16,0},... | collective-permute-start | bytes 36872 | tf_op jit(solution)/shard_map/ppermute | solution.py:861
  35.6 4.8 %collective-permute-start = (bf16[8,768]{1,0:T(8,128)(2,1)}, bf16[8,768]{1,0:T(8,128)(2,1)S(1)}, u32[]{:S(2)}, u32[]{:S(2)}) collective-permute-start(bf16[8,768]{1,0:T(8,128)(2,1)} %get-tuple-element.212.refs_0_), channel_id=1, source_target_pairs={{0,8},{2,10},{4,12},{6,14},{8,0},{10,2},{12,4},{14,6},{16,24},{18,... | collective-permute-start | bytes 36872 | tf_op jit(solution)/shard_map/ppermute | solution.py:861
  40.4 0.7 copy-start.13
  41.1 5.4 %collective-permute-start.5 = (bf16[32,768]{1,0:T(8,128)(2,1)S(1)}, bf16[32,768]{1,0:T(8,128)(2,1)S(1)}, u32[]{:S(2)}, u32[]{:S(2)}) collective-permute-start(bf16[32,768]{1,0:T(8,128)(2,1)S(1)} %join.2.refs_0_), channel_id=1, source_target_pairs={{0,5},{1,4},{2,7},{3,6},{4,1},{5,0},{6,3},{7,2},{8,13},{9,12},{10,... | collective-permute-start | bytes 147464 | tf_op jit(solution)/shard_map/ppermute | solution.py:865
  43.6 4.1 %collective-permute-start.4 = (bf16[32,768]{1,0:T(8,128)(2,1)S(1)}, bf16[32,768]{1,0:T(8,128)(2,1)S(1)}, u32[]{:S(2)}, u32[]{:S(2)}) collective-permute-start(bf16[32,768]{1,0:T(8,128)(2,1)S(1)} %join.2.refs_0_), channel_id=1, source_target_pairs={{0,1},{1,0},{2,3},{3,2},{4,5},{5,4},{6,7},{7,6},{8,9},{9,8},{10,11... | collective-permute-start | bytes 147464 | tf_op jit(solution)/shard_map/ppermute | solution.py:863
  44.1 4.1 %collective-permute-start.3 = (bf16[32,768]{1,0:T(8,128)(2,1)S(1)}, bf16[32,768]{1,0:T(8,128)(2,1)S(1)}, u32[]{:S(2)}, u32[]{:S(2)}) collective-permute-start(bf16[32,768]{1,0:T(8,128)(2,1)S(1)} %join.2.refs_0_), channel_id=1, source_target_pairs={{0,4},{2,6},{4,0},{6,2},{8,12},{10,14},{12,8},{14,10},{16,20},{18,... | collective-permute-start | bytes 147464 | tf_op jit(solution)/shard_map/ppermute | solution.py:861
  48.2 1.5 copy-start.2
  48.2 1.5 collective-permute-start.6
  50.4 30.5 %copy-start.7 = (bf16[320,768]{1,0:T(8,128)(2,1)S(1)}, bf16[320,768]{1,0:T(8,128)(2,1)}, u32[]{:S(2)}) copy-start(bf16[320,768]{1,0:T(8,128)(2,1)} %get-tuple-element.229.refs_31_.refs_0_) | copy-start | bytes 1474564
  50.4 30.5 %copy-start.8 = (bf16[320,768]{1,0:T(8,128)(2,1)S(1)}, bf16[320,768]{1,0:T(8,128)(2,1)}, u32[]{:S(2)}) copy-start(bf16[320,768]{1,0:T(8,128)(2,1)} %get-tuple-element.230.refs_32_.refs_1_) | copy-start | bytes 1474564
  50.4 30.5 %copy-start.19 = (s32[2]{0:T(128)S(1)}, s32[2]{0:T(128)}, u32[]{:S(2)}) copy-start(s32[2]{0:T(128)} %pad_add_fusion.refs_0_.me_ref) | copy-start | bytes 28
  50.4 30.5 %copy-start.27 = (bf16[8,768]{1,0:T(8,128)(2,1)S(1)}, bf16[8,768]{1,0:T(8,128)(2,1)}, u32[]{:S(2)}) copy-start(bf16[8,768]{1,0:T(8,128)(2,1)} %get-tuple-element.240.refs_5_) | copy-start | bytes 36868
  80.5 10.6 %collective-permute-start.7 = (bf16[16,768,128]{2,1,0:T(8,128)(2,1)}, bf16[16,768,128]{2,1,0:T(8,128)(2,1)S(1)}, u32[]{:S(2)}, u32[]{:S(2)}) collective-permute-start(bf16[16,768,128]{2,1,0:T(8,128)(2,1)} %get-tuple-element.236), channel_id=1, source_target_pairs={{0,2},{2,0},{4,6},{6,4},{8,10},{10,8},{12,14},{14,12},{16,18},{18,... | collective-permute-start | bytes 9437192 | tf_op jit(solution)/shard_map/ppermute | solution.py:861
  80.9 0.7 copy-start.24
  81.6 9.5 %copy-start = (bf16[16,768,128]{2,1,0:T(8,128)(2,1)S(1)}, bf16[16,768,128]{2,1,0:T(8,128)(2,1)}, u32[]{:S(2)}) copy-start(bf16[16,768,128]{2,1,0:T(8,128)(2,1)} %get-tuple-element.235.refs_0_) | copy-start | bytes 9437188
  91.1 3.3 %copy-start.5 = (bf16[320,768]{1,0:T(8,128)(2,1)S(1)}, bf16[320,768]{1,0:T(8,128)(2,1)}, u32[]{:S(2)}) copy-start(bf16[320,768]{1,0:T(8,128)(2,1)} %get-tuple-element.263.refs_13_) | copy-start | bytes 1474564
  91.1 3.3 %copy-start.6 = (bf16[320,768]{1,0:T(8,128)(2,1)S(1)}, bf16[320,768]{1,0:T(8,128)(2,1)}, u32[]{:S(2)}) copy-start(bf16[320,768]{1,0:T(8,128)(2,1)} %get-tuple-element.264.refs_14_) | copy-start | bytes 1474564
  91.1 3.3 %copy-start.9 = (bf16[1,256,768]{2,1,0:T(8,128)(2,1)S(1)}, bf16[1,256,768]{2,1,0:T(8,128)(2,1)}, u32[]{:S(2)}) copy-start(bf16[1,256,768]{2,1,0:T(8,128)(2,1)} %param.19) | copy-start | bytes 1179652
  91.1 3.3 %copy-start.10 = (bf16[12,64,64]{2,1,0:T(8,128)(2,1)S(1)}, bf16[12,64,64]{2,1,0:T(8,128)(2,1)}, u32[]{:S(2)}) copy-start(bf16[12,64,64]{2,1,0:T(8,128)(2,1)} %get-tuple-element.268.refs_18_) | copy-start | bytes 294916
  91.1 3.3 %copy-start.11 = (bf16[1,64,768]{2,1,0:T(8,128)(2,1)S(1)}, bf16[1,64,768]{2,1,0:T(8,128)(2,1)}, u32[]{:S(2)}) copy-start(bf16[1,64,768]{2,1,0:T(8,128)(2,1)} %param.17) | copy-start | bytes 294916
  91.2 3.3 %copy-start.12 = (f32[3,768]{1,0:T(4,128)S(1)}, f32[3,768]{1,0:T(4,128)}, u32[]{:S(2)}) copy-start(f32[3,768]{1,0:T(4,128)} %refs_0_.1) | copy-start | bytes 27652
  91.2 3.3 %copy-start.14 = (f32[1,768]{1,0:T(1,128)S(1)}, f32[1,768]{1,0:T(1,128)}, u32[]{:S(2)}) copy-start(f32[1,768]{1,0:T(1,128)} %get-tuple-element.257.refs_4_) | copy-start | bytes 9220
  91.2 3.3 %copy-start.15 = (f32[1,768]{1,0:T(1,128)S(1)}, f32[1,768]{1,0:T(1,128)}, u32[]{:S(2)}) copy-start(f32[1,768]{1,0:T(1,128)} %get-tuple-element.256.refs_3_) | copy-start | bytes 9220
  91.2 3.3 %copy-start.16 = (f32[1,768]{1,0:T(1,128)S(1)}, f32[1,768]{1,0:T(1,128)}, u32[]{:S(2)}) copy-start(f32[1,768]{1,0:T(1,128)} %get-tuple-element.255.refs_2_) | copy-start | bytes 9220
  91.2 3.3 %copy-start.17 = (s32[511]{0:T(512)S(1)}, s32[511]{0:T(512)}, u32[]{:S(2)}) copy-start(s32[511]{0:T(512)} %param.22) | copy-start | bytes 6136
  91.2 3.3 %copy-start.18 = (f32[1,128]{1,0:T(1,128)S(1)}, f32[1,128]{1,0:T(1,128)}, u32[]{:S(2)}) copy-start(f32[1,128]{1,0:T(1,128)} %get-tuple-element.258.refs_5_) | copy-start | bytes 1540
  92.1 20.3 %collective-permute-start.10 = (bf16[16,528,128]{2,1,0:T(8,128)(2,1)}, bf16[16,528,128]{2,1,0:T(8,128)(2,1)S(1)}, u32[]{:S(2)}, u32[]{:S(2)}) collective-permute-start(bf16[16,528,128]{2,1,0:T(8,128)(2,1)} %get-tuple-element.254), channel_id=1, source_target_pairs={{0,2},{2,0},{4,6},{6,4},{8,10},{10,8},{12,14},{14,12},{16,18},{18,... | collective-permute-start | bytes 6488072 | tf_op jit(solution)/shard_map/ppermute | solution.py:861
  92.4 19.9 %collective-permute-start.8 = (bf16[8,384,128]{2,1,0:T(8,128)(2,1)S(1)}, bf16[8,384,128]{2,1,0:T(8,128)(2,1)S(1)}, u32[]{:S(2)}, u32[]{:S(2)}) collective-permute-start(bf16[8,384,128]{2,1,0:T(8,128)(2,1)S(1)} %get-tuple-element.252), channel_id=1, source_target_pairs={{0,4},{2,6},{4,0},{6,2},{8,12},{10,14},{12,8},{14,10},{16,20},{18,... | collective-permute-start | bytes 2359304 | tf_op jit(solution)/shard_map/ppermute | solution.py:861
  92.9 19.5 %collective-permute-start.9 = (bf16[8,384,128]{2,1,0:T(8,128)(2,1)S(1)}, bf16[8,384,128]{2,1,0:T(8,128)(2,1)S(1)}, u32[]{:S(2)}, u32[]{:S(2)}) collective-permute-start(bf16[8,384,128]{2,1,0:T(8,128)(2,1)S(1)} %get-tuple-element.253), channel_id=1, source_target_pairs={{0,1},{1,0},{2,3},{3,2},{4,5},{5,4},{6,7},{7,6},{8,9},{9,8},{10,11... | collective-permute-start | bytes 2359304 | tf_op jit(solution)/shard_map/ppermute | solution.py:863
  94.5 17.9 %copy-start.1 = (bf16[16,528,128]{2,1,0:T(8,128)(2,1)S(1)}, bf16[16,528,128]{2,1,0:T(8,128)(2,1)}, u32[]{:S(2)}) copy-start(bf16[16,528,128]{2,1,0:T(8,128)(2,1)} %get-tuple-element.279.refs_4_) | copy-start | bytes 6488068
  112.4 5.3 %copy-start.3 = (bf16[320,768]{1,0:T(8,128)(2,1)S(1)}, bf16[320,768]{1,0:T(8,128)(2,1)}, u32[]{:S(2)}) copy-start(bf16[320,768]{1,0:T(8,128)(2,1)} %get-tuple-element.266.refs_16_.refs_2_) | copy-start | bytes 1474564
  112.4 5.3 %copy-start.4 = (bf16[320,768]{1,0:T(8,128)(2,1)S(1)}, bf16[320,768]{1,0:T(8,128)(2,1)}, u32[]{:S(2)}) copy-start(bf16[320,768]{1,0:T(8,128)(2,1)} %get-tuple-element.219.refs_18_.refs_3_) | copy-start | bytes 1474564
  112.4 5.3 %copy-start.20 = (bf16[320,768]{1,0:T(8,128)(2,1)S(1)}, bf16[320,768]{1,0:T(8,128)(2,1)}, u32[]{:S(2)}) copy-start(bf16[320,768]{1,0:T(8,128)(2,1)} %get-tuple-element.300.refs_1_) | copy-start | bytes 1474564
  112.4 5.3 %copy-start.21 = (bf16[320,768]{1,0:T(8,128)(2,1)S(1)}, bf16[320,768]{1,0:T(8,128)(2,1)}, u32[]{:S(2)}) copy-start(bf16[320,768]{1,0:T(8,128)(2,1)} %get-tuple-element.302.refs_5_) | copy-start | bytes 1474564
  112.4 5.3 %copy-start.22 = (bf16[320,768]{1,0:T(8,128)(2,1)S(1)}, bf16[320,768]{1,0:T(8,128)(2,1)}, u32[]{:S(2)}) copy-start(bf16[320,768]{1,0:T(8,128)(2,1)} %get-tuple-element.306.refs_9_) | copy-start | bytes 1474564
  112.5 5.3 %copy-start.23 = (bf16[320,768]{1,0:T(8,128)(2,1)S(1)}, bf16[320,768]{1,0:T(8,128)(2,1)}, u32[]{:S(2)}) copy-start(bf16[320,768]{1,0:T(8,128)(2,1)} %get-tuple-element.308.refs_11_) | copy-start | bytes 1474564
  112.5 5.3 %copy-start.25 = (bf16[320,768]{1,0:T(8,128)(2,1)S(1)}, bf16[320,768]{1,0:T(8,128)(2,1)}, u32[]{:S(2)}) copy-start(bf16[320,768]{1,0:T(8,128)(2,1)} %get-tuple-element.303.refs_6_) | copy-start | bytes 1474564
  112.5 5.3 %copy-start.26 = (bf16[320,768]{1,0:T(8,128)(2,1)S(1)}, bf16[320,768]{1,0:T(8,128)(2,1)}, u32[]{:S(2)}) copy-start(bf16[320,768]{1,0:T(8,128)(2,1)} %get-tuple-element.304.refs_7_) | copy-start | bytes 1474564
  113.6 22.8 %collective-permute-start.14 = (bf16[8,272,128]{2,1,0:T(8,128)(2,1)S(1)}, bf16[8,272,128]{2,1,0:T(8,128)(2,1)S(1)}, u32[]{:S(2)}, u32[]{:S(2)}) collective-permute-start(bf16[8,272,128]{2,1,0:T(8,128)(2,1)S(1)} %get-tuple-element.297), channel_id=1, source_target_pairs={{0,1},{1,0},{2,3},{3,2},{4,5},{5,4},{6,7},{7,6},{8,9},{9,8},{10,11... | collective-permute-start | bytes 1671176 | tf_op jit(solution)/shard_map/ppermute | solution.py:863
  115.2 21.2 %collective-permute-start.13 = (bf16[8,256,128]{2,1,0:T(8,128)(2,1)S(1)}, bf16[8,256,128]{2,1,0:T(8,128)(2,1)S(1)}, u32[]{:S(2)}, u32[]{:S(2)}) collective-permute-start(bf16[8,256,128]{2,1,0:T(8,128)(2,1)S(1)} %get-tuple-element.296), channel_id=1, source_target_pairs={{0,4},{2,6},{4,0},{6,2},{8,12},{10,14},{12,8},{14,10},{16,20},{18,... | collective-permute-start | bytes 1572872 | tf_op jit(solution)/shard_map/ppermute | solution.py:861
  116.6 19.7 %collective-permute-start.11 = (bf16[4,384,128]{2,1,0:T(8,128)(2,1)S(1)}, bf16[4,384,128]{2,1,0:T(8,128)(2,1)S(1)}, u32[]{:S(2)}, u32[]{:S(2)}) collective-permute-start(bf16[4,384,128]{2,1,0:T(8,128)(2,1)S(1)} %get-tuple-element.294), channel_id=1, source_target_pairs={{0,1},{1,0},{2,3},{3,2},{4,5},{5,4},{6,7},{7,6},{8,9},{9,8},{10,11... | collective-permute-start | bytes 1179656 | tf_op jit(solution)/shard_map/ppermute | solution.py:863
  117.2 19.2 %collective-permute-start.12 = (bf16[4,384,128]{2,1,0:T(8,128)(2,1)S(1)}, bf16[4,384,128]{2,1,0:T(8,128)(2,1)S(1)}, u32[]{:S(2)}, u32[]{:S(2)}) collective-permute-start(bf16[4,384,128]{2,1,0:T(8,128)(2,1)S(1)} %get-tuple-element.295), channel_id=1, source_target_pairs={{0,4},{2,6},{4,0},{6,2},{8,12},{10,14},{12,8},{14,10},{16,20},{18,... | collective-permute-start | bytes 1179656 | tf_op jit(solution)/shard_map/ppermute | solution.py:861
  117.7 10.7 %collective-permute-start.15 = (f32[16,768]{1,0:T(8,128)S(1)}, f32[16,768]{1,0:T(8,128)S(1)}, u32[]{:S(2)}, u32[]{:S(2)}) collective-permute-start(f32[16,768]{1,0:T(8,128)S(1)} %get-tuple-element.298), channel_id=1, source_target_pairs={{0,8},{2,10},{4,12},{6,14},{8,0},{10,2},{12,4},{14,6},{16,24},{18,... | collective-permute-start | bytes 147464 | tf_op jit(solution)/shard_map/ppermute | solution.py:861
  136.9 12.7 %collective-permute-start.16 = (bf16[16,576,128]{2,1,0:T(8,128)(2,1)S(1)}, bf16[16,576,128]{2,1,0:T(8,128)(2,1)S(1)}, u32[]{:S(2)}, u32[]{:S(2)}) collective-permute-start(bf16[16,576,128]{2,1,0:T(8,128)(2,1)S(1)} %get-tuple-element.332), channel_id=1, source_target_pairs={{0,2},{2,0},{4,6},{6,4},{8,10},{10,8},{12,14},{14,12},{16,18},{18,... | collective-permute-start | bytes 7077896 | tf_op jit(solution)/shard_map/ppermute | solution.py:861
  137.0 12.6 %collective-permute-start.19 = (bf16[2,768,128]{2,1,0:T(8,128)(2,1)S(1)}, bf16[2,768,128]{2,1,0:T(8,128)(2,1)S(1)}, u32[]{:S(2)}, u32[]{:S(2)}) collective-permute-start(bf16[2,768,128]{2,1,0:T(8,128)(2,1)S(1)} %get-tuple-element.335), channel_id=1, source_target_pairs={{0,8},{2,10},{4,12},{6,14},{8,0},{10,2},{12,4},{14,6},{16,24},{18,... | collective-permute-start | bytes 1179656 | tf_op jit(solution)/shard_map/ppermute | solution.py:861
  137.0 10.3 %collective-permute-start.18 = (bf16[4,272,128]{2,1,0:T(8,128)(2,1)S(1)}, bf16[4,272,128]{2,1,0:T(8,128)(2,1)S(1)}, u32[]{:S(2)}, u32[]{:S(2)}) collective-permute-start(bf16[4,272,128]{2,1,0:T(8,128)(2,1)S(1)} %get-tuple-element.334), channel_id=1, source_target_pairs={{0,4},{2,6},{4,0},{6,2},{8,12},{10,14},{12,8},{14,10},{16,20},{18,... | collective-permute-start | bytes 835592 | tf_op jit(solution)/shard_map/ppermute | solution.py:861
  138.6 8.8 %collective-permute-start.17 = (bf16[4,256,128]{2,1,0:T(8,128)(2,1)S(1)}, bf16[4,256,128]{2,1,0:T(8,128)(2,1)S(1)}, u32[]{:S(2)}, u32[]{:S(2)}) collective-permute-start(bf16[4,256,128]{2,1,0:T(8,128)(2,1)S(1)} %get-tuple-element.333), channel_id=1, source_target_pairs={{0,1},{1,0},{2,3},{3,2},{4,5},{5,4},{6,7},{7,6},{8,9},{9,8},{10,11... | collective-permute-start | bytes 786440 | tf_op jit(solution)/shard_map/ppermute | solution.py:863
  139.6 7.7 %collective-permute-start.20 = (f32[16,768]{1,0:T(8,128)S(1)}, f32[16,768]{1,0:T(8,128)S(1)}, u32[]{:S(2)}, u32[]{:S(2)}) collective-permute-start(f32[16,768]{1,0:T(8,128)S(1)} %add.15), channel_id=1, source_target_pairs={{0,16},{2,18},{4,20},{6,22},{8,24},{10,26},{12,28},{14,30},{16,0},... | collective-permute-start | bytes 147464 | tf_op jit(solution)/shard_map/ppermute | solution.py:861
  150.5 15.4 %collective-permute-start.21 = (bf16[8,288,128]{2,1,0:T(8,128)(2,1)S(1)}, bf16[8,288,128]{2,1,0:T(8,128)(2,1)S(1)}, u32[]{:S(2)}, u32[]{:S(2)}) collective-permute-start(bf16[8,288,128]{2,1,0:T(8,128)(2,1)S(1)} %get-tuple-element.354), channel_id=1, source_target_pairs={{0,4},{2,6},{4,0},{6,2},{8,12},{10,14},{12,8},{14,10},{16,20},{18,... | collective-permute-start | bytes 1769480 | tf_op jit(solution)/shard_map/ppermute | solution.py:861
  152.0 14.5 %collective-permute-start.22 = (bf16[8,288,128]{2,1,0:T(8,128)(2,1)S(1)}, bf16[8,288,128]{2,1,0:T(8,128)(2,1)S(1)}, u32[]{:S(2)}, u32[]{:S(2)}) collective-permute-start(bf16[8,288,128]{2,1,0:T(8,128)(2,1)S(1)} %get-tuple-element.355), channel_id=1, source_target_pairs={{0,1},{1,0},{2,3},{3,2},{4,5},{5,4},{6,7},{7,6},{8,9},{9,8},{10,11... | collective-permute-start | bytes 1769480 | tf_op jit(solution)/shard_map/ppermute | solution.py:863
  153.0 12.8 %collective-permute-start.23 = (bf16[2,528,128]{2,1,0:T(8,128)(2,1)S(1)}, bf16[2,528,128]{2,1,0:T(8,128)(2,1)S(1)}, u32[]{:S(2)}, u32[]{:S(2)}) collective-permute-start(bf16[2,528,128]{2,1,0:T(8,128)(2,1)S(1)} %get-tuple-element.356), channel_id=1, source_target_pairs={{0,8},{2,10},{4,12},{6,14},{8,0},{10,2},{12,4},{14,6},{16,24},{18,... | collective-permute-start | bytes 811016 | tf_op jit(solution)/shard_map/ppermute | solution.py:861
  155.1 10.7 %collective-permute-start.24 = (bf16[1,768,128]{2,1,0:T(8,128)(2,1)S(1)}, bf16[1,768,128]{2,1,0:T(8,128)(2,1)S(1)}, u32[]{:S(2)}, u32[]{:S(2)}) collective-permute-start(bf16[1,768,128]{2,1,0:T(8,128)(2,1)S(1)} %get-tuple-element.357), channel_id=1, source_target_pairs={{0,16},{2,18},{4,20},{6,22},{8,24},{10,26},{12,28},{14,30},{16,0},... | collective-permute-start | bytes 589832 | tf_op jit(solution)/shard_map/ppermute | solution.py:861
  155.3 1.2 collective-permute-start.25
  156.6 12.6 %copy-start.30 = (f32[8,768]{1,0:T(8,128)S(1)}, f32[8,768]{1,0:T(8,128)}, u32[]{:S(2)}) copy-start(f32[8,768]{1,0:T(8,128)} %get-tuple-element.393) | copy-start | bytes 73732
  156.6 16.8 %copy-start.28 = (f32[320,768]{1,0:T(8,128)S(1)}, f32[320,768]{1,0:T(8,128)}, u32[]{:S(2)}) copy-start(f32[320,768]{1,0:T(8,128)} %get-tuple-element.394) | copy-start | bytes 2949124
  167.7 11.6 %collective-permute-start.26 = (bf16[4,288,128]{2,1,0:T(8,128)(2,1)S(1)}, bf16[4,288,128]{2,1,0:T(8,128)(2,1)S(1)}, u32[]{:S(2)}, u32[]{:S(2)}) collective-permute-start(bf16[4,288,128]{2,1,0:T(8,128)(2,1)S(1)} %get-tuple-element.374), channel_id=1, source_target_pairs={{0,1},{1,0},{2,3},{3,2},{4,5},{5,4},{6,7},{7,6},{8,9},{9,8},{10,11... | collective-permute-start | bytes 884744 | tf_op jit(solution)/shard_map/ppermute | solution.py:863
  168.7 10.6 %collective-permute-start.27 = (bf16[4,288,128]{2,1,0:T(8,128)(2,1)S(1)}, bf16[4,288,128]{2,1,0:T(8,128)(2,1)S(1)}, u32[]{:S(2)}, u32[]{:S(2)}) collective-permute-start(bf16[4,288,128]{2,1,0:T(8,128)(2,1)S(1)} %get-tuple-element.375), channel_id=1, source_target_pairs={{0,4},{2,6},{4,0},{6,2},{8,12},{10,14},{12,8},{14,10},{16,20},{18,... | collective-permute-start | bytes 884744 | tf_op jit(solution)/shard_map/ppermute | solution.py:861
  170.4 6.4 %collective-permute-start.29 = (f32[16,768]{1,0:T(8,128)S(1)}, f32[16,768]{1,0:T(8,128)S(1)}, u32[]{:S(2)}, u32[]{:S(2)}) collective-permute-start(f32[16,768]{1,0:T(8,128)S(1)} %add.17), channel_id=1, source_target_pairs={{0,4},{2,6},{4,0},{6,2},{8,12},{10,14},{12,8},{14,10},{16,20},{18,... | collective-permute-start | bytes 147464 | tf_op jit(solution)/shard_map/ppermute | solution.py:861
  171.9 7.4 %collective-permute-start.28 = (bf16[1,528,128]{2,1,0:T(8,128)(2,1)S(1)}, bf16[1,528,128]{2,1,0:T(8,128)(2,1)S(1)}, u32[]{:S(2)}, u32[]{:S(2)}) collective-permute-start(bf16[1,528,128]{2,1,0:T(8,128)(2,1)S(1)} %get-tuple-element.376), channel_id=1, source_target_pairs={{0,16},{2,18},{4,20},{6,22},{8,24},{10,26},{12,28},{14,30},{16,0},... | collective-permute-start | bytes 405512 | tf_op jit(solution)/shard_map/ppermute | solution.py:861
  180.1 6.1 %collective-permute-start.33 = (f32[16,768]{1,0:T(8,128)S(1)}, f32[16,768]{1,0:T(8,128)S(1)}, u32[]{:S(2)}, u32[]{:S(2)}) collective-permute-start(f32[16,768]{1,0:T(8,128)S(1)} %add.18), channel_id=1, source_target_pairs={{0,1},{1,0},{2,3},{3,2},{4,5},{5,4},{6,7},{7,6},{8,9},{9,8},{10,11... | collective-permute-start | bytes 147464 | tf_op jit(solution)/shard_map/ppermute | solution.py:863
  181.1 10.4 %collective-permute-start.30 = (bf16[1,576,128]{2,1,0:T(8,128)(2,1)S(1)}, bf16[1,576,128]{2,1,0:T(8,128)(2,1)S(1)}, u32[]{:S(2)}, u32[]{:S(2)}) collective-permute-start(bf16[1,576,128]{2,1,0:T(8,128)(2,1)S(1)} %get-tuple-element.388), channel_id=1, source_target_pairs={{0,16},{2,18},{4,20},{6,22},{8,24},{10,26},{12,28},{14,30},{16,0},... | collective-permute-start | bytes 442376 | tf_op jit(solution)/shard_map/ppermute | solution.py:861
  181.2 10.2 %collective-permute-start.31 = (bf16[1,576,128]{2,1,0:T(8,128)(2,1)S(1)}, bf16[1,576,128]{2,1,0:T(8,128)(2,1)S(1)}, u32[]{:S(2)}, u32[]{:S(2)}) collective-permute-start(bf16[1,576,128]{2,1,0:T(8,128)(2,1)S(1)} %get-tuple-element.389), channel_id=1, source_target_pairs={{0,8},{2,10},{4,12},{6,14},{8,0},{10,2},{12,4},{14,6},{16,24},{18,... | collective-permute-start | bytes 442376 | tf_op jit(solution)/shard_map/ppermute | solution.py:861
  183.6 7.8 %collective-permute-start.32 = (bf16[1,576,128]{2,1,0:T(8,128)(2,1)S(1)}, bf16[1,576,128]{2,1,0:T(8,128)(2,1)S(1)}, u32[]{:S(2)}, u32[]{:S(2)}) collective-permute-start(bf16[1,576,128]{2,1,0:T(8,128)(2,1)S(1)} %get-tuple-element.390), channel_id=1, source_target_pairs={{0,24},{2,26},{4,28},{6,30},{8,16},{10,18},{12,20},{14,22},{16,8},... | collective-permute-start | bytes 442376 | tf_op jit(solution)/shard_map/ppermute | solution.py:861
  (1 other events, 0.7 us)

commit v3 on v2

--- a/solution.py
+++ b/solution.py
@@ -96,7 +96,7 @@
             o_ref[rows, lanes] = low(total)
         return carry
 
-    lax.fori_loop(0, pairs, pair, 0, unroll=2)
+    lax.fori_loop(0, pairs, pair, 0, unroll=3)
 
 
 def attend_back_kernel(

time: 194 us -> 194 us (level)
  transfers between devices with their start and end apart: 34 -> 34, of which waited for: 16 -> 15; matrix products, arithmetic and copies ran while one was open for 3% -> 3% of each run, Pallas kernels for 20% -> 20%
where the time goes in v3:
time: 194 us
  Pallas kernels  104 us (54%)
  waiting for transfers between devices  43.5 us (22%)
  starting transfers between devices  35.7 us (18%)
  local copies, waits for them, and re-layouts  6.76 us (3%)
  between operations  3.58 us (2%)
    ppermute x25, waiting for transfers between devices, swap(): return lax.ppermute(a, 'wide', [(i, i ^ dw) for i in range(wide)])  31.7 us
    pallas_call x1, Pallas kernels, loss_and_back(): pl.pallas_call(functools.partial(back_kernel, narrow, stages, qlen, 4, n_...  30.1 us
    pallas_call x1, Pallas kernels, forward(): pl.pallas_call(functools.partial(forward_kernel, qlen, plen, 4), out_shap...  29.5 us
    ppermute x25, starting transfers between devices, swap(): return lax.ppermute(a, 'wide', [(i, i ^ dw) for i in range(wide)])  24.9 us
    pallas_call x2, Pallas kernels, wgrad(): pl.pallas_call(functools.partial(wgrad_kernel, full, groups, len(ops)), o...  20.1 us
    pallas_call x1, Pallas kernels, rest_back(): pl.pallas_call(functools.partial(rest_kernel, qlen, buckets, len(fetched)...  17.8 us
    ppermute x8, waiting for transfers between devices, swap(): return lax.ppermute(a, 'narrow', [(i, i ^ dn) for i in range(narrow)])  9.8 us
    ppermute x8, starting transfers between devices, swap(): return lax.ppermute(a, 'narrow', [(i, i ^ dn) for i in range(narrow)])  8.28 us
  transfers between devices with their start and end apart: 34, of which 15 were waited for; matrix products, arithmetic and copies ran while one was open for 3% of the time, Pallas kernels for 20%

profile of v3, /device:TPU:0, one launch (start us, length us, event | category | flops | bytes accessed | tf_op | source)
XLA Modules:
  0.0 193.7 jit_solution(18284594438950485882)
XLA Ops:
  0.6 29.5 %forward.1 = (bf16[8,768]{1,0:T(8,128)(2,1)}, f32[8,768]{1,0:T(8,128)}, f32[8,768]{1,0:T(8,128)}, bf16[8,768]{1,0:T(8,128)(2,1)}, f32[320,768]{1,0:T(8,128)}, /*...) custom-call(bf16[64,768]{1,0:T(8,128)(2,1)} %bitcast.20, ...), custom_call_target="tpu_custom_call" | custom-call | flops 9814671360 | bytes 15335424 | tf_op jit(solution)/shard_map/forward/pallas_call | solution.py:332
  30.2 5.1 %collective-permute-start.2 = (bf16[8,768]{1,0:T(8,128)(2,1)}, bf16[8,768]{1,0:T(8,128)(2,1)S(1)}, u32[]{:S(2)}, u32[]{:S(2)}) collective-permute-start(bf16[8,768]{1,0:T(8,128)(2,1)} %get-tuple-element.212.refs_0_), channel_id=1, source_target_pairs={{0,24},{2,26},{4,28},{6,30},{8,16},{10,18},{12,20},{14,22},{16,8},... | collective-permute-start | bytes 36872 | tf_op jit(solution)/shard_map/ppermute | solution.py:861
  35.3 0.6 collective-permute-start
  35.9 1.2 collective-permute-done.2.refs_3_
  37.1 2.9 %collective-permute-done.1.refs_2_ = bf16[8,768]{1,0:T(8,128)(2,1)S(1)} collective-permute-done((bf16[8,768]{1,0:T(8,128)(2,1)}, bf16[8,768]{1,0:T(8,128)(2,1)S(1)}, u32[]{:S(2)}, u32[]{:S(2)}) %collective-permute-start.1) | collective-permute-done | bytes 12320 | tf_op jit(solution)/shard_map/ppermute | solution.py:861
  40.1 0.7 copy-done.13
  40.8 2.5 %collective-permute-start.5 = (bf16[32,768]{1,0:T(8,128)(2,1)S(1)}, bf16[32,768]{1,0:T(8,128)(2,1)S(1)}, u32[]{:S(2)}, u32[]{:S(2)}) collective-permute-start(bf16[32,768]{1,0:T(8,128)(2,1)S(1)} %join.2.refs_0_), channel_id=1, source_target_pairs={{0,5},{1,4},{2,7},{3,6},{4,1},{5,0},{6,3},{7,2},{8,13},{9,12},{10,... | collective-permute-start | bytes 147464 | tf_op jit(solution)/shard_map/ppermute | solution.py:865
  43.3 0.5 collective-permute-start.4
  43.8 0.5 collective-permute-start.3
  44.3 2.0 %collective-permute-done.5.refs_3_ = bf16[32,768]{1,0:T(8,128)(2,1)S(1)} collective-permute-done((bf16[32,768]{1,0:T(8,128)(2,1)S(1)}, bf16[32,768]{1,0:T(8,128)(2,1)S(1)}, u32[]{:S(2)}, u32[]{:S(2)}) %collective-permute-start.5) | collective-permute-done | bytes 49184 | tf_op jit(solution)/shard_map/ppermute | solution.py:865
  46.2 1.1 collective-permute-done.4.refs_2_
  47.4 0.5 collective-permute-done.3.refs_1_
  48.6 0.6 pad_add_fusion.refs_0_.me_ref
  49.4 0.7 copy-done.29
  50.1 30.1 %loss_and_back.1 = (f32[1,768]{1,0:T(1,128)}, f32[1,128]{1,0:T(1,128)}, bf16[8,768]{1,0:T(8,128)(2,1)}, f32[1,768]{1,0:T(1,128)}, f32[1,768]{1,0:T(1,128)}, /*in...) custom-call(s32[2]{0:T(128)} %pad_add_fusion.refs_0_.me_ref, ...), custom_call_target="tpu_custom_call" | custom-call | flops 7361003520 | bytes 15335424 | tf_op jit(solution)/shard_map/loss_and_back/pallas_call | solution.py:575
  80.2 0.4 collective-permute-start.7
  80.6 0.7 copy-done.24
  81.3 9.5 %wgrad.2 = (bf16[16,528,128]{2,1,0:T(8,128)(2,1)}, bf16[16,528,128]{2,1,0:T(8,128)(2,1)}) custom-call(s32[2]{0:T(128)S(1)} %copy-done.19, bf16[320,768]{1,0:T(8,128)(2,1)S(1)} %copy-done.7, bf16[320,768]{1,0:T(8,128)(2,1)S(1)} %copy-done.8, bf16[320,2048]{1,0:T(8,128)(2,1)} %get-tuple-element.260.refs_2_.refs_8_, ...), custom_call_target="tpu_custom_call" | custom-call | flops 2022703104 | bytes 7901184 | tf_op jit(solution)/shard_map/wgrad/pallas_call | solution.py:842
  90.9 0.9 advance.7
  91.8 0.3 collective-permute-start.10
  92.1 0.5 collective-permute-start.8
  92.6 1.6 collective-permute-start.9
  94.2 17.8 %rest_back.1 = (f32[16,768]{1,0:T(8,128)S(1)}, bf16[320,768]{1,0:T(8,128)(2,1)S(1)}, bf16[320,768]{1,0:T(8,128)(2,1)S(1)}, bf16[320,768]{1,0:T(8,128)(2,1)S(1)},...) custom-call(f32[3,768]{1,0:T(4,128)S(1)} %copy-done.12, s32[1,511]{1,0:T(1,128)S(1)} %bitcast.23, ...), custom_call_target="tpu_custom_call" | custom-call | flops 5284823040 | bytes 11010048 | tf_op jit(solution)/shard_map/rest_back/pallas_call | solution.py:672
  112.2 1.1 advance.8
  113.3 1.6 collective-permute-start.14
  114.9 1.5 collective-permute-start.13
  116.4 0.5 collective-permute-start.11
  116.9 0.5 collective-permute-start.12
  117.4 10.6 %wgrad.3 = (bf16[16,576,128]{2,1,0:T(8,128)(2,1)S(1)}, bf16[16,576,128]{2,1,0:T(8,128)(2,1)S(1)}) custom-call(s32[2]{0:T(128)S(1)} %copy-done.19, bf16[320,768]{1,0:T(8,128)(2,1)S(1)} %get-tuple-element.299.refs_0_, bf16[320,768]{1,0:T(8,128)(2,1)S(1)} %copy-done.20, bf16[320,768]{1,0:T(8,128)(2,1)S(1)} %copy-done.3, bf16[320,768]{1,0:T(8,128)(2,1)S(1)} %copy-done.4, ...), custom_call_target="tpu_custom_call" | custom-call | flops 3019898880 | bytes 11796480 | tf_op jit(solution)/shard_map/wgrad/pallas_call | solution.py:842
  128.1 7.9 %collective-permute-done.11.refs_1_ = bf16[4,384,128]{2,1,0:T(8,128)(2,1)S(1)} collective-permute-done((bf16[4,384,128]{2,1,0:T(8,128)(2,1)S(1)}, bf16[4,384,128]{2,1,0:T(8,128)(2,1)S(1)}, u32[]{:S(2)}, u32[]{:S(2)}) %collective-permute-start.11) | collective-permute-done | bytes 393248 | tf_op jit(solution)/shard_map/ppermute | solution.py:863
  136.1 0.5 advance.9
  136.8 1.5 collective-permute-start.18
  138.3 1.0 collective-permute-start.17
  139.3 2.0 %collective-permute-start.20 = (f32[16,768]{1,0:T(8,128)S(1)}, f32[16,768]{1,0:T(8,128)S(1)}, u32[]{:S(2)}, u32[]{:S(2)}) collective-permute-start(f32[16,768]{1,0:T(8,128)S(1)} %add.15), channel_id=1, source_target_pairs={{0,16},{2,18},{4,20},{6,22},{8,24},{10,26},{12,28},{14,30},{16,0},... | collective-permute-start | bytes 147464 | tf_op jit(solution)/shard_map/ppermute | solution.py:861
  141.3 5.7 %collective-permute-done.20 = f32[16,768]{1,0:T(8,128)S(1)} collective-permute-done((f32[16,768]{1,0:T(8,128)S(1)}, f32[16,768]{1,0:T(8,128)S(1)}, u32[]{:S(2)}, u32[]{:S(2)}) %collective-permute-start.20) | collective-permute-done | bytes 49184 | tf_op jit(solution)/shard_map/ppermute | solution.py:861
  147.1 2.2 %collective-permute-done.19.refs_7_ = bf16[2,768,128]{2,1,0:T(8,128)(2,1)S(1)} collective-permute-done((bf16[2,768,128]{2,1,0:T(8,128)(2,1)S(1)}, bf16[2,768,128]{2,1,0:T(8,128)(2,1)S(1)}, u32[]{:S(2)}, u32[]{:S(2)}) %collective-permute-start.19) | collective-permute-done | bytes 393248 | tf_op jit(solution)/shard_map/ppermute | solution.py:861
  149.2 0.9 advance.10
  150.2 1.5 collective-permute-start.21
  151.7 1.0 collective-permute-start.22
  152.8 2.1 %collective-permute-start.23 = (bf16[2,528,128]{2,1,0:T(8,128)(2,1)S(1)}, bf16[2,528,128]{2,1,0:T(8,128)(2,1)S(1)}, u32[]{:S(2)}, u32[]{:S(2)}) collective-permute-start(bf16[2,528,128]{2,1,0:T(8,128)(2,1)S(1)} %get-tuple-element.356), channel_id=1, source_target_pairs={{0,8},{2,10},{4,12},{6,14},{8,0},{10,2},{12,4},{14,6},{16,24},{18,... | collective-permute-start | bytes 811016 | tf_op jit(solution)/shard_map/ppermute | solution.py:861
  154.8 0.2 collective-permute-start.24
  155.1 1.2 collective-permute-done.25
  156.3 9.2 %collective-permute-done.24.refs_7_ = bf16[1,768,128]{2,1,0:T(8,128)(2,1)S(1)} collective-permute-done((bf16[1,768,128]{2,1,0:T(8,128)(2,1)S(1)}, bf16[1,768,128]{2,1,0:T(8,128)(2,1)S(1)}, u32[]{:S(2)}, u32[]{:S(2)}) %collective-permute-start.24) | collective-permute-done | bytes 196640 | tf_op jit(solution)/shard_map/ppermute | solution.py:861
  165.6 0.7 collective-permute-done.22.refs_3_
  166.3 1.1 advance.11
  167.4 1.0 collective-permute-start.26
  168.4 0.5 collective-permute-start.27
  168.9 0.6 slice.25
  169.5 0.6 slice.24
  170.1 1.5 collective-permute-start.29
  171.6 1.5 collective-permute-start.28
  173.1 0.9 slice_bitcast_fusion
  174.1 2.4 %collective-permute-done.29 = f32[16,768]{1,0:T(8,128)S(1)} collective-permute-done((f32[16,768]{1,0:T(8,128)S(1)}, f32[16,768]{1,0:T(8,128)S(1)}, u32[]{:S(2)}, u32[]{:S(2)}) %collective-permute-start.29) | collective-permute-done | bytes 49184 | tf_op jit(solution)/shard_map/ppermute | solution.py:861
  176.5 2.5 %collective-permute-done.28.refs_5_ = bf16[1,528,128]{2,1,0:T(8,128)(2,1)S(1)} collective-permute-done((bf16[1,528,128]{2,1,0:T(8,128)(2,1)S(1)}, bf16[1,528,128]{2,1,0:T(8,128)(2,1)S(1)}, u32[]{:S(2)}, u32[]{:S(2)}) %collective-permute-start.28) | collective-permute-done | bytes 135200 | tf_op jit(solution)/shard_map/ppermute | solution.py:861
  179.0 0.8 advance.12
  179.8 1.0 collective-permute-start.33
  181.0 2.4 %collective-permute-start.31 = (bf16[1,576,128]{2,1,0:T(8,128)(2,1)S(1)}, bf16[1,576,128]{2,1,0:T(8,128)(2,1)S(1)}, u32[]{:S(2)}, u32[]{:S(2)}) collective-permute-start(bf16[1,576,128]{2,1,0:T(8,128)(2,1)S(1)} %get-tuple-element.389), channel_id=1, source_target_pairs={{0,8},{2,10},{4,12},{6,14},{8,0},{10,2},{12,4},{14,6},{16,24},{18,... | collective-permute-start | bytes 442376 | tf_op jit(solution)/shard_map/ppermute | solution.py:861
  183.3 1.8 collective-permute-start.32
  185.2 0.7 slice_bitcast_fusion.1
  185.9 0.5 slice.30
  186.4 0.6 slice.29
  187.0 0.6 slice.28
  187.6 3.5 %collective-permute-done.30.refs_1_ = bf16[1,576,128]{2,1,0:T(8,128)(2,1)S(1)} collective-permute-done((bf16[1,576,128]{2,1,0:T(8,128)(2,1)S(1)}, bf16[1,576,128]{2,1,0:T(8,128)(2,1)S(1)}, u32[]{:S(2)}, u32[]{:S(2)}) %collective-permute-start.30) | collective-permute-done | bytes 147488 | tf_op jit(solution)/shard_map/ppermute | solution.py:861
  191.8 0.7 advance.13
  (93 shorter events, 0.9 us)
Async XLA Ops:
  30.2 7.0 %collective-permute-start.2 = (bf16[8,768]{1,0:T(8,128)(2,1)}, bf16[8,768]{1,0:T(8,128)(2,1)S(1)}, u32[]{:S(2)}, u32[]{:S(2)}) collective-permute-start(bf16[8,768]{1,0:T(8,128)(2,1)} %get-tuple-element.212.refs_0_), channel_id=1, source_target_pairs={{0,24},{2,26},{4,28},{6,30},{8,16},{10,18},{12,20},{14,22},{16,8},... | collective-permute-start | bytes 36872 | tf_op jit(solution)/shard_map/ppermute | solution.py:861
  35.3 4.8 %collective-permute-start.1 = (bf16[8,768]{1,0:T(8,128)(2,1)}, bf16[8,768]{1,0:T(8,128)(2,1)S(1)}, u32[]{:S(2)}, u32[]{:S(2)}) collective-permute-start(bf16[8,768]{1,0:T(8,128)(2,1)} %get-tuple-element.212.refs_0_), channel_id=1, source_target_pairs={{0,16},{2,18},{4,20},{6,22},{8,24},{10,26},{12,28},{14,30},{16,0},... | collective-permute-start | bytes 36872 | tf_op jit(solution)/shard_map/ppermute | solution.py:861
  35.3 4.8 %collective-permute-start = (bf16[8,768]{1,0:T(8,128)(2,1)}, bf16[8,768]{1,0:T(8,128)(2,1)S(1)}, u32[]{:S(2)}, u32[]{:S(2)}) collective-permute-start(bf16[8,768]{1,0:T(8,128)(2,1)} %get-tuple-element.212.refs_0_), channel_id=1, source_target_pairs={{0,8},{2,10},{4,12},{6,14},{8,0},{10,2},{12,4},{14,6},{16,24},{18,... | collective-permute-start | bytes 36872 | tf_op jit(solution)/shard_map/ppermute | solution.py:861
  40.1 0.7 copy-start.13
  40.8 5.4 %collective-permute-start.5 = (bf16[32,768]{1,0:T(8,128)(2,1)S(1)}, bf16[32,768]{1,0:T(8,128)(2,1)S(1)}, u32[]{:S(2)}, u32[]{:S(2)}) collective-permute-start(bf16[32,768]{1,0:T(8,128)(2,1)S(1)} %join.2.refs_0_), channel_id=1, source_target_pairs={{0,5},{1,4},{2,7},{3,6},{4,1},{5,0},{6,3},{7,2},{8,13},{9,12},{10,... | collective-permute-start | bytes 147464 | tf_op jit(solution)/shard_map/ppermute | solution.py:865
  43.3 4.1 %collective-permute-start.4 = (bf16[32,768]{1,0:T(8,128)(2,1)S(1)}, bf16[32,768]{1,0:T(8,128)(2,1)S(1)}, u32[]{:S(2)}, u32[]{:S(2)}) collective-permute-start(bf16[32,768]{1,0:T(8,128)(2,1)S(1)} %join.2.refs_0_), channel_id=1, source_target_pairs={{0,1},{1,0},{2,3},{3,2},{4,5},{5,4},{6,7},{7,6},{8,9},{9,8},{10,11... | collective-permute-start | bytes 147464 | tf_op jit(solution)/shard_map/ppermute | solution.py:863
  43.8 4.1 %collective-permute-start.3 = (bf16[32,768]{1,0:T(8,128)(2,1)S(1)}, bf16[32,768]{1,0:T(8,128)(2,1)S(1)}, u32[]{:S(2)}, u32[]{:S(2)}) collective-permute-start(bf16[32,768]{1,0:T(8,128)(2,1)S(1)} %join.2.refs_0_), channel_id=1, source_target_pairs={{0,4},{2,6},{4,0},{6,2},{8,12},{10,14},{12,8},{14,10},{16,20},{18,... | collective-permute-start | bytes 147464 | tf_op jit(solution)/shard_map/ppermute | solution.py:861
  47.9 1.5 copy-start.2
  47.9 1.5 collective-permute-start.6
  50.1 30.5 %copy-start.7 = (bf16[320,768]{1,0:T(8,128)(2,1)S(1)}, bf16[320,768]{1,0:T(8,128)(2,1)}, u32[]{:S(2)}) copy-start(bf16[320,768]{1,0:T(8,128)(2,1)} %get-tuple-element.229.refs_31_.refs_0_) | copy-start | bytes 1474564
  50.1 30.5 %copy-start.8 = (bf16[320,768]{1,0:T(8,128)(2,1)S(1)}, bf16[320,768]{1,0:T(8,128)(2,1)}, u32[]{:S(2)}) copy-start(bf16[320,768]{1,0:T(8,128)(2,1)} %get-tuple-element.230.refs_32_.refs_1_) | copy-start | bytes 1474564
  50.1 30.5 %copy-start.19 = (s32[2]{0:T(128)S(1)}, s32[2]{0:T(128)}, u32[]{:S(2)}) copy-start(s32[2]{0:T(128)} %pad_add_fusion.refs_0_.me_ref) | copy-start | bytes 28
  50.1 30.5 %copy-start.27 = (bf16[8,768]{1,0:T(8,128)(2,1)S(1)}, bf16[8,768]{1,0:T(8,128)(2,1)}, u32[]{:S(2)}) copy-start(bf16[8,768]{1,0:T(8,128)(2,1)} %get-tuple-element.240.refs_5_) | copy-start | bytes 36868
  80.2 10.6 %collective-permute-start.7 = (bf16[16,768,128]{2,1,0:T(8,128)(2,1)}, bf16[16,768,128]{2,1,0:T(8,128)(2,1)S(1)}, u32[]{:S(2)}, u32[]{:S(2)}) collective-permute-start(bf16[16,768,128]{2,1,0:T(8,128)(2,1)} %get-tuple-element.236), channel_id=1, source_target_pairs={{0,2},{2,0},{4,6},{6,4},{8,10},{10,8},{12,14},{14,12},{16,18},{18,... | collective-permute-start | bytes 9437192 | tf_op jit(solution)/shard_map/ppermute | solution.py:861
  80.6 0.7 copy-start.24
  81.3 9.5 %copy-start = (bf16[16,768,128]{2,1,0:T(8,128)(2,1)S(1)}, bf16[16,768,128]{2,1,0:T(8,128)(2,1)}, u32[]{:S(2)}) copy-start(bf16[16,768,128]{2,1,0:T(8,128)(2,1)} %get-tuple-element.235.refs_0_) | copy-start | bytes 9437188
  90.8 3.3 %copy-start.5 = (bf16[320,768]{1,0:T(8,128)(2,1)S(1)}, bf16[320,768]{1,0:T(8,128)(2,1)}, u32[]{:S(2)}) copy-start(bf16[320,768]{1,0:T(8,128)(2,1)} %get-tuple-element.263.refs_13_) | copy-start | bytes 1474564
  90.8 3.3 %copy-start.6 = (bf16[320,768]{1,0:T(8,128)(2,1)S(1)}, bf16[320,768]{1,0:T(8,128)(2,1)}, u32[]{:S(2)}) copy-start(bf16[320,768]{1,0:T(8,128)(2,1)} %get-tuple-element.264.refs_14_) | copy-start | bytes 1474564
  90.8 3.3 %copy-start.9 = (bf16[1,256,768]{2,1,0:T(8,128)(2,1)S(1)}, bf16[1,256,768]{2,1,0:T(8,128)(2,1)}, u32[]{:S(2)}) copy-start(bf16[1,256,768]{2,1,0:T(8,128)(2,1)} %param.19) | copy-start | bytes 1179652
  90.8 3.3 %copy-start.10 = (bf16[12,64,64]{2,1,0:T(8,128)(2,1)S(1)}, bf16[12,64,64]{2,1,0:T(8,128)(2,1)}, u32[]{:S(2)}) copy-start(bf16[12,64,64]{2,1,0:T(8,128)(2,1)} %get-tuple-element.268.refs_18_) | copy-start | bytes 294916
  90.9 3.3 %copy-start.11 = (bf16[1,64,768]{2,1,0:T(8,128)(2,1)S(1)}, bf16[1,64,768]{2,1,0:T(8,128)(2,1)}, u32[]{:S(2)}) copy-start(bf16[1,64,768]{2,1,0:T(8,128)(2,1)} %param.17) | copy-start | bytes 294916
  90.9 3.3 %copy-start.12 = (f32[3,768]{1,0:T(4,128)S(1)}, f32[3,768]{1,0:T(4,128)}, u32[]{:S(2)}) copy-start(f32[3,768]{1,0:T(4,128)} %refs_0_.1) | copy-start | bytes 27652
  90.9 3.3 %copy-start.14 = (f32[1,768]{1,0:T(1,128)S(1)}, f32[1,768]{1,0:T(1,128)}, u32[]{:S(2)}) copy-start(f32[1,768]{1,0:T(1,128)} %get-tuple-element.257.refs_4_) | copy-start | bytes 9220
  90.9 3.3 %copy-start.15 = (f32[1,768]{1,0:T(1,128)S(1)}, f32[1,768]{1,0:T(1,128)}, u32[]{:S(2)}) copy-start(f32[1,768]{1,0:T(1,128)} %get-tuple-element.256.refs_3_) | copy-start | bytes 9220
  90.9 3.3 %copy-start.16 = (f32[1,768]{1,0:T(1,128)S(1)}, f32[1,768]{1,0:T(1,128)}, u32[]{:S(2)}) copy-start(f32[1,768]{1,0:T(1,128)} %get-tuple-element.255.refs_2_) | copy-start | bytes 9220
  90.9 3.3 %copy-start.17 = (s32[511]{0:T(512)S(1)}, s32[511]{0:T(512)}, u32[]{:S(2)}) copy-start(s32[511]{0:T(512)} %param.22) | copy-start | bytes 6136
  90.9 3.3 %copy-start.18 = (f32[1,128]{1,0:T(1,128)S(1)}, f32[1,128]{1,0:T(1,128)}, u32[]{:S(2)}) copy-start(f32[1,128]{1,0:T(1,128)} %get-tuple-element.258.refs_5_) | copy-start | bytes 1540
  91.8 20.2 %collective-permute-start.10 = (bf16[16,528,128]{2,1,0:T(8,128)(2,1)}, bf16[16,528,128]{2,1,0:T(8,128)(2,1)S(1)}, u32[]{:S(2)}, u32[]{:S(2)}) collective-permute-start(bf16[16,528,128]{2,1,0:T(8,128)(2,1)} %get-tuple-element.254), channel_id=1, source_target_pairs={{0,2},{2,0},{4,6},{6,4},{8,10},{10,8},{12,14},{14,12},{16,18},{18,... | collective-permute-start | bytes 6488072 | tf_op jit(solution)/shard_map/ppermute | solution.py:861
  92.1 19.9 %collective-permute-start.8 = (bf16[8,384,128]{2,1,0:T(8,128)(2,1)S(1)}, bf16[8,384,128]{2,1,0:T(8,128)(2,1)S(1)}, u32[]{:S(2)}, u32[]{:S(2)}) collective-permute-start(bf16[8,384,128]{2,1,0:T(8,128)(2,1)S(1)} %get-tuple-element.252), channel_id=1, source_target_pairs={{0,4},{2,6},{4,0},{6,2},{8,12},{10,14},{12,8},{14,10},{16,20},{18,... | collective-permute-start | bytes 2359304 | tf_op jit(solution)/shard_map/ppermute | solution.py:861
  92.6 19.5 %collective-permute-start.9 = (bf16[8,384,128]{2,1,0:T(8,128)(2,1)S(1)}, bf16[8,384,128]{2,1,0:T(8,128)(2,1)S(1)}, u32[]{:S(2)}, u32[]{:S(2)}) collective-permute-start(bf16[8,384,128]{2,1,0:T(8,128)(2,1)S(1)} %get-tuple-element.253), channel_id=1, source_target_pairs={{0,1},{1,0},{2,3},{3,2},{4,5},{5,4},{6,7},{7,6},{8,9},{9,8},{10,11... | collective-permute-start | bytes 2359304 | tf_op jit(solution)/shard_map/ppermute | solution.py:863
  94.2 17.8 %copy-start.1 = (bf16[16,528,128]{2,1,0:T(8,128)(2,1)S(1)}, bf16[16,528,128]{2,1,0:T(8,128)(2,1)}, u32[]{:S(2)}) copy-start(bf16[16,528,128]{2,1,0:T(8,128)(2,1)} %get-tuple-element.279.refs_4_) | copy-start | bytes 6488068
  112.1 5.3 %copy-start.3 = (bf16[320,768]{1,0:T(8,128)(2,1)S(1)}, bf16[320,768]{1,0:T(8,128)(2,1)}, u32[]{:S(2)}) copy-start(bf16[320,768]{1,0:T(8,128)(2,1)} %get-tuple-element.266.refs_16_.refs_2_) | copy-start | bytes 1474564
  112.1 5.3 %copy-start.4 = (bf16[320,768]{1,0:T(8,128)(2,1)S(1)}, bf16[320,768]{1,0:T(8,128)(2,1)}, u32[]{:S(2)}) copy-start(bf16[320,768]{1,0:T(8,128)(2,1)} %get-tuple-element.219.refs_18_.refs_3_) | copy-start | bytes 1474564
  112.1 5.3 %copy-start.20 = (bf16[320,768]{1,0:T(8,128)(2,1)S(1)}, bf16[320,768]{1,0:T(8,128)(2,1)}, u32[]{:S(2)}) copy-start(bf16[320,768]{1,0:T(8,128)(2,1)} %get-tuple-element.300.refs_1_) | copy-start | bytes 1474564
  112.1 5.3 %copy-start.21 = (bf16[320,768]{1,0:T(8,128)(2,1)S(1)}, bf16[320,768]{1,0:T(8,128)(2,1)}, u32[]{:S(2)}) copy-start(bf16[320,768]{1,0:T(8,128)(2,1)} %get-tuple-element.302.refs_5_) | copy-start | bytes 1474564
  112.1 5.3 %copy-start.22 = (bf16[320,768]{1,0:T(8,128)(2,1)S(1)}, bf16[320,768]{1,0:T(8,128)(2,1)}, u32[]{:S(2)}) copy-start(bf16[320,768]{1,0:T(8,128)(2,1)} %get-tuple-element.306.refs_9_) | copy-start | bytes 1474564
  112.1 5.3 %copy-start.23 = (bf16[320,768]{1,0:T(8,128)(2,1)S(1)}, bf16[320,768]{1,0:T(8,128)(2,1)}, u32[]{:S(2)}) copy-start(bf16[320,768]{1,0:T(8,128)(2,1)} %get-tuple-element.308.refs_11_) | copy-start | bytes 1474564
  112.1 5.3 %copy-start.25 = (bf16[320,768]{1,0:T(8,128)(2,1)S(1)}, bf16[320,768]{1,0:T(8,128)(2,1)}, u32[]{:S(2)}) copy-start(bf16[320,768]{1,0:T(8,128)(2,1)} %get-tuple-element.303.refs_6_) | copy-start | bytes 1474564
  112.1 5.3 %copy-start.26 = (bf16[320,768]{1,0:T(8,128)(2,1)S(1)}, bf16[320,768]{1,0:T(8,128)(2,1)}, u32[]{:S(2)}) copy-start(bf16[320,768]{1,0:T(8,128)(2,1)} %get-tuple-element.304.refs_7_) | copy-start | bytes 1474564
  113.3 22.8 %collective-permute-start.14 = (bf16[8,272,128]{2,1,0:T(8,128)(2,1)S(1)}, bf16[8,272,128]{2,1,0:T(8,128)(2,1)S(1)}, u32[]{:S(2)}, u32[]{:S(2)}) collective-permute-start(bf16[8,272,128]{2,1,0:T(8,128)(2,1)S(1)} %get-tuple-element.297), channel_id=1, source_target_pairs={{0,1},{1,0},{2,3},{3,2},{4,5},{5,4},{6,7},{7,6},{8,9},{9,8},{10,11... | collective-permute-start | bytes 1671176 | tf_op jit(solution)/shard_map/ppermute | solution.py:863
  114.9 21.2 %collective-permute-start.13 = (bf16[8,256,128]{2,1,0:T(8,128)(2,1)S(1)}, bf16[8,256,128]{2,1,0:T(8,128)(2,1)S(1)}, u32[]{:S(2)}, u32[]{:S(2)}) collective-permute-start(bf16[8,256,128]{2,1,0:T(8,128)(2,1)S(1)} %get-tuple-element.296), channel_id=1, source_target_pairs={{0,4},{2,6},{4,0},{6,2},{8,12},{10,14},{12,8},{14,10},{16,20},{18,... | collective-permute-start | bytes 1572872 | tf_op jit(solution)/shard_map/ppermute | solution.py:861
  116.4 19.7 %collective-permute-start.11 = (bf16[4,384,128]{2,1,0:T(8,128)(2,1)S(1)}, bf16[4,384,128]{2,1,0:T(8,128)(2,1)S(1)}, u32[]{:S(2)}, u32[]{:S(2)}) collective-permute-start(bf16[4,384,128]{2,1,0:T(8,128)(2,1)S(1)} %get-tuple-element.294), channel_id=1, source_target_pairs={{0,1},{1,0},{2,3},{3,2},{4,5},{5,4},{6,7},{7,6},{8,9},{9,8},{10,11... | collective-permute-start | bytes 1179656 | tf_op jit(solution)/shard_map/ppermute | solution.py:863
  116.9 19.2 %collective-permute-start.12 = (bf16[4,384,128]{2,1,0:T(8,128)(2,1)S(1)}, bf16[4,384,128]{2,1,0:T(8,128)(2,1)S(1)}, u32[]{:S(2)}, u32[]{:S(2)}) collective-permute-start(bf16[4,384,128]{2,1,0:T(8,128)(2,1)S(1)} %get-tuple-element.295), channel_id=1, source_target_pairs={{0,4},{2,6},{4,0},{6,2},{8,12},{10,14},{12,8},{14,10},{16,20},{18,... | collective-permute-start | bytes 1179656 | tf_op jit(solution)/shard_map/ppermute | solution.py:861
  117.4 10.7 %collective-permute-start.15 = (f32[16,768]{1,0:T(8,128)S(1)}, f32[16,768]{1,0:T(8,128)S(1)}, u32[]{:S(2)}, u32[]{:S(2)}) collective-permute-start(f32[16,768]{1,0:T(8,128)S(1)} %get-tuple-element.298), channel_id=1, source_target_pairs={{0,8},{2,10},{4,12},{6,14},{8,0},{10,2},{12,4},{14,6},{16,24},{18,... | collective-permute-start | bytes 147464 | tf_op jit(solution)/shard_map/ppermute | solution.py:861
  136.6 12.7 %collective-permute-start.16 = (bf16[16,576,128]{2,1,0:T(8,128)(2,1)S(1)}, bf16[16,576,128]{2,1,0:T(8,128)(2,1)S(1)}, u32[]{:S(2)}, u32[]{:S(2)}) collective-permute-start(bf16[16,576,128]{2,1,0:T(8,128)(2,1)S(1)} %get-tuple-element.332), channel_id=1, source_target_pairs={{0,2},{2,0},{4,6},{6,4},{8,10},{10,8},{12,14},{14,12},{16,18},{18,... | collective-permute-start | bytes 7077896 | tf_op jit(solution)/shard_map/ppermute | solution.py:861
  136.7 12.6 %collective-permute-start.19 = (bf16[2,768,128]{2,1,0:T(8,128)(2,1)S(1)}, bf16[2,768,128]{2,1,0:T(8,128)(2,1)S(1)}, u32[]{:S(2)}, u32[]{:S(2)}) collective-permute-start(bf16[2,768,128]{2,1,0:T(8,128)(2,1)S(1)} %get-tuple-element.335), channel_id=1, source_target_pairs={{0,8},{2,10},{4,12},{6,14},{8,0},{10,2},{12,4},{14,6},{16,24},{18,... | collective-permute-start | bytes 1179656 | tf_op jit(solution)/shard_map/ppermute | solution.py:861
  136.8 10.3 %collective-permute-start.18 = (bf16[4,272,128]{2,1,0:T(8,128)(2,1)S(1)}, bf16[4,272,128]{2,1,0:T(8,128)(2,1)S(1)}, u32[]{:S(2)}, u32[]{:S(2)}) collective-permute-start(bf16[4,272,128]{2,1,0:T(8,128)(2,1)S(1)} %get-tuple-element.334), channel_id=1, source_target_pairs={{0,4},{2,6},{4,0},{6,2},{8,12},{10,14},{12,8},{14,10},{16,20},{18,... | collective-permute-start | bytes 835592 | tf_op jit(solution)/shard_map/ppermute | solution.py:861
  138.3 8.8 %collective-permute-start.17 = (bf16[4,256,128]{2,1,0:T(8,128)(2,1)S(1)}, bf16[4,256,128]{2,1,0:T(8,128)(2,1)S(1)}, u32[]{:S(2)}, u32[]{:S(2)}) collective-permute-start(bf16[4,256,128]{2,1,0:T(8,128)(2,1)S(1)} %get-tuple-element.333), channel_id=1, source_target_pairs={{0,1},{1,0},{2,3},{3,2},{4,5},{5,4},{6,7},{7,6},{8,9},{9,8},{10,11... | collective-permute-start | bytes 786440 | tf_op jit(solution)/shard_map/ppermute | solution.py:863
  139.3 7.7 %collective-permute-start.20 = (f32[16,768]{1,0:T(8,128)S(1)}, f32[16,768]{1,0:T(8,128)S(1)}, u32[]{:S(2)}, u32[]{:S(2)}) collective-permute-start(f32[16,768]{1,0:T(8,128)S(1)} %add.15), channel_id=1, source_target_pairs={{0,16},{2,18},{4,20},{6,22},{8,24},{10,26},{12,28},{14,30},{16,0},... | collective-permute-start | bytes 147464 | tf_op jit(solution)/shard_map/ppermute | solution.py:861
  150.2 15.4 %collective-permute-start.21 = (bf16[8,288,128]{2,1,0:T(8,128)(2,1)S(1)}, bf16[8,288,128]{2,1,0:T(8,128)(2,1)S(1)}, u32[]{:S(2)}, u32[]{:S(2)}) collective-permute-start(bf16[8,288,128]{2,1,0:T(8,128)(2,1)S(1)} %get-tuple-element.354), channel_id=1, source_target_pairs={{0,4},{2,6},{4,0},{6,2},{8,12},{10,14},{12,8},{14,10},{16,20},{18,... | collective-permute-start | bytes 1769480 | tf_op jit(solution)/shard_map/ppermute | solution.py:861
  151.7 14.5 %collective-permute-start.22 = (bf16[8,288,128]{2,1,0:T(8,128)(2,1)S(1)}, bf16[8,288,128]{2,1,0:T(8,128)(2,1)S(1)}, u32[]{:S(2)}, u32[]{:S(2)}) collective-permute-start(bf16[8,288,128]{2,1,0:T(8,128)(2,1)S(1)} %get-tuple-element.355), channel_id=1, source_target_pairs={{0,1},{1,0},{2,3},{3,2},{4,5},{5,4},{6,7},{7,6},{8,9},{9,8},{10,11... | collective-permute-start | bytes 1769480 | tf_op jit(solution)/shard_map/ppermute | solution.py:863
  152.8 12.8 %collective-permute-start.23 = (bf16[2,528,128]{2,1,0:T(8,128)(2,1)S(1)}, bf16[2,528,128]{2,1,0:T(8,128)(2,1)S(1)}, u32[]{:S(2)}, u32[]{:S(2)}) collective-permute-start(bf16[2,528,128]{2,1,0:T(8,128)(2,1)S(1)} %get-tuple-element.356), channel_id=1, source_target_pairs={{0,8},{2,10},{4,12},{6,14},{8,0},{10,2},{12,4},{14,6},{16,24},{18,... | collective-permute-start | bytes 811016 | tf_op jit(solution)/shard_map/ppermute | solution.py:861
  154.8 10.7 %collective-permute-start.24 = (bf16[1,768,128]{2,1,0:T(8,128)(2,1)S(1)}, bf16[1,768,128]{2,1,0:T(8,128)(2,1)S(1)}, u32[]{:S(2)}, u32[]{:S(2)}) collective-permute-start(bf16[1,768,128]{2,1,0:T(8,128)(2,1)S(1)} %get-tuple-element.357), channel_id=1, source_target_pairs={{0,16},{2,18},{4,20},{6,22},{8,24},{10,26},{12,28},{14,30},{16,0},... | collective-permute-start | bytes 589832 | tf_op jit(solution)/shard_map/ppermute | solution.py:861
  155.1 1.2 collective-permute-start.25
  156.3 12.6 %copy-start.30 = (f32[8,768]{1,0:T(8,128)S(1)}, f32[8,768]{1,0:T(8,128)}, u32[]{:S(2)}) copy-start(f32[8,768]{1,0:T(8,128)} %get-tuple-element.393) | copy-start | bytes 73732
  156.3 16.8 %copy-start.28 = (f32[320,768]{1,0:T(8,128)S(1)}, f32[320,768]{1,0:T(8,128)}, u32[]{:S(2)}) copy-start(f32[320,768]{1,0:T(8,128)} %get-tuple-element.394) | copy-start | bytes 2949124
  167.4 11.6 %collective-permute-start.26 = (bf16[4,288,128]{2,1,0:T(8,128)(2,1)S(1)}, bf16[4,288,128]{2,1,0:T(8,128)(2,1)S(1)}, u32[]{:S(2)}, u32[]{:S(2)}) collective-permute-start(bf16[4,288,128]{2,1,0:T(8,128)(2,1)S(1)} %get-tuple-element.374), channel_id=1, source_target_pairs={{0,1},{1,0},{2,3},{3,2},{4,5},{5,4},{6,7},{7,6},{8,9},{9,8},{10,11... | collective-permute-start | bytes 884744 | tf_op jit(solution)/shard_map/ppermute | solution.py:863
  168.4 10.6 %collective-permute-start.27 = (bf16[4,288,128]{2,1,0:T(8,128)(2,1)S(1)}, bf16[4,288,128]{2,1,0:T(8,128)(2,1)S(1)}, u32[]{:S(2)}, u32[]{:S(2)}) collective-permute-start(bf16[4,288,128]{2,1,0:T(8,128)(2,1)S(1)} %get-tuple-element.375), channel_id=1, source_target_pairs={{0,4},{2,6},{4,0},{6,2},{8,12},{10,14},{12,8},{14,10},{16,20},{18,... | collective-permute-start | bytes 884744 | tf_op jit(solution)/shard_map/ppermute | solution.py:861
  170.1 6.4 %collective-permute-start.29 = (f32[16,768]{1,0:T(8,128)S(1)}, f32[16,768]{1,0:T(8,128)S(1)}, u32[]{:S(2)}, u32[]{:S(2)}) collective-permute-start(f32[16,768]{1,0:T(8,128)S(1)} %add.17), channel_id=1, source_target_pairs={{0,4},{2,6},{4,0},{6,2},{8,12},{10,14},{12,8},{14,10},{16,20},{18,... | collective-permute-start | bytes 147464 | tf_op jit(solution)/shard_map/ppermute | solution.py:861
  171.6 7.4 %collective-permute-start.28 = (bf16[1,528,128]{2,1,0:T(8,128)(2,1)S(1)}, bf16[1,528,128]{2,1,0:T(8,128)(2,1)S(1)}, u32[]{:S(2)}, u32[]{:S(2)}) collective-permute-start(bf16[1,528,128]{2,1,0:T(8,128)(2,1)S(1)} %get-tuple-element.376), channel_id=1, source_target_pairs={{0,16},{2,18},{4,20},{6,22},{8,24},{10,26},{12,28},{14,30},{16,0},... | collective-permute-start | bytes 405512 | tf_op jit(solution)/shard_map/ppermute | solution.py:861
  179.8 6.1 %collective-permute-start.33 = (f32[16,768]{1,0:T(8,128)S(1)}, f32[16,768]{1,0:T(8,128)S(1)}, u32[]{:S(2)}, u32[]{:S(2)}) collective-permute-start(f32[16,768]{1,0:T(8,128)S(1)} %add.18), channel_id=1, source_target_pairs={{0,1},{1,0},{2,3},{3,2},{4,5},{5,4},{6,7},{7,6},{8,9},{9,8},{10,11... | collective-permute-start | bytes 147464 | tf_op jit(solution)/shard_map/ppermute | solution.py:863
  180.8 10.4 %collective-permute-start.30 = (bf16[1,576,128]{2,1,0:T(8,128)(2,1)S(1)}, bf16[1,576,128]{2,1,0:T(8,128)(2,1)S(1)}, u32[]{:S(2)}, u32[]{:S(2)}) collective-permute-start(bf16[1,576,128]{2,1,0:T(8,128)(2,1)S(1)} %get-tuple-element.388), channel_id=1, source_target_pairs={{0,16},{2,18},{4,20},{6,22},{8,24},{10,26},{12,28},{14,30},{16,0},... | collective-permute-start | bytes 442376 | tf_op jit(solution)/shard_map/ppermute | solution.py:861
  181.0 10.2 %collective-permute-start.31 = (bf16[1,576,128]{2,1,0:T(8,128)(2,1)S(1)}, bf16[1,576,128]{2,1,0:T(8,128)(2,1)S(1)}, u32[]{:S(2)}, u32[]{:S(2)}) collective-permute-start(bf16[1,576,128]{2,1,0:T(8,128)(2,1)S(1)} %get-tuple-element.389), channel_id=1, source_target_pairs={{0,8},{2,10},{4,12},{6,14},{8,0},{10,2},{12,4},{14,6},{16,24},{18,... | collective-permute-start | bytes 442376 | tf_op jit(solution)/shard_map/ppermute | solution.py:861
  183.3 7.8 %collective-permute-start.32 = (bf16[1,576,128]{2,1,0:T(8,128)(2,1)S(1)}, bf16[1,576,128]{2,1,0:T(8,128)(2,1)S(1)}, u32[]{:S(2)}, u32[]{:S(2)}) collective-permute-start(bf16[1,576,128]{2,1,0:T(8,128)(2,1)S(1)} %get-tuple-element.390), channel_id=1, source_target_pairs={{0,24},{2,26},{4,28},{6,30},{8,16},{10,18},{12,20},{14,22},{16,8},... | collective-permute-start | bytes 442376 | tf_op jit(solution)/shard_map/ppermute | solution.py:861
  (1 other events, 0.7 us)
